TPU v7x, 32 devices: a whole 2x2x4 slice. The times are simulated.
32 devices in a mesh: gx: 8 (over y, x, core), gy: 4 (over z).
Axes of the slice: x: 2, y: 2, z: 4, core: 2. Of those that a mesh axis runs over, the one named last changes fastest.
Arguments:
- eigen_block: float32 [16, 64, 64, 128], P(None, 'gx', 'gy'), may hold values from -25 to 25, as said below
- search_dirs: float32 [16, 64, 64, 128], P(None, 'gx', 'gy'), may hold values from -3 to 3
Outputs:
- new_block: float32 [16, 64, 64, 128], P(None, 'gx', 'gy')
- new_search: float32 [16, 64, 64, 128], P(None, 'gx', 'gy')
Inputs may be any that keep to these rules, and one draw needn't show every extreme that they name: `eigen_block`: real numbers whose typical size changes along the first grid dimension.
All inputs are finite; a program needn't handle non-finite values.
Results may differ from a plain program's by a relative error of at most 0.0003.
Values sent between devices are 32-bit elements; how exact they have to be, the bound alone decides.
No kernel may reach another device: no remote copies, remote signals or barrier semaphores. Data moves between devices by JAX's collectives and lax.ppermute only.
A program may use at most 64 MiB of HBM per device.

v0:
```python
import functools

import jax
import jax.numpy as jnp
from jax import lax
from jax.experimental import pallas as pl
from jax.experimental.pallas import tpu as pltpu
from jax.sharding import PartitionSpec as P

RELAX = 1.0 / 9.0
COARSE_RELAX = 1.0 / 36.0
SHIFT = 13.0
DEEP = 4
POST = 3
CO = 3
PAD = 8

F32 = jnp.float32
VMEM = pl.BlockSpec(memory_space=pltpu.VMEM)
SMEM = pl.BlockSpec(memory_space=pltpu.SMEM)


def shape(*dims):
    return jax.ShapeDtypeStruct(dims, F32)


def call(kernel, outs, scratch, args, name, smem=0):
    specs = [SMEM] * smem + [VMEM] * (len(args) - smem)
    return pl.pallas_call(
        kernel,
        out_shape=outs,
        in_specs=specs,
        out_specs=[VMEM] * len(outs),
        scratch_shapes=scratch,
        name=name,
    )(*args)


def along_z(plane, step, lanes):
    size = plane.shape[-1]
    low = jnp.where(lanes >= step, pltpu.roll(plane, step, 1), 0.0)
    high = jnp.where(lanes < size - step, pltpu.roll(plane, size - step, 1), 0.0)
    return low + high


def beside(work, i, row, rows, center, before, after, lanes, step=1):
    total = before + after
    total = total + work[i, pl.ds(row - 1, rows), :] + work[i, pl.ds(row + 1, rows), :]
    return total + along_z(center, step, lanes)


def lane_index(rows):
    return lax.broadcasted_iota(jnp.int32, (rows, 128), 1)


def pack_kernel(x_ref, p_ref, ylo, yhi, xlo, xhi):
    cols, nx, ny, _ = x_ref.shape

    def body(f, carry):
        for i in range(nx):
            ylo[f, pl.ds(i * DEEP, DEEP), :] = x_ref[f, i, pl.ds(0, DEEP), :]
            yhi[f, pl.ds(i * DEEP, DEEP), :] = x_ref[f, i, pl.ds(ny - DEEP, DEEP), :]
            ylo[f, pl.ds(nx * DEEP + i, 1), :] = p_ref[f, i, pl.ds(0, 1), :]
            yhi[f, pl.ds(nx * DEEP + i, 1), :] = p_ref[f, i, pl.ds(ny - 1, 1), :]
        for i in range(DEEP):
            xlo[f, i] = x_ref[f, i]
            xhi[f, i] = x_ref[f, nx - DEEP + i]
        xlo[f, DEEP] = p_ref[f, 0]
        xhi[f, DEEP] = p_ref[f, nx - 1]
        return carry

    lax.fori_loop(0, cols, body, 0)


def theta_kernel(x_ref, ylo, yhi, xlo, xhi, out_ref, clo, chi, work):
    cols, nx, ny, _ = x_ref.shape
    lanes = lane_index(ny)
    spot = lane_index(8)
    half = nx // 2 * DEEP

    def body(f, carry):
        work[0, pl.ds(PAD, ny), :] = xlo[f, DEEP - 1]
        work[nx + 1, pl.ds(PAD, ny), :] = xhi[f, 0]
        for i in range(nx):
            work[i + 1, pl.ds(PAD, ny), :] = x_ref[f, i]
            work[i + 1, pl.ds(PAD - 1, 1), :] = ylo[f, pl.ds(i * DEEP + DEEP - 1, 1), :]
            work[i + 1, pl.ds(PAD + ny, 1), :] = yhi[f, pl.ds(i * DEEP, 1), :]
        numer = jnp.zeros((ny, 128), F32)
        denom = jnp.zeros((ny, 128), F32)
        before = work[0, pl.ds(PAD, ny), :]
        center = work[1, pl.ds(PAD, ny), :]
        for i in range(nx):
            after = work[i + 2, pl.ds(PAD, ny), :]
            image = 6.0 * center - beside(work, i + 1, PAD, ny, center, before, after, lanes)
            numer = numer + center * image
            denom = denom + center * center
            before, center = center, after
        numer = jnp.sum(numer, axis=(0, 1), keepdims=True)
        denom = jnp.sum(denom, axis=(0, 1), keepdims=True)
        clo[f, pl.ds(0, half), :] = ylo[f, pl.ds(0, half), :]
        clo[f, pl.ds(half, half), :] = yhi[f, pl.ds(0, half), :]
        chi[f, pl.ds(0, half), :] = ylo[f, pl.ds(half, half), :]
        chi[f, pl.ds(half, half), :] = yhi[f, pl.ds(half, half), :]
        carry = jnp.where(spot == f, numer, carry)
        return jnp.where(spot == f + cols, denom, carry)

    sums = lax.fori_loop(0, cols, body, jnp.zeros((8, 128), F32))
    for k in range(out_ref.shape[0]):
        out_ref[k] = sums


def pre_kernel(
    flags, sums, x_ref, ylo, yhi, xlo, xhi, clo, chi,
    r_ref, e_ref, c_ref, slo, shi,
    work, other, rhs, small, coarse,
):
    cols, nx, ny, _ = x_ref.shape
    tall = ny + 2 * DEEP
    wide = nx + 2 * DEEP
    lanes = lane_index(tall)
    own = lane_index(ny)
    spot = lane_index(8)
    has = [flags[k].astype(F32) for k in range(4)]
    row = lax.broadcasted_iota(jnp.int32, (tall, 128), 0)
    mask_y = RELAX * jnp.where(row < DEEP, has[2], jnp.where(row >= ny + DEEP, has[3], 1.0))

    def relax_of(i):
        if i < DEEP:
            return mask_y * has[0]
        if i >= nx + DEEP:
            return mask_y * has[1]
        return mask_y

    total = sums[0]
    for k in range(1, sums.shape[0]):
        total = total + sums[k]
    theta = total / pltpu.roll(total, 128 - cols, 1)

    @pl.when(jnp.bool_(True))
    def _():
        zero = jnp.zeros((8, 128), F32)
        for i in range(wide):
            for buf in (work, other):
                buf[i, pl.ds(0, PAD), :] = zero
                buf[i, pl.ds(PAD + tall, 8), :] = zero

    data = pl.ds(PAD, tall)

    def body(f, carry):
        th = jnp.sum(jnp.where(spot == f, theta, 0.0)) * 0.125
        for i in range(DEEP):
            lo, hi = i, nx + DEEP + i
            work[lo, pl.ds(PAD + DEEP, ny), :] = xlo[f, i]
            work[hi, pl.ds(PAD + DEEP, ny), :] = xhi[f, i]
            for plane, buf in ((lo, clo), (hi, chi)):
                work[plane, pl.ds(PAD, DEEP), :] = buf[f, pl.ds(i * DEEP, DEEP), :]
                work[plane, pl.ds(PAD + DEEP + ny, DEEP), :] = buf[
                    f, pl.ds(DEEP * DEEP + i * DEEP, DEEP), :
                ]
        for i in range(nx):
            work[i + DEEP, pl.ds(PAD + DEEP, ny), :] = x_ref[f, i]
            work[i + DEEP, pl.ds(PAD, DEEP), :] = ylo[f, pl.ds(i * DEEP, DEEP), :]
            work[i + DEEP, pl.ds(PAD + DEEP + ny, DEEP), :] = yhi[f, pl.ds(i * DEEP, DEEP), :]
        before = work[0, data, :]
        center = work[1, data, :]
        for i in range(1, wide - 1):
            after = work[i + 1, data, :]
            image = 6.0 * center - beside(work, i, PAD, tall, center, before, after, lanes)
            res = image - th * center
            rhs[i] = res
            other[i, data, :] = relax_of(i) * res
            before, center = center, after
        src, dst = other, work
        for depth in (2, 3):
            before = src[depth - 1, data, :]
            center = src[depth, data, :]
            for i in range(depth, wide - depth):
                after = src[i + 1, data, :]
                near = beside(src, i, PAD, tall, center, before, after, lanes)
                dst[i, data, :] = center + relax_of(i) * (rhs[i] - 6.0 * center + near)
                before, center = center, after
            src, dst = dst, src
        own_rows = pl.ds(PAD + DEEP, ny)
        before = src[DEEP - 1, own_rows, :]
        center = src[DEEP, own_rows, :]
        held = None
        for i in range(DEEP, nx + DEEP):
            after = src[i + 1, own_rows, :]
            near = beside(src, i, PAD + DEEP, ny, center, before, after, own)
            rest = rhs[i, pl.ds(DEEP, ny), :] - 6.0 * center + near
            e_ref[f, i - DEEP] = center
            if held is None:
                held = rest
            else:
                small[...] = held + rest
                pair = small[pl.ds(0, ny // 2, stride=2), :] + small[pl.ds(1, ny // 2, stride=2), :]
                mate = jnp.where(
                    spot % 2 == 0, pltpu.roll(pair, 127, 1), pltpu.roll(pair, 1, 1)
                )
                coarse[f, (i - DEEP) // 2] = pair + mate
                held = None
            before, center = center, after
        for i in range(2, wide - 2):
            r_ref[f, i - 2] = rhs[i]
        return carry

    lax.fori_loop(0, cols, body, 0)
    half, cx, cy = cols // 2, nx // 2, ny // 2
    even = spot % 2 == 0
    for g in range(half):
        for i in range(cx):
            both = jnp.where(even, coarse[g, i], coarse[g + half, i])
            c_ref[g, i] = both
            small[pl.ds(0, 8), :] = both
            at = (g * cx + i) * CO
            slo[pl.ds(at, CO), :] = small[pl.ds(0, CO), :]
            shi[pl.ds(at, CO), :] = small[pl.ds(cy - CO, CO), :]


def coarse_pack_kernel(c_ref, ylo, yhi, xlo, xhi):
    half, cx, cy, _ = c_ref.shape
    tall = cy + 2 * CO
    for g in range(half):
        for out, first in ((xlo, 0), (xhi, cx - CO)):
            for i in range(CO):
                at = (g * CO + i) * tall
                src = (g * cx + first + i) * CO
                out[pl.ds(at, CO), :] = ylo[pl.ds(src, CO), :]
                out[pl.ds(at + CO, cy), :] = c_ref[g, first + i]
                out[pl.ds(at + CO + cy, CO), :] = yhi[pl.ds(src, CO), :]


def coarse_kernel(
    flags, c_ref, ylo, yhi, xlo, xhi, e_ref, corr_ref, slo, shi, work, other, rhs, small
):
    half, cx, cy, _ = c_ref.shape
    cols, nx, ny, _ = e_ref.shape
    tall = cy + 2 * CO
    full = 16
    wide = cx + 2 * CO
    lanes = lane_index(full)
    spot = lane_index(8)
    odd = spot % 2 == 1
    has = [flags[k].astype(F32) for k in range(4)]
    row = lax.broadcasted_iota(jnp.int32, (full, 128), 0)
    mask_y = COARSE_RELAX * jnp.where(row < CO, has[2], jnp.where(row >= cy + CO, has[3], 1.0))
    zero = jnp.zeros((8, 128), F32)
    for i in range(wide):
        rhs[i, pl.ds(8, 8), :] = zero
        for buf in (work, other):
            buf[i, pl.ds(0, PAD), :] = zero
            buf[i, pl.ds(PAD + full, 8), :] = zero

    def relax_of(i):
        if i < CO:
            return mask_y * has[0]
        if i >= cx + CO:
            return mask_y * has[1]
        return mask_y

    data = pl.ds(PAD, full)

    def body(g, carry):
        for i in range(CO):
            rhs[i, pl.ds(0, tall), :] = xlo[pl.ds((g * CO + i) * tall, tall), :]
            rhs[cx + CO + i, pl.ds(0, tall), :] = xhi[pl.ds((g * CO + i) * tall, tall), :]
        for i in range(cx):
            at = pl.ds((g * cx + i) * CO, CO)
            rhs[i + CO, pl.ds(0, CO), :] = ylo[at, :]
            rhs[i + CO, pl.ds(CO, cy), :] = c_ref[g, i]
            rhs[i + CO, pl.ds(CO + cy, CO), :] = yhi[at, :]
        for i in range(wide):
            work[i, data, :] = relax_of(i) * rhs[i]
        src, dst = work, other
        for depth in (1, 2, 3):
            before = src[depth - 1, data, :]
            center = src[depth, data, :]
            for i in range(depth, wide - depth):
                after = src[i + 1, data, :]
                near = beside(src, i, PAD, full, center, before, after, lanes, 2)
                dst[i, data, :] = center + relax_of(i) * (rhs[i] - 4.0 * (6.0 * center - near))
                before, center = center, after
            src, dst = dst, src
        for i in range(cx):
            both = src[i + CO, pl.ds(PAD + CO, cy), :]
            first = jnp.where(odd, pltpu.roll(both, 1, 1), both)
            second = jnp.where(odd, both, pltpu.roll(both, 127, 1))
            for f, value in ((g, first), (g + half, second)):
                small[pl.ds(0, cy, stride=2), :] = value
                small[pl.ds(1, cy, stride=2), :] = value
                for k in (2 * i, 2 * i + 1):
                    corr = e_ref[f, k] + small[...]
                    corr_ref[f, k] = corr
                    slo[f, pl.ds(k * POST, POST), :] = corr_ref[f, k, pl.ds(0, POST), :]
                    shi[f, pl.ds(k * POST, POST), :] = corr_ref[f, k, pl.ds(ny - POST, POST), :]
        return carry

    lax.fori_loop(0, half, body, 0)


def post_pack_kernel(corr_ref, ylo, yhi, xlo, xhi):
    cols, nx, ny, _ = corr_ref.shape
    tall = ny + 2 * POST

    def body(f, carry):
        for out, first in ((xlo, 0), (xhi, nx - POST)):
            for i in range(POST):
                at = i * tall
                src = pl.ds((first + i) * POST, POST)
                out[f, pl.ds(at, POST), :] = ylo[f, src, :]
                out[f, pl.ds(at + POST, ny), :] = corr_ref[f, first + i]
                out[f, pl.ds(at + POST + ny, POST), :] = yhi[f, src, :]
        return carry

    lax.fori_loop(0, cols, body, 0)


def post_kernel(
    flags, corr_ref, ylo, yhi, xlo, xhi, r_ref, w_ref, image_ref, work, other
):
    cols, nx, ny, _ = corr_ref.shape
    tall = ny + 2 * DEEP
    wide = nx + 2 * POST
    span = ny + 2 * POST
    gap = DEEP - POST
    lanes = lane_index(tall)
    own = lane_index(ny)
    has = [flags[k].astype(F32) for k in range(4)]
    row = lax.broadcasted_iota(jnp.int32, (tall, 128), 0)
    mask_y = RELAX * jnp.where(row < DEEP, has[2], jnp.where(row >= ny + DEEP, has[3], 1.0))
    zero = jnp.zeros((PAD + 8, 128), F32)
    for i in range(wide):
        for buf in (work, other):
            buf[i, pl.ds(0, PAD + 8), :] = zero
            buf[i, pl.ds(PAD + tall - 8, 16), :] = zero

    def relax_of(i):
        if i < POST:
            return mask_y * has[0]
        if i >= nx + POST:
            return mask_y * has[1]
        return mask_y

    data = pl.ds(PAD, tall)

    def body(f, carry):
        for i in range(POST):
            work[i, pl.ds(PAD + gap, span), :] = xlo[f, pl.ds(i * span, span), :]
            work[nx + POST + i, pl.ds(PAD + gap, span), :] = xhi[f, pl.ds(i * span, span), :]
        for i in range(nx):
            at = pl.ds(i * POST, POST)
            work[i + POST, pl.ds(PAD + gap, POST), :] = ylo[f, at, :]
            work[i + POST, pl.ds(PAD + DEEP, ny), :] = corr_ref[f, i]
            work[i + POST, pl.ds(PAD + DEEP + ny, POST), :] = yhi[f, at, :]
        src, dst = work, other
        for depth in (1, 2):
            before = src[depth - 1, data, :]
            center = src[depth, data, :]
            for i in range(depth, wide - depth):
                after = src[i + 1, data, :]
                near = beside(src, i, PAD, tall, center, before, after, lanes)
                dst[i, data, :] = center + relax_of(i) * (r_ref[f, i - 1] - 6.0 * center + near)
                before, center = center, after
            src, dst = dst, src
        own_rows = pl.ds(PAD + DEEP, ny)
        before = src[POST - 1, own_rows, :]
        center = src[POST, own_rows, :]
        for i in range(POST, nx + POST):
            after = src[i + 1, own_rows, :]
            near = beside(src, i, PAD + DEEP, ny, center, before, after, own)
            w_ref[f, i - POST] = center
            image_ref[f, i - POST] = 6.0 * center - near
            before, center = center, after
        return carry

    lax.fori_loop(0, cols, body, 0)


def image_kernel(x_ref, p_ref, ylo, yhi, xlo, xhi, ax_ref, ap_ref, work):
    cols, nx, ny, _ = x_ref.shape
    lanes = lane_index(ny)

    def body(f, carry):
        for ref, out, lo, hi, base, deep in (
            (x_ref, ax_ref, DEEP - 1, 0, 0, DEEP),
            (p_ref, ap_ref, DEEP, DEEP, nx * DEEP, 1),
        ):
            work[0, pl.ds(PAD, ny), :] = xlo[f, lo]
            work[nx + 1, pl.ds(PAD, ny), :] = xhi[f, hi]
            for i in range(nx):
                work[i + 1, pl.ds(PAD, ny), :] = ref[f, i]
                work[i + 1, pl.ds(PAD - 1, 1), :] = ylo[f, pl.ds(base + i * deep + deep - 1, 1), :]
                work[i + 1, pl.ds(PAD + ny, 1), :] = yhi[f, pl.ds(base + i * deep, 1), :]
            before = work[0, pl.ds(PAD, ny), :]
            center = work[1, pl.ds(PAD, ny), :]
            for i in range(nx):
                after = work[i + 2, pl.ds(PAD, ny), :]
                near = beside(work, i + 1, PAD, ny, center, before, after, lanes)
                out[f, i] = 6.0 * center - near
                before, center = center, after
        return carry

    lax.fori_loop(0, cols, body, 0)


def from_low(value, axis):
    count = lax.axis_size(axis)
    return lax.ppermute(value, axis, [(i, i + 1) for i in range(count - 1)])


def from_high(value, axis):
    count = lax.axis_size(axis)
    return lax.ppermute(value, axis, [(i + 1, i) for i in range(count - 1)])


def radices(count):
    out = []
    if count % 2 == 0 and count % 4 == 0 and (count.bit_length() - 1) % 2 == 1:
        out.append(2)
        count //= 2
    while count % 4 == 0:
        out.append(4)
        count //= 4
    if count > 1:
        out.append(count)
    return out


def sum_all(value):
    for axis in ("gx", "gy"):
        count = lax.axis_size(axis)
        stride = 1
        for radix in radices(count):
            index = lax.axis_index(axis)
            parts = [value]
            for k in range(1, radix):
                pairs = []
                for i in range(count):
                    digit = i // stride % radix
                    target = i + ((digit + k) % radix - digit) * stride
                    pairs.append((i, target))
                parts.append(lax.ppermute(value, axis, pairs))
            digit = index // stride % radix
            if radix == 2:
                value = parts[0] + parts[1]
            elif radix == 4:
                even = parts[0] + parts[2]
                odd = parts[1] + parts[3]
                value = even + odd
            else:
                value = functools.reduce(jnp.add, parts)
            stride *= radix
    return value


def ritz_coef(gram, proj, ncells):
    hp = lax.Precision.HIGHEST
    proj = 0.5 * (proj + proj.T)
    lower = jnp.linalg.cholesky(gram)
    inner = jax.scipy.linalg.solve_triangular(lower, proj, lower=True)
    ritz = jax.scipy.linalg.solve_triangular(lower, inner.T, lower=True)
    ritz = 0.5 * (ritz + ritz.T)
    nbasis = gram.shape[0]
    kcount = nbasis // 3
    filtered = SHIFT * jnp.eye(nbasis, dtype=jnp.float32)[:, :kcount] - ritz[:, :kcount]
    small = jnp.linalg.cholesky(jnp.dot(filtered.T, filtered, precision=hp))
    scaled = jax.scipy.linalg.solve_triangular(small, filtered.T, lower=True).T
    coef = jax.scipy.linalg.solve_triangular(lower, scaled, lower=True, trans="T")
    return coef * jnp.sqrt(jnp.float32(ncells))


def body(x, p):
    hp = lax.Precision.HIGHEST
    cols, nx, ny, nz = x.shape
    ngx, ngy = lax.axis_size("gx"), lax.axis_size("gy")
    ix, iy = lax.axis_index("gx"), lax.axis_index("gy")
    flags = jnp.stack([ix > 0, ix < ngx - 1, iy > 0, iy < ngy - 1]).astype(jnp.int32)
    half, cx, cy = cols // 2, nx // 2, ny // 2
    work = pltpu.VMEM

    yrows = nx * DEEP + nx
    to_ylo, to_yhi, to_xlo, to_xhi = call(
        pack_kernel,
        [shape(cols, yrows, nz)] * 2 + [shape(cols, DEEP + 1, ny, nz)] * 2,
        [], (x, p), "pack",
    )
    ylo, yhi = from_low(to_yhi, "gy"), from_high(to_ylo, "gy")
    xlo, xhi = from_low(to_xhi, "gx"), from_high(to_xlo, "gx")

    devices = ngx * ngy
    sums, to_clo, to_chi = call(
        theta_kernel,
        [shape(devices, 8, 128)] + [shape(cols, nx * DEEP, nz)] * 2,
        [work((nx + 2, PAD + ny + 8, nz), F32)],
        (x, ylo, yhi, xlo, xhi), "theta",
    )
    clo, chi = from_low(to_chi, "gx"), from_high(to_clo, "gx")
    sums = lax.all_to_all(sums, ("gx", "gy"), 0, 0)

    tall, wide = ny + 2 * DEEP, nx + 2 * DEEP
    plane = PAD + tall + 8
    r, e, c, to_ylo, to_yhi = call(
        pre_kernel,
        [shape(cols, wide - 4, tall, nz), shape(cols, nx, ny, nz), shape(half, cx, cy, nz)]
        + [shape(half * cx * CO, nz)] * 2,
        [work((wide, plane, nz), F32)] * 2
        + [work((wide, tall, nz), F32), work((ny, nz), F32), work((cols, cx, cy, nz), F32)],
        (flags, sums, x, ylo, yhi, xlo, xhi, clo, chi), "pre", smem=1,
    )

    cylo, cyhi = from_low(to_yhi, "gy"), from_high(to_ylo, "gy")
    to_xlo, to_xhi = call(
        coarse_pack_kernel, [shape(half * CO * (cy + 2 * CO), nz)] * 2, [], (c, cylo, cyhi), "cpack"
    )
    cxlo, cxhi = from_low(to_xhi, "gx"), from_high(to_xlo, "gx")
    cwide = cx + 2 * CO
    corr, to_ylo, to_yhi = call(
        coarse_kernel,
        [shape(cols, nx, ny, nz)] + [shape(cols, nx * POST, nz)] * 2,
        [work((cwide, PAD + 16 + 8, nz), F32)] * 2
        + [work((cwide, 16, nz), F32), work((ny, nz), F32)],
        (flags, c, cylo, cyhi, cxlo, cxhi, e), "coarse", smem=1,
    )

    eylo, eyhi = from_low(to_yhi, "gy"), from_high(to_ylo, "gy")
    to_xlo, to_xhi = call(
        post_pack_kernel, [shape(cols, POST * (ny + 2 * POST), nz)] * 2, [], (corr, eylo, eyhi), "ppack"
    )
    exlo, exhi = from_low(to_xhi, "gx"), from_high(to_xlo, "gx")

    image_x, image_p = call(
        image_kernel, [shape(cols, nx, ny, nz)] * 2,
        [work((nx + 2, PAD + ny + 8, nz), F32)],
        (x, p, ylo, yhi, xlo, xhi), "image",
    )
    w, image_w = call(
        post_kernel, [shape(cols, nx, ny, nz)] * 2,
        [work((nx + 2 * POST, plane, nz), F32)] * 2,
        (flags, corr, eylo, eyhi, exlo, exhi, r), "post", smem=1,
    )

    basis = jnp.concatenate([x, w, p], axis=0)
    images = jnp.concatenate([image_x, image_w, image_p], axis=0)
    both = jnp.concatenate([basis, images], axis=0)
    part = jnp.einsum("kxyz,lxyz->kl", basis, both, precision=hp)
    part = sum_all(part)
    nb = 3 * cols
    coef = ritz_coef(part[:, :nb], part[:, nb:], nx * ny * nz * devices)
    new_search = jnp.einsum("lk,lxyz->kxyz", coef[cols:], basis[cols:], precision=hp)
    new_block = new_search + jnp.einsum("lk,lxyz->kxyz", coef[:cols], x, precision=hp)
    return (new_block, new_search)


def solution(mesh):
    spec = P(None, "gx", "gy", None)
    return jax.shard_map(
        body, mesh=mesh, in_specs=(spec, spec), out_specs=(spec, spec), check_vma=False
    )
```

profile of v0, /device:TPU:0, one launch (start us, length us, event | category | flops | bytes accessed | tf_op | source)
XLA Modules:
  0.0 195.0 jit_solution(11498124526747694337)
XLA Ops:
  0.6 3.1 %pack.1 = (f32[16,40,128]{2,1,0:T(8,128)}, f32[16,40,128]{2,1,0:T(8,128)}, f32[16,5,16,128]{3,2,1,0:T(8,128)}, f32[16,5,16,128]{3,2,1,0:T(8,128)}) custom-call(f32[16,8,16,128]{3,2,1,0:T(8,128)} %x_ref.7, f32[16,8,16,128]{3,2,1,0:T(8,128)} %p_ref.3), custom_call_target="tpu_custom_call" | custom-call | tf_op jit(solution)/shard_map/pack/pallas_call | solution.py:29
  7.6 4.3 %collective-permute-start = (f32[16,40,128]{2,1,0:T(8,128)}, f32[16,40,128]{2,1,0:T(8,128)S(1)}, u32[]{:S(2)}, u32[]{:S(2)}) collective-permute-start(f32[16,40,128]{2,1,0:T(8,128)} %get-tuple-element.26), channel_id=1, source_target_pairs={{0,1},{1,2},{2,3},{4,5},{5,6},{6,7},{8,9},{9,10},{10,11},{12,13},{... | collective-permute-start | bytes 983048 | tf_op jit(solution)/shard_map/ppermute | solution.py:408
  13.2 5.7 %collective-permute-done.ylo = f32[16,40,128]{2,1,0:T(8,128)S(1)} collective-permute-done((f32[16,40,128]{2,1,0:T(8,128)}, f32[16,40,128]{2,1,0:T(8,128)S(1)}, u32[]{:S(2)}, u32[]{:S(2)}) %collective-permute-start) | collective-permute-done | bytes 327712 | tf_op jit(solution)/shard_map/ppermute | solution.py:408
  18.9 4.6 %collective-permute-done.1.yhi = f32[16,40,128]{2,1,0:T(8,128)S(1)} collective-permute-done((f32[16,40,128]{2,1,0:T(8,128)}, f32[16,40,128]{2,1,0:T(8,128)S(1)}, u32[]{:S(2)}, u32[]{:S(2)}) %collective-permute-start.1) | collective-permute-done | bytes 327712 | tf_op jit(solution)/shard_map/ppermute | solution.py:413
  25.3 6.1 %theta.1 = (f32[32,8,128]{2,1,0:T(8,128)}, f32[16,32,128]{2,1,0:T(8,128)}, f32[16,32,128]{2,1,0:T(8,128)}) custom-call(f32[16,8,16,128]{3,2,1,0:T(8,128)} %x_ref.7, f32[16,40,128]{2,1,0:T(8,128)} %copy-done.6, f32[16,40,128]{2,1,0:T(8,128)} %copy-done.7, f32[16,5,16,128]{3,2,1,0:T(8,128)} %copy-done.4, f32[16,5,16,128]{3,2,1,0:T(8,128)} %copy-done.5), custom_call_target="tpu_custom_call" | custom-call | tf_op jit(solution)/shard_map/theta/pallas_call | solution.py:29
  31.4 2.8 %collective-permute-start.4 = (f32[16,32,128]{2,1,0:T(8,128)}, f32[16,32,128]{2,1,0:T(8,128)S(1)}, u32[]{:S(2)}, u32[]{:S(2)}) collective-permute-start(f32[16,32,128]{2,1,0:T(8,128)} %get-tuple-element.31), channel_id=1, source_target_pairs={{0,4},{4,8},{8,12},{12,16},{16,20},{20,24},{24,28},{1,5},{5,9},{9,... | collective-permute-start | bytes 786440 | tf_op jit(solution)/shard_map/ppermute | solution.py:408
  35.6 8.4 %all-to-all-start = ((f32[32,8,128]{2,1,0:T(8,128)}), f32[32,8,128]{2,1,0:T(8,128)S(1)}, u32[]{:S(2)}, u32[]{:S(2)}) async-start(f32[32,8,128]{2,1,0:T(8,128)} %get-tuple-element.30), calls=%async_computation | async-start | bytes 262144 | tf_op jit(solution)/shard_map/all_to_all | solution.py:498
  44.7 7.7 %all-to-all-done.sums = f32[32,8,128]{2,1,0:T(8,128)S(1)} async-done(((f32[32,8,128]{2,1,0:T(8,128)}), f32[32,8,128]{2,1,0:T(8,128)S(1)}, u32[]{:S(2)}, u32[]{:S(2)}) %all-to-all-start) | async-done | bytes 131104 | tf_op jit(solution)/shard_map/all_to_all | solution.py:498
  53.9 11.8 %pre.1 = (f32[16,12,24,128]{3,2,1,0:T(8,128)}, f32[16,8,16,128]{3,2,1,0:T(8,128)}, f32[8,4,8,128]{3,2,1,0:T(8,128)}, f32[96,128]{1,0:T(8,128)}, f32[96,128]{1,0:T(8,128)}) custom-call(s32[4]{0:T(128)} %add_convert_fusion.flags, f32[32,8,128]{2,1,0:T(8,128)} %copy-done.13, f32[16,8,16,128]{3,2,1,0:T(8,128)} %x_ref.7, f32[16,40,128]{2,1,0:T(8,128)} %copy-done.6, ...), custom_call_target="tpu_custom_call" | custom-call | tf_op jit(solution)/shard_map/pre/pallas_call | solution.py:29
  69.3 4.0 %collective-permute-done.7.yhi = f32[96,128]{1,0:T(8,128)S(1)} collective-permute-done((f32[96,128]{1,0:T(8,128)}, f32[96,128]{1,0:T(8,128)S(1)}, u32[]{:S(2)}, u32[]{:S(2)}) %collective-permute-start.7) | collective-permute-done | bytes 49184 | tf_op jit(solution)/shard_map/ppermute | solution.py:413
  78.4 3.2 %collective-permute-done.9.xhi = f32[336,128]{1,0:T(8,128)S(1)} collective-permute-done((f32[336,128]{1,0:T(8,128)}, f32[336,128]{1,0:T(8,128)S(1)}, u32[]{:S(2)}, u32[]{:S(2)}) %collective-permute-start.9) | collective-permute-done | bytes 172064 | tf_op jit(solution)/shard_map/ppermute | solution.py:413
  82.4 5.7 %coarse.1 = (f32[16,8,16,128]{3,2,1,0:T(8,128)}, f32[16,24,128]{2,1,0:T(8,128)}, f32[16,24,128]{2,1,0:T(8,128)}) custom-call(s32[4]{0:T(128)} %add_convert_fusion.flags, f32[8,4,8,128]{3,2,1,0:T(8,128)} %get-tuple-element.33.c_ref, f32[96,128]{1,0:T(8,128)} %copy-done.16, f32[96,128]{1,0:T(8,128)} %copy-done.17, f32[336,128]{1,0:T(8,128)} %copy-done.18, ...), custom_call_target="tpu_custom_call" | custom-call | tf_op jit(solution)/shard_map/coarse/pallas_call | solution.py:29
  88.1 2.9 %collective-permute-start.10 = (f32[16,24,128]{2,1,0:T(8,128)}, f32[16,24,128]{2,1,0:T(8,128)S(1)}, u32[]{:S(2)}, u32[]{:S(2)}) collective-permute-start(f32[16,24,128]{2,1,0:T(8,128)} %get-tuple-element.40), channel_id=1, source_target_pairs={{0,1},{1,2},{2,3},{4,5},{5,6},{6,7},{8,9},{9,10},{10,11},{12,13},{... | collective-permute-start | bytes 589832 | tf_op jit(solution)/shard_map/ppermute | solution.py:408
  94.5 4.3 %collective-permute-done.11.yhi = f32[16,24,128]{2,1,0:T(8,128)S(1)} collective-permute-done((f32[16,24,128]{2,1,0:T(8,128)}, f32[16,24,128]{2,1,0:T(8,128)S(1)}, u32[]{:S(2)}, u32[]{:S(2)}) %collective-permute-start.11) | collective-permute-done | bytes 196640 | tf_op jit(solution)/shard_map/ppermute | solution.py:413
  104.0 5.2 %collective-permute-start.12 = (f32[16,66,128]{2,0,1:T(8,128)}, f32[16,66,128]{2,0,1:T(8,128)}, u32[]{:S(2)}, u32[]{:S(2)}) collective-permute-start(f32[16,66,128]{2,0,1:T(8,128)} %copy.18), channel_id=1, source_target_pairs={{0,4},{4,8},{8,12},{12,16},{16,20},{20,24},{24,28},{1,5},{5,9},{9,... | collective-permute-start | bytes 1622024 | tf_op jit(solution)/shard_map/ppermute | solution.py:408
  113.7 5.9 %image.1 = (f32[16,8,16,128]{3,2,1,0:T(8,128)}, f32[16,8,16,128]{3,2,1,0:T(8,128)}) custom-call(f32[16,8,16,128]{3,2,1,0:T(8,128)} %x_ref.7, f32[16,8,16,128]{3,2,1,0:T(8,128)} %p_ref.3, f32[16,40,128]{2,1,0:T(8,128)} %copy-done.6, f32[16,40,128]{2,1,0:T(8,128)} %copy-done.7, f32[16,5,16,128]{3,2,1,0:T(8,128)} %copy-done.4, f32[16,5,16,128]{3,2,1,0:T(8,128)} %copy-done.5), custom_call_target="tpu_custom_call" | custom-call | tf_op jit(solution)/shard_map/image/pallas_call | solution.py:29
  123.6 9.0 %post.1 = (f32[16,8,16,128]{3,2,1,0:T(8,128)}, f32[16,8,16,128]{3,2,1,0:T(8,128)}) custom-call(s32[4]{0:T(128)} %add_convert_fusion.flags, f32[16,8,16,128]{3,2,1,0:T(8,128)} %get-tuple-element.39.corr_ref, f32[16,24,128]{2,1,0:T(8,128)} %copy-done.11, f32[16,24,128]{2,1,0:T(8,128)} %copy-done.12, f32[16,66,128]{2,1,0:T(8,128)} %copy.20.xlo, ...), custom_call_target="tpu_custom_call" | custom-call | tf_op jit(solution)/shard_map/post/pallas_call | solution.py:29
  139.7 13.7 %fusion.5 = f32[48,96]{0,1:T(8,128)S(1)} fusion(f32[96,8,16,128]{3,2,1,0:T(8,128)} %constant_dynamic-update-slice_fusion, f32[48,8,16,128]{3,2,1,0:T(8,128)S(1)} %pad_maximum_fusion), kind=kOutput, calls=%fused_computation.8 | convolution fusion | flops 905969664 | bytes 9455616 | tf_op jit(solution)/shard_map/kxyz,lxyz->kl/dot_general | solution.py:545
  153.4 4.0 %collective-permute-start.14 = (f32[48,96]{0,1:T(8,128)S(1)}, f32[48,96]{0,1:T(8,128)S(1)}, u32[]{:S(2)}, u32[]{:S(2)}) collective-permute-start(f32[48,96]{0,1:T(8,128)S(1)} %fusion.5), channel_id=1, source_target_pairs={{0,4},{4,0},{8,12},{12,8},{16,20},{20,16},{24,28},{28,24},{1,5},{5... | collective-permute-start | bytes 55304 | tf_op jit(solution)/shard_map/ppermute | solution.py:442
  160.3 2.9 %collective-permute-start.17 = (f32[48,96]{0,1:T(8,128)S(1)}, f32[48,96]{0,1:T(8,128)S(1)}, u32[]{:S(2)}, u32[]{:S(2)}) collective-permute-start(f32[48,96]{0,1:T(8,128)S(1)} %add.56), channel_id=1, source_target_pairs={{0,24},{4,28},{8,0},{12,4},{16,8},{20,12},{24,16},{28,20},{1,25},{... | collective-permute-start | bytes 55304 | tf_op jit(solution)/shard_map/ppermute | solution.py:442
  166.6 3.5 %collective-permute-start.20 = (f32[48,96]{0,1:T(8,128)S(1)}, f32[48,96]{0,1:T(8,128)S(1)}, u32[]{:S(2)}, u32[]{:S(2)}) collective-permute-start(f32[48,96]{0,1:T(8,128)S(1)} %add_add_fusion.1), channel_id=1, source_target_pairs={{0,3},{1,0},{2,1},{3,2},{4,7},{5,4},{6,5},{7,6},{8,11},{9,8},{10,9... | collective-permute-start | bytes 55304 | tf_op jit(solution)/shard_map/ppermute | solution.py:442
  172.4 4.4 %cholesky.30 = f32[48,48]{1,0:T(8,128)S(1)} custom-call(f32[48,48]{1,0:T(8,128)S(1)} %copy.28), custom_call_target="Cholesky" | custom-call | tf_op jit(solution)/shard_map/jit(cholesky)/cholesky | solution.py:459
  178.1 3.7 %custom-call.17 = f32[1,48,48]{1,2,0:T(8,128)S(1)} custom-call(f32[1,48,48]{2,1,0:T(8,128)S(1)} %fusion.11), custom_call_target="InvertDiagBlocksLowerTriangular" | custom-call | tf_op jit(solution)/shard_map/jit(_solve_triangular)/triangular_solve | solution.py:468
  187.1 3.8 %fusion.3 = f32[16,8,16,128]{3,0,2,1:T(8,128)S(1)} fusion(f32[32,8,16,128]{3,2,1,0:T(8,128)} %pad_maximum_fusion.1, f32[48,16]{0,1:T(8,128)S(1)} %convolution_multiply_fusion), kind=kOutput, calls=%fused_computation.5 | convolution fusion | flops 100663296 | bytes 3148800 | tf_op jit(solution)/shard_map/lk,lxyz->kxyz/dot_general | solution.py:549
  (113 shorter events, 63.3 us)
Async XLA Ops:
  3.7 108.8 %copy-start = (f32[16,8,16,128]{3,2,1,0:T(8,128)S(1)}, f32[16,8,16,128]{3,2,1,0:T(8,128)}, u32[]{:S(2)}) copy-start(f32[16,8,16,128]{3,2,1,0:T(8,128)} %x_ref.7) | copy-start | bytes 3145732
  3.7 19.8 %collective-permute-start.2 = (f32[16,5,16,128]{3,2,1,0:T(8,128)}, f32[16,5,16,128]{3,2,1,0:T(8,128)S(1)}, u32[]{:S(2)}, u32[]{:S(2)}) collective-permute-start(f32[16,5,16,128]{3,2,1,0:T(8,128)} %get-tuple-element.28), channel_id=1, source_target_pairs={{0,4},{4,8},{8,12},{12,16},{16,20},{20,24},{24,28},{1,5},{5,9},{9,... | collective-permute-start | bytes 1966088 | tf_op jit(solution)/shard_map/ppermute | solution.py:408
  6.3 17.2 %collective-permute-start.3 = (f32[16,5,16,128]{3,2,1,0:T(8,128)}, f32[16,5,16,128]{3,2,1,0:T(8,128)S(1)}, u32[]{:S(2)}, u32[]{:S(2)}) collective-permute-start(f32[16,5,16,128]{3,2,1,0:T(8,128)} %get-tuple-element.29), channel_id=1, source_target_pairs={{4,0},{8,4},{12,8},{16,12},{20,16},{24,20},{28,24},{5,1},{9,5},{13... | collective-permute-start | bytes 1966088 | tf_op jit(solution)/shard_map/ppermute | solution.py:413
  7.6 11.3 %collective-permute-start = (f32[16,40,128]{2,1,0:T(8,128)}, f32[16,40,128]{2,1,0:T(8,128)S(1)}, u32[]{:S(2)}, u32[]{:S(2)}) collective-permute-start(f32[16,40,128]{2,1,0:T(8,128)} %get-tuple-element.26), channel_id=1, source_target_pairs={{0,1},{1,2},{2,3},{4,5},{5,6},{6,7},{8,9},{9,10},{10,11},{12,13},{... | collective-permute-start | bytes 983048 | tf_op jit(solution)/shard_map/ppermute | solution.py:408
  11.9 11.6 %collective-permute-start.1 = (f32[16,40,128]{2,1,0:T(8,128)}, f32[16,40,128]{2,1,0:T(8,128)S(1)}, u32[]{:S(2)}, u32[]{:S(2)}) collective-permute-start(f32[16,40,128]{2,1,0:T(8,128)} %get-tuple-element.27), channel_id=1, source_target_pairs={{1,0},{2,1},{3,2},{5,4},{6,5},{7,6},{9,8},{10,9},{11,10},{13,12},{... | collective-permute-start | bytes 983048 | tf_op jit(solution)/shard_map/ppermute | solution.py:413
  31.4 21.0 %collective-permute-start.4 = (f32[16,32,128]{2,1,0:T(8,128)}, f32[16,32,128]{2,1,0:T(8,128)S(1)}, u32[]{:S(2)}, u32[]{:S(2)}) collective-permute-start(f32[16,32,128]{2,1,0:T(8,128)} %get-tuple-element.31), channel_id=1, source_target_pairs={{0,4},{4,8},{8,12},{12,16},{16,20},{20,24},{24,28},{1,5},{5,9},{9,... | collective-permute-start | bytes 786440 | tf_op jit(solution)/shard_map/ppermute | solution.py:408
  34.3 18.1 %collective-permute-start.5 = (f32[16,32,128]{2,1,0:T(8,128)}, f32[16,32,128]{2,1,0:T(8,128)S(1)}, u32[]{:S(2)}, u32[]{:S(2)}) collective-permute-start(f32[16,32,128]{2,1,0:T(8,128)} %get-tuple-element.32), channel_id=1, source_target_pairs={{4,0},{8,4},{12,8},{16,12},{20,16},{24,20},{28,24},{5,1},{9,5},{13... | collective-permute-start | bytes 786440 | tf_op jit(solution)/shard_map/ppermute | solution.py:413
  35.6 16.8 %all-to-all-start = ((f32[32,8,128]{2,1,0:T(8,128)}), f32[32,8,128]{2,1,0:T(8,128)S(1)}, u32[]{:S(2)}, u32[]{:S(2)}) async-start(f32[32,8,128]{2,1,0:T(8,128)} %get-tuple-element.30), calls=%async_computation | async-start | bytes 262144 | tf_op jit(solution)/shard_map/all_to_all | solution.py:498
  65.6 3.7 %collective-permute-start.6 = (f32[96,128]{1,0:T(8,128)}, f32[96,128]{1,0:T(8,128)S(1)}, u32[]{:S(2)}, u32[]{:S(2)}) collective-permute-start(f32[96,128]{1,0:T(8,128)} %get-tuple-element.34), channel_id=1, source_target_pairs={{0,1},{1,2},{2,3},{4,5},{5,6},{6,7},{8,9},{9,10},{10,11},{12,13},{... | collective-permute-start | bytes 147464 | tf_op jit(solution)/shard_map/ppermute | solution.py:408
  67.1 6.2 %collective-permute-start.7 = (f32[96,128]{1,0:T(8,128)}, f32[96,128]{1,0:T(8,128)S(1)}, u32[]{:S(2)}, u32[]{:S(2)}) collective-permute-start(f32[96,128]{1,0:T(8,128)} %get-tuple-element.35), channel_id=1, source_target_pairs={{1,0},{2,1},{3,2},{5,4},{6,5},{7,6},{9,8},{10,9},{11,10},{13,12},{... | collective-permute-start | bytes 147464 | tf_op jit(solution)/shard_map/ppermute | solution.py:413
  75.6 2.8 %collective-permute-start.8 = (f32[336,128]{1,0:T(8,128)}, f32[336,128]{1,0:T(8,128)S(1)}, u32[]{:S(2)}, u32[]{:S(2)}) collective-permute-start(f32[336,128]{1,0:T(8,128)} %get-tuple-element.36), channel_id=1, source_target_pairs={{0,4},{4,8},{8,12},{12,16},{16,20},{20,24},{24,28},{1,5},{5,9},{9,... | collective-permute-start | bytes 516104 | tf_op jit(solution)/shard_map/ppermute | solution.py:408
  77.1 4.6 %collective-permute-start.9 = (f32[336,128]{1,0:T(8,128)}, f32[336,128]{1,0:T(8,128)S(1)}, u32[]{:S(2)}, u32[]{:S(2)}) collective-permute-start(f32[336,128]{1,0:T(8,128)} %get-tuple-element.37), channel_id=1, source_target_pairs={{4,0},{8,4},{12,8},{16,12},{20,16},{24,20},{28,24},{5,1},{9,5},{13... | collective-permute-start | bytes 516104 | tf_op jit(solution)/shard_map/ppermute | solution.py:413
  88.1 6.4 %collective-permute-start.10 = (f32[16,24,128]{2,1,0:T(8,128)}, f32[16,24,128]{2,1,0:T(8,128)S(1)}, u32[]{:S(2)}, u32[]{:S(2)}) collective-permute-start(f32[16,24,128]{2,1,0:T(8,128)} %get-tuple-element.40), channel_id=1, source_target_pairs={{0,1},{1,2},{2,3},{4,5},{5,6},{6,7},{8,9},{9,10},{10,11},{12,13},{... | collective-permute-start | bytes 589832 | tf_op jit(solution)/shard_map/ppermute | solution.py:408
  91.0 7.8 %collective-permute-start.11 = (f32[16,24,128]{2,1,0:T(8,128)}, f32[16,24,128]{2,1,0:T(8,128)S(1)}, u32[]{:S(2)}, u32[]{:S(2)}) collective-permute-start(f32[16,24,128]{2,1,0:T(8,128)} %get-tuple-element.41), channel_id=1, source_target_pairs={{1,0},{2,1},{3,2},{5,4},{6,5},{7,6},{9,8},{10,9},{11,10},{13,12},{... | collective-permute-start | bytes 589832 | tf_op jit(solution)/shard_map/ppermute | solution.py:413
  104.0 15.6 %collective-permute-start.12 = (f32[16,66,128]{2,0,1:T(8,128)}, f32[16,66,128]{2,0,1:T(8,128)}, u32[]{:S(2)}, u32[]{:S(2)}) collective-permute-start(f32[16,66,128]{2,0,1:T(8,128)} %copy.18), channel_id=1, source_target_pairs={{0,4},{4,8},{8,12},{12,16},{16,20},{20,24},{24,28},{1,5},{5,9},{9,... | collective-permute-start | bytes 1622024 | tf_op jit(solution)/shard_map/ppermute | solution.py:408
  111.1 21.5 %copy-start.2 = (f32[16,8,16,128]{3,2,1,0:T(8,128)S(1)}, f32[16,8,16,128]{3,2,1,0:T(8,128)}, u32[]{:S(2)}) copy-start(f32[16,8,16,128]{3,2,1,0:T(8,128)} %p_ref.3) | copy-start | bytes 3145732
  111.1 10.4 %collective-permute-start.13 = (f32[16,66,128]{2,0,1:T(8,128)}, f32[16,66,128]{2,0,1:T(8,128)}, u32[]{:S(2)}, u32[]{:S(2)}) collective-permute-start(f32[16,66,128]{2,0,1:T(8,128)} %copy.19), channel_id=1, source_target_pairs={{4,0},{8,4},{12,8},{16,12},{20,16},{24,20},{28,24},{5,1},{9,5},{13... | collective-permute-start | bytes 1622024 | tf_op jit(solution)/shard_map/ppermute | solution.py:413
  153.4 4.8 %collective-permute-start.14 = (f32[48,96]{0,1:T(8,128)S(1)}, f32[48,96]{0,1:T(8,128)S(1)}, u32[]{:S(2)}, u32[]{:S(2)}) collective-permute-start(f32[48,96]{0,1:T(8,128)S(1)} %fusion.5), channel_id=1, source_target_pairs={{0,4},{4,0},{8,12},{12,8},{16,20},{20,16},{24,28},{28,24},{1,5},{5... | collective-permute-start | bytes 55304 | tf_op jit(solution)/shard_map/ppermute | solution.py:442
  158.3 4.9 %collective-permute-start.15 = (f32[48,96]{0,1:T(8,128)S(1)}, f32[48,96]{0,1:T(8,128)S(1)}, u32[]{:S(2)}, u32[]{:S(2)}) collective-permute-start(f32[48,96]{0,1:T(8,128)S(1)} %add.56), channel_id=1, source_target_pairs={{0,16},{4,20},{8,24},{12,28},{16,0},{20,4},{24,8},{28,12},{1,17},{... | collective-permute-start | bytes 55304 | tf_op jit(solution)/shard_map/ppermute | solution.py:442
  160.3 5.0 %collective-permute-start.16 = (f32[48,96]{0,1:T(8,128)S(1)}, f32[48,96]{0,1:T(8,128)S(1)}, u32[]{:S(2)}, u32[]{:S(2)}) collective-permute-start(f32[48,96]{0,1:T(8,128)S(1)} %add.56), channel_id=1, source_target_pairs={{0,8},{4,12},{8,16},{12,20},{16,24},{20,28},{24,0},{28,4},{1,9},{5... | collective-permute-start | bytes 55304 | tf_op jit(solution)/shard_map/ppermute | solution.py:442
  160.3 5.0 %collective-permute-start.17 = (f32[48,96]{0,1:T(8,128)S(1)}, f32[48,96]{0,1:T(8,128)S(1)}, u32[]{:S(2)}, u32[]{:S(2)}) collective-permute-start(f32[48,96]{0,1:T(8,128)S(1)} %add.56), channel_id=1, source_target_pairs={{0,24},{4,28},{8,0},{12,4},{16,8},{20,12},{24,16},{28,20},{1,25},{... | collective-permute-start | bytes 55304 | tf_op jit(solution)/shard_map/ppermute | solution.py:442
  165.3 6.3 %collective-permute-start.18 = (f32[48,96]{0,1:T(8,128)S(1)}, f32[48,96]{0,1:T(8,128)S(1)}, u32[]{:S(2)}, u32[]{:S(2)}) collective-permute-start(f32[48,96]{0,1:T(8,128)S(1)} %add_add_fusion.1), channel_id=1, source_target_pairs={{0,2},{1,3},{2,0},{3,1},{4,6},{5,7},{6,4},{7,5},{8,10},{9,11},{10,... | collective-permute-start | bytes 55304 | tf_op jit(solution)/shard_map/ppermute | solution.py:442
  166.3 5.9 %collective-permute-start.19 = (f32[48,96]{0,1:T(8,128)S(1)}, f32[48,96]{0,1:T(8,128)S(1)}, u32[]{:S(2)}, u32[]{:S(2)}) collective-permute-start(f32[48,96]{0,1:T(8,128)S(1)} %add_add_fusion.1), channel_id=1, source_target_pairs={{0,1},{1,2},{2,3},{3,0},{4,5},{5,6},{6,7},{7,4},{8,9},{9,10},{10,1... | collective-permute-start | bytes 55304 | tf_op jit(solution)/shard_map/ppermute | solution.py:442
  166.6 5.6 %collective-permute-start.20 = (f32[48,96]{0,1:T(8,128)S(1)}, f32[48,96]{0,1:T(8,128)S(1)}, u32[]{:S(2)}, u32[]{:S(2)}) collective-permute-start(f32[48,96]{0,1:T(8,128)S(1)} %add_add_fusion.1), channel_id=1, source_target_pairs={{0,3},{1,0},{2,1},{3,2},{4,7},{5,4},{6,5},{7,6},{8,11},{9,8},{10,9... | collective-permute-start | bytes 55304 | tf_op jit(solution)/shard_map/ppermute | solution.py:442
  (18 other events, 60.9 us)
where the time goes:
time: 196 us; the launch traced here: 195 us
  starting transfers between devices  52.1 us (27%)
  Pallas kernels  45.7 us (23%)
  waiting for transfers between devices  36.1 us (18%)
  local copies, waits for them, and re-layouts  22.7 us (12%)
  matrix products  20 us (10%)
  other arithmetic  17.3 us (9%)
    pallas_call x8, Pallas kernels, call(): pl.pallas_call(kernel, out_shape=outs, in_specs=specs, out_specs=[VMEM] *...  45.7 us
    ppermute x7, starting transfers between devices, from_low(): return lax.ppermute(value, axis, [(i, i + 1) for i in range(count - 1)])  20.8 us
    ppermute x7, waiting for transfers between devices, from_high(): return lax.ppermute(value, axis, [(i + 1, i) for i in range(count - 1)])  16.1 us
    dot_general x1, matrix products, body(): part = jnp.einsum('kxyz,lxyz->kl', basis, both, precision=hp)  13.7 us
    ppermute x7, starting transfers between devices, sum_all(): parts.append(lax.ppermute(value, axis, pairs))  13.7 us
    unnamed x47, local copies, waits for them, and re-layouts  13.3 us
    ppermute x7, starting transfers between devices, from_high(): return lax.ppermute(value, axis, [(i + 1, i) for i in range(count - 1)])  9.16 us
    ppermute x7, waiting for transfers between devices, from_low(): return lax.ppermute(value, axis, [(i, i + 1) for i in range(count - 1)])  8.78 us
  transfers between devices with their start and end apart: 22, of which 11 were waited for; matrix products, arithmetic and copies ran while one was open for 4% of the time, Pallas kernels for 3%

commit v1 on v0

--- a/solution.py
+++ b/solution.py
@@ -47,6 +47,13 @@
     total = before + after
     total = total + work[i, pl.ds(row - 1, rows), :] + work[i, pl.ds(row + 1, rows), :]
     return total + along_z(center, step, lanes)
+
+
+def dot_nt(a, b):
+    return lax.dot_general(
+        a, b, (((1,), (1,)), ((), ())),
+        precision=lax.Precision.HIGHEST, preferred_element_type=F32,
+    )
 
 
 def lane_index(rows):
@@ -72,11 +79,11 @@
     lax.fori_loop(0, cols, body, 0)
 
 
-def theta_kernel(x_ref, ylo, yhi, xlo, xhi, out_ref, clo, chi, work):
+def theta_kernel(x_ref, ylo, yhi, xlo, xhi, out_ref, clo, chi, work, parts):
     cols, nx, ny, _ = x_ref.shape
     lanes = lane_index(ny)
-    spot = lane_index(8)
     half = nx // 2 * DEEP
+    parts[pl.ds(2 * cols * 8, 128 * 8 - 2 * cols * 8), :] = jnp.ones((128 * 8 - 2 * cols * 8, 128), F32)
 
     def body(f, carry):
         work[0, pl.ds(PAD, ny), :] = xlo[f, DEEP - 1]
@@ -95,18 +102,25 @@
             numer = numer + center * image
             denom = denom + center * center
             before, center = center, after
-        numer = jnp.sum(numer, axis=(0, 1), keepdims=True)
-        denom = jnp.sum(denom, axis=(0, 1), keepdims=True)
+        parts[pl.ds(pl.multiple_of(f * 8, 8), 8), :] = numer[0:8] + numer[8:16]
+        parts[pl.ds(pl.multiple_of((cols + f) * 8, 8), 8), :] = denom[0:8] + denom[8:16]
         clo[f, pl.ds(0, half), :] = ylo[f, pl.ds(0, half), :]
         clo[f, pl.ds(half, half), :] = yhi[f, pl.ds(0, half), :]
         chi[f, pl.ds(0, half), :] = ylo[f, pl.ds(half, half), :]
         chi[f, pl.ds(half, half), :] = yhi[f, pl.ds(half, half), :]
-        carry = jnp.where(spot == f, numer, carry)
-        return jnp.where(spot == f + cols, denom, carry)
-
-    sums = lax.fori_loop(0, cols, body, jnp.zeros((8, 128), F32))
-    for k in range(out_ref.shape[0]):
+        return carry
+
+    lax.fori_loop(0, cols, body, 0)
+    total = parts[pl.ds(0, 128, stride=8), :]
+    for k in range(1, 8):
+        total = total + parts[pl.ds(k, 128, stride=8), :]
+    sums = dot_nt(jnp.ones((8, 128), F32), total)
+
+    def spread(k, carry):
         out_ref[k] = sums
+        return carry
+
+    lax.fori_loop(0, out_ref.shape[0], spread, 0)
 
 
 def pre_kernel(
@@ -305,11 +319,11 @@
     def body(f, carry):
         for out, first in ((xlo, 0), (xhi, nx - POST)):
             for i in range(POST):
-                at = i * tall
+                at = (f * POST + i) * tall
                 src = pl.ds((first + i) * POST, POST)
-                out[f, pl.ds(at, POST), :] = ylo[f, src, :]
-                out[f, pl.ds(at + POST, ny), :] = corr_ref[f, first + i]
-                out[f, pl.ds(at + POST + ny, POST), :] = yhi[f, src, :]
+                out[pl.ds(at, POST), :] = ylo[f, src, :]
+                out[pl.ds(at + POST, ny), :] = corr_ref[f, first + i]
+                out[pl.ds(at + POST + ny, POST), :] = yhi[f, src, :]
         return carry
 
     lax.fori_loop(0, cols, body, 0)
@@ -345,8 +359,9 @@
 
     def body(f, carry):
         for i in range(POST):
-            work[i, pl.ds(PAD + gap, span), :] = xlo[f, pl.ds(i * span, span), :]
-            work[nx + POST + i, pl.ds(PAD + gap, span), :] = xhi[f, pl.ds(i * span, span), :]
+            at = pl.ds((f * POST + i) * span, span)
+            work[i, pl.ds(PAD + gap, span), :] = xlo[at, :]
+            work[nx + POST + i, pl.ds(PAD + gap, span), :] = xhi[at, :]
         for i in range(nx):
             at = pl.ds(i * POST, POST)
             work[i + POST, pl.ds(PAD + gap, POST), :] = ylo[f, at, :]
@@ -453,24 +468,111 @@
     return value
 
 
-def ritz_coef(gram, proj, ncells):
-    hp = lax.Precision.HIGHEST
-    proj = 0.5 * (proj + proj.T)
-    lower = jnp.linalg.cholesky(gram)
-    inner = jax.scipy.linalg.solve_triangular(lower, proj, lower=True)
-    ritz = jax.scipy.linalg.solve_triangular(lower, inner.T, lower=True)
-    ritz = 0.5 * (ritz + ritz.T)
-    nbasis = gram.shape[0]
-    kcount = nbasis // 3
-    filtered = SHIFT * jnp.eye(nbasis, dtype=jnp.float32)[:, :kcount] - ritz[:, :kcount]
-    small = jnp.linalg.cholesky(jnp.dot(filtered.T, filtered, precision=hp))
-    scaled = jax.scipy.linalg.solve_triangular(small, filtered.T, lower=True).T
-    coef = jax.scipy.linalg.solve_triangular(lower, scaled, lower=True, trans="T")
-    return coef * jnp.sqrt(jnp.float32(ncells))
+BF16 = jnp.bfloat16
+
+
+def gram_kernel(x_ref, w_ref, p_ref, ax_ref, aw_ref, ap_ref, out_ref, s_ref, image):
+    chunks, rows, wide = s_ref.shape
+    cols = rows // 6
+    ny = wide // 128
+    stride = x_ref.shape[0] // cols
+
+    def body(c, carry):
+        for k, (b_ref, a_ref) in enumerate(((x_ref, ax_ref), (w_ref, aw_ref), (p_ref, ap_ref))):
+            for y in range(ny):
+                pick = pl.ds(c * ny + y, cols, stride=stride)
+                at = pl.ds(y * 128, 128)
+                for ref, put in (
+                    (b_ref, lambda r, v: s_ref.__setitem__((c, r, at), v)),
+                    (a_ref, lambda r, v: image.__setitem__((r, at), v)),
+                ):
+                    value = ref[pick, :]
+                    high = value.astype(BF16)
+                    low = (value - high.astype(F32)).astype(BF16)
+                    put(pl.ds(k * cols, cols), high)
+                    put(pl.ds((3 + k) * cols, cols), low)
+        left = s_ref[c]
+        dims = (((1,), (1,)), ((), ()))
+        proj = lax.dot_general(left, image[...], dims, preferred_element_type=F32)
+        gram = lax.dot_general(left, left, dims, preferred_element_type=F32)
+        return (carry[0] + proj, carry[1] + gram)
+
+    zero = jnp.zeros((rows, rows), F32)
+    proj, gram = lax.fori_loop(0, chunks, body, (zero, zero))
+    nb = 3 * cols
+    for k, full in enumerate((proj, gram)):
+        full = full[:nb] + full[nb:]
+        out_ref[:, pl.ds(k * nb, nb)] = full[:, :nb] + full[:, nb:]
+
+
+def eliminate(left, right, first):
+    size = left.shape[0]
+    row = lax.broadcasted_iota(jnp.int32, (size, 1), 0)
+    scale = jnp.zeros((size, 1), F32)
+    for k in range(size):
+        pivot = left[k : k + 1, first + k : first + k + 1]
+        column = left[:, first + k : first + k + 1]
+        factor = jnp.where(row > k, column / pivot, 0.0)
+        scale = jnp.where(row == k, pivot, scale)
+        line, other = left[k : k + 1], right[k : k + 1]
+        left = left - factor * line
+        right = right - factor * other
+    scale = lax.rsqrt(scale)
+    return left * scale, right * scale
+
+
+def finish_kernel(ncells, sums_ref, s_ref, block_ref, search_ref, bufs, sems):
+    nb = sums_ref.shape[0]
+    cols = nb // 3
+    chunks, rows, wide = s_ref.shape
+    ny = wide // 128
+    row = lax.broadcasted_iota(jnp.int32, (nb, 128), 0)
+    lane = lax.broadcasted_iota(jnp.int32, (nb, 128), 1)
+    eye = jnp.where((lane == row) | (lane == row + nb), 1.0, 0.0)
+    left, inverse = eliminate(sums_ref[...], eye, nb)
+    flat = -dot_nt(inverse[:cols, :nb], left[:, :nb])
+    flat = flat + jnp.where(lane[:cols, :nb] == row[:cols, :nb], SHIFT, 0.0)
+    _, scaled = eliminate(dot_nt(flat, flat), flat, 0)
+    coef = jnp.dot(
+        scaled, inverse, precision=lax.Precision.HIGHEST, preferred_element_type=F32
+    )
+    coef = coef[:, :rows] * jnp.sqrt(F32(ncells))
+    slot = lax.broadcasted_iota(jnp.int32, (cols, rows), 1)
+    first = (slot < cols) | ((slot >= nb) & (slot < nb + cols))
+    terms = []
+    for part in (jnp.where(first, coef, 0.0), jnp.where(first, 0.0, coef)):
+        high = part.astype(BF16)
+        terms += [high, (part - high.astype(F32)).astype(BF16)]
+    terms = jnp.concatenate(terms, axis=0)
+
+    def copies(c, slot):
+        return [
+            pltpu.make_async_copy(bufs.at[slot, k], ref.at[:, c], sems.at[slot, k])
+            for k, ref in enumerate((block_ref, search_ref))
+        ]
+
+    for c in range(chunks):
+        slot = c % 2
+        if c >= 2:
+            for copy in copies(c - 2, slot):
+                copy.wait()
+        for y in range(0, ny, 2):
+            got = jnp.dot(
+                terms, s_ref[c, :, pl.ds(y * 128, 256)], preferred_element_type=F32
+            )
+            search = got[2 * cols : 3 * cols] + got[3 * cols :]
+            block = search + (got[:cols] + got[cols : 2 * cols])
+            for k, value in enumerate((block, search)):
+                for j in range(2):
+                    bufs[slot, k, :, y + j, :] = value[:, j * 128 : (j + 1) * 128]
+        for copy in copies(c, slot):
+            copy.start()
+    for c in range(max(chunks - 2, 0), chunks):
+        for copy in copies(c, c % 2):
+            copy.wait()
 
 
 def body(x, p):
-    hp = lax.Precision.HIGHEST
     cols, nx, ny, nz = x.shape
     ngx, ngy = lax.axis_size("gx"), lax.axis_size("gy")
     ix, iy = lax.axis_index("gx"), lax.axis_index("gy")
@@ -491,7 +593,7 @@
     sums, to_clo, to_chi = call(
         theta_kernel,
         [shape(devices, 8, 128)] + [shape(cols, nx * DEEP, nz)] * 2,
-        [work((nx + 2, PAD + ny + 8, nz), F32)],
+        [work((nx + 2, PAD + ny + 8, nz), F32), work((128 * 8, nz), F32)],
         (x, ylo, yhi, xlo, xhi), "theta",
     )
     clo, chi = from_low(to_chi, "gx"), from_high(to_clo, "gx")
@@ -524,7 +626,7 @@
 
     eylo, eyhi = from_low(to_yhi, "gy"), from_high(to_ylo, "gy")
     to_xlo, to_xhi = call(
-        post_pack_kernel, [shape(cols, POST * (ny + 2 * POST), nz)] * 2, [], (corr, eylo, eyhi), "ppack"
+        post_pack_kernel, [shape(cols * POST * (ny + 2 * POST), nz)] * 2, [], (corr, eylo, eyhi), "ppack"
     )
     exlo, exhi = from_low(to_xhi, "gx"), from_high(to_xlo, "gx")
 
@@ -539,15 +641,27 @@
         (flags, corr, eylo, eyhi, exlo, exhi, r), "post", smem=1,
     )
 
-    basis = jnp.concatenate([x, w, p], axis=0)
-    images = jnp.concatenate([image_x, image_w, image_p], axis=0)
-    both = jnp.concatenate([basis, images], axis=0)
-    part = jnp.einsum("kxyz,lxyz->kl", basis, both, precision=hp)
+    flat = [v.reshape(cols * nx * ny, nz) for v in (x, w, p, image_x, image_w, image_p)]
+    nb = 3 * cols
+    part, split = call(
+        gram_kernel,
+        [shape(nb, 128), jax.ShapeDtypeStruct((nx, 2 * nb, ny * nz), BF16)],
+        [work((2 * nb, ny * nz), BF16)],
+        flat, "gram",
+    )
     part = sum_all(part)
-    nb = 3 * cols
-    coef = ritz_coef(part[:, :nb], part[:, nb:], nx * ny * nz * devices)
-    new_search = jnp.einsum("lk,lxyz->kxyz", coef[cols:], basis[cols:], precision=hp)
-    new_block = new_search + jnp.einsum("lk,lxyz->kxyz", coef[:cols], x, precision=hp)
+    any_space = pl.BlockSpec(memory_space=pl.ANY)
+    new_block, new_search = pl.pallas_call(
+        functools.partial(finish_kernel, nx * ny * nz * devices),
+        out_shape=[shape(cols, nx, ny, nz)] * 2,
+        in_specs=[VMEM, VMEM],
+        out_specs=[any_space] * 2,
+        scratch_shapes=[
+            work((2, 2, cols, ny, nz), F32),
+            pltpu.SemaphoreType.DMA((2, 2)),
+        ],
+        name="finish",
+    )(part, split)
     return (new_block, new_search)
 
 

time: 196 us -> 171 us (0.87)
  Pallas kernels: 45.7 us -> 67.8 us
  matrix products: 20 us -> 0 us
  local copies, waits for them, and re-layouts: 22.7 us -> 6.21 us
  other arithmetic: 17.3 us -> 2.02 us
  starting transfers between devices: 52.1 us -> 55.1 us
    dot_general x4 -> x0, matrix products: 19.2 us -> none  [the longest x1 13.7 us: body(): part = jnp.einsum('kxyz,lxyz->kl', basis, both, precision=hp)]
    another operation x11 -> x0, other arithmetic: 13.4 us -> none  [the longest x4 5.07 us: ritz_coef(): lower = jnp.linalg.cholesky(gram)]
    pallas_call x0 -> x1, Pallas kernels: none -> 12.3 us  [body(): pl.pallas_call(functools.partial(finish_kernel, nx * ny * nz * devices),...]
    pallas_call x8 -> x9, Pallas kernels: 45.7 us -> 55.5 us  [call(): pl.pallas_call(kernel, out_shape=outs, in_specs=specs, out_specs=[VMEM] *...]
    unnamed x47 -> x30, local copies, waits for them, and re-layouts: 13.3 us -> 6.21 us
    ppermute x2 -> x0, local copies, waits for them, and re-layouts: 4.09 us -> none  [the longest x1 2.05 us: from_low(): return lax.ppermute(value, axis, [(i, i + 1) for i in range(count - 1)])]
    ppermute x7, starting transfers between devices: 13.7 us -> 17.7 us  [sum_all(): parts.append(lax.ppermute(value, axis, pairs))]
    pallas_call x2 -> x0, local copies, waits for them, and re-layouts: 3.96 us -> none  [call(): pl.pallas_call(kernel, out_shape=outs, in_specs=specs, out_specs=[VMEM] *...]
  transfers between devices with their start and end apart: 22 -> 22, of which waited for: 11 -> 13; matrix products, arithmetic and copies ran while one was open for 4% -> 0% of each run, Pallas kernels for 3% -> 3%
where the time goes in v1:
time: 171 us; the launch traced here: 170 us
  Pallas kernels  67.8 us (40%)
  starting transfers between devices  55.1 us (32%)
  waiting for transfers between devices  37.8 us (22%)
  local copies, waits for them, and re-layouts  6.21 us (4%)
  other arithmetic  2.02 us (1%)
    pallas_call x9, Pallas kernels, call(): pl.pallas_call(kernel, out_shape=outs, in_specs=specs, out_specs=[VMEM] *...  55.5 us
    ppermute x7, starting transfers between devices, from_low(): return lax.ppermute(value, axis, [(i, i + 1) for i in range(count - 1)])  19.9 us
    ppermute x7, starting transfers between devices, sum_all(): parts.append(lax.ppermute(value, axis, pairs))  17.7 us
    ppermute x7, waiting for transfers between devices, from_high(): return lax.ppermute(value, axis, [(i + 1, i) for i in range(count - 1)])  16.1 us
    pallas_call x1, Pallas kernels, body(): pl.pallas_call(functools.partial(finish_kernel, nx * ny * nz * devices),...  12.3 us
    ppermute x7, starting transfers between devices, from_high(): return lax.ppermute(value, axis, [(i + 1, i) for i in range(count - 1)])  9.04 us
    ppermute x7, waiting for transfers between devices, from_low(): return lax.ppermute(value, axis, [(i, i + 1) for i in range(count - 1)])  8.78 us
    all_to_all x1, starting transfers between devices, body(): sums = lax.all_to_all(sums, ('gx', 'gy'), 0, 0)  8.44 us
  transfers between devices with their start and end apart: 22, of which 13 were waited for; matrix products, arithmetic and copies ran while one was open for 0% of the time, Pallas kernels for 3%

profile of v1, /device:TPU:0, one launch (start us, length us, event | category | flops | bytes accessed | tf_op | source)
XLA Modules:
  0.0 169.8 jit_solution(14128003945657051535)
XLA Ops:
  0.6 3.1 %pack.1 = (f32[16,40,128]{2,1,0:T(8,128)}, f32[16,40,128]{2,1,0:T(8,128)}, f32[16,5,16,128]{3,2,1,0:T(8,128)}, f32[16,5,16,128]{3,2,1,0:T(8,128)}) custom-call(f32[16,8,16,128]{3,2,1,0:T(8,128)} %x_ref.7, f32[16,8,16,128]{3,2,1,0:T(8,128)} %p_ref.3), custom_call_target="tpu_custom_call" | custom-call | tf_op jit(solution)/shard_map/pack/pallas_call | solution.py:29
  3.7 2.4 %collective-permute-start.2 = (f32[16,5,16,128]{3,2,1,0:T(8,128)}, f32[16,5,16,128]{3,2,1,0:T(8,128)S(1)}, u32[]{:S(2)}, u32[]{:S(2)}) collective-permute-start(f32[16,5,16,128]{3,2,1,0:T(8,128)} %get-tuple-element.29), channel_id=1, source_target_pairs={{0,4},{4,8},{8,12},{12,16},{16,20},{20,24},{24,28},{1,5},{5,9},{9,... | collective-permute-start | bytes 1966088 | tf_op jit(solution)/shard_map/ppermute | solution.py:423
  7.5 4.3 %collective-permute-start = (f32[16,40,128]{2,1,0:T(8,128)}, f32[16,40,128]{2,1,0:T(8,128)S(1)}, u32[]{:S(2)}, u32[]{:S(2)}) collective-permute-start(f32[16,40,128]{2,1,0:T(8,128)} %get-tuple-element.27), channel_id=1, source_target_pairs={{0,1},{1,2},{2,3},{4,5},{5,6},{6,7},{8,9},{9,10},{10,11},{12,13},{... | collective-permute-start | bytes 983048 | tf_op jit(solution)/shard_map/ppermute | solution.py:423
  13.1 5.7 %collective-permute-done.ylo = f32[16,40,128]{2,1,0:T(8,128)S(1)} collective-permute-done((f32[16,40,128]{2,1,0:T(8,128)}, f32[16,40,128]{2,1,0:T(8,128)S(1)}, u32[]{:S(2)}, u32[]{:S(2)}) %collective-permute-start) | collective-permute-done | bytes 327712 | tf_op jit(solution)/shard_map/ppermute | solution.py:423
  18.8 4.6 %collective-permute-done.1.yhi = f32[16,40,128]{2,1,0:T(8,128)S(1)} collective-permute-done((f32[16,40,128]{2,1,0:T(8,128)}, f32[16,40,128]{2,1,0:T(8,128)S(1)}, u32[]{:S(2)}, u32[]{:S(2)}) %collective-permute-start.1) | collective-permute-done | bytes 327712 | tf_op jit(solution)/shard_map/ppermute | solution.py:428
  25.2 4.8 %theta.1 = (f32[32,8,128]{2,1,0:T(8,128)}, f32[16,32,128]{2,1,0:T(8,128)}, f32[16,32,128]{2,1,0:T(8,128)}) custom-call(f32[16,8,16,128]{3,2,1,0:T(8,128)} %x_ref.7, f32[16,40,128]{2,1,0:T(8,128)} %copy-done.2, f32[16,40,128]{2,1,0:T(8,128)} %copy-done.3, f32[16,5,16,128]{3,2,1,0:T(8,128)} %copy-done, f32[16,5,16,128]{3,2,1,0:T(8,128)} %copy-done.1), custom_call_target="tpu_custom_call" | custom-call | tf_op jit(solution)/shard_map/theta/pallas_call | solution.py:29
  30.0 2.8 %collective-permute-start.4 = (f32[16,32,128]{2,1,0:T(8,128)}, f32[16,32,128]{2,1,0:T(8,128)S(1)}, u32[]{:S(2)}, u32[]{:S(2)}) collective-permute-start(f32[16,32,128]{2,1,0:T(8,128)} %get-tuple-element.32), channel_id=1, source_target_pairs={{0,4},{4,8},{8,12},{12,16},{16,20},{20,24},{24,28},{1,5},{5,9},{9,... | collective-permute-start | bytes 786440 | tf_op jit(solution)/shard_map/ppermute | solution.py:423
  34.2 8.4 %all-to-all-start = ((f32[32,8,128]{2,1,0:T(8,128)}), f32[32,8,128]{2,1,0:T(8,128)S(1)}, u32[]{:S(2)}, u32[]{:S(2)}) async-start(f32[32,8,128]{2,1,0:T(8,128)} %get-tuple-element.31), calls=%async_computation | async-start | bytes 262144 | tf_op jit(solution)/shard_map/all_to_all | solution.py:600
  43.3 7.7 %all-to-all-done.sums = f32[32,8,128]{2,1,0:T(8,128)S(1)} async-done(((f32[32,8,128]{2,1,0:T(8,128)}), f32[32,8,128]{2,1,0:T(8,128)S(1)}, u32[]{:S(2)}, u32[]{:S(2)}) %all-to-all-start) | async-done | bytes 131104 | tf_op jit(solution)/shard_map/all_to_all | solution.py:600
  52.4 11.7 %pre.1 = (f32[16,12,24,128]{3,2,1,0:T(8,128)}, f32[16,8,16,128]{3,2,1,0:T(8,128)}, f32[8,4,8,128]{3,2,1,0:T(8,128)}, f32[96,128]{1,0:T(8,128)}, f32[96,128]{1,0:T(8,128)}) custom-call(s32[4]{0:T(128)} %add_convert_fusion.flags, f32[32,8,128]{2,1,0:T(8,128)} %copy-done.8, f32[16,8,16,128]{3,2,1,0:T(8,128)} %x_ref.7, f32[16,40,128]{2,1,0:T(8,128)} %copy-done.2, ...), custom_call_target="tpu_custom_call" | custom-call | tf_op jit(solution)/shard_map/pre/pallas_call | solution.py:29
  67.8 4.0 %collective-permute-done.7.yhi = f32[96,128]{1,0:T(8,128)S(1)} collective-permute-done((f32[96,128]{1,0:T(8,128)}, f32[96,128]{1,0:T(8,128)S(1)}, u32[]{:S(2)}, u32[]{:S(2)}) %collective-permute-start.7) | collective-permute-done | bytes 49184 | tf_op jit(solution)/shard_map/ppermute | solution.py:428
  77.0 3.2 %collective-permute-done.9.xhi = f32[336,128]{1,0:T(8,128)S(1)} collective-permute-done((f32[336,128]{1,0:T(8,128)}, f32[336,128]{1,0:T(8,128)S(1)}, u32[]{:S(2)}, u32[]{:S(2)}) %collective-permute-start.9) | collective-permute-done | bytes 172064 | tf_op jit(solution)/shard_map/ppermute | solution.py:428
  80.9 5.7 %coarse.1 = (f32[16,8,16,128]{3,2,1,0:T(8,128)}, f32[16,24,128]{2,1,0:T(8,128)}, f32[16,24,128]{2,1,0:T(8,128)}) custom-call(s32[4]{0:T(128)} %add_convert_fusion.flags, f32[8,4,8,128]{3,2,1,0:T(8,128)} %get-tuple-element.34.c_ref, f32[96,128]{1,0:T(8,128)} %copy-done.11, f32[96,128]{1,0:T(8,128)} %copy-done.12, f32[336,128]{1,0:T(8,128)} %copy-done.13, ...), custom_call_target="tpu_custom_call" | custom-call | tf_op jit(solution)/shard_map/coarse/pallas_call | solution.py:29
  86.6 2.9 %collective-permute-start.10 = (f32[16,24,128]{2,1,0:T(8,128)}, f32[16,24,128]{2,1,0:T(8,128)S(1)}, u32[]{:S(2)}, u32[]{:S(2)}) collective-permute-start(f32[16,24,128]{2,1,0:T(8,128)} %get-tuple-element.41), channel_id=1, source_target_pairs={{0,1},{1,2},{2,3},{4,5},{5,6},{6,7},{8,9},{9,10},{10,11},{12,13},{... | collective-permute-start | bytes 589832 | tf_op jit(solution)/shard_map/ppermute | solution.py:423
  93.0 4.3 %collective-permute-done.11.yhi = f32[16,24,128]{2,1,0:T(8,128)S(1)} collective-permute-done((f32[16,24,128]{2,1,0:T(8,128)}, f32[16,24,128]{2,1,0:T(8,128)S(1)}, u32[]{:S(2)}, u32[]{:S(2)}) %collective-permute-start.11) | collective-permute-done | bytes 196640 | tf_op jit(solution)/shard_map/ppermute | solution.py:428
  98.0 2.5 %ppack.1 = (f32[1056,128]{1,0:T(8,128)}, f32[1056,128]{1,0:T(8,128)}) custom-call(f32[16,8,16,128]{3,2,1,0:T(8,128)} %get-tuple-element.40.corr_ref, f32[16,24,128]{2,1,0:T(8,128)} %copy-done.4, f32[16,24,128]{2,1,0:T(8,128)} %copy-done.5), custom_call_target="tpu_custom_call" | custom-call | tf_op jit(solution)/shard_map/ppack/pallas_call | solution.py:29
  100.5 4.4 %collective-permute-start.12 = (f32[1056,128]{1,0:T(8,128)}, f32[1056,128]{1,0:T(8,128)S(1)}, u32[]{:S(2)}, u32[]{:S(2)}) collective-permute-start(f32[1056,128]{1,0:T(8,128)} %get-tuple-element.43), channel_id=1, source_target_pairs={{0,4},{4,8},{8,12},{12,16},{16,20},{20,24},{24,28},{1,5},{5,9},{9,... | collective-permute-start | bytes 1622024 | tf_op jit(solution)/shard_map/ppermute | solution.py:423
  106.2 5.8 %image.1 = (f32[16,8,16,128]{3,2,1,0:T(8,128)}, f32[16,8,16,128]{3,2,1,0:T(8,128)}) custom-call(f32[16,8,16,128]{3,2,1,0:T(8,128)} %x_ref.7, f32[16,8,16,128]{3,2,1,0:T(8,128)} %p_ref.3, f32[16,40,128]{2,1,0:T(8,128)} %copy-done.2, f32[16,40,128]{2,1,0:T(8,128)} %copy-done.3, f32[16,5,16,128]{3,2,1,0:T(8,128)} %copy-done, f32[16,5,16,128]{3,2,1,0:T(8,128)} %copy-done.1), custom_call_target="tpu_custom_call" | custom-call | tf_op jit(solution)/shard_map/image/pallas_call | solution.py:29
  113.0 9.0 %post.1 = (f32[16,8,16,128]{3,2,1,0:T(8,128)}, f32[16,8,16,128]{3,2,1,0:T(8,128)}) custom-call(s32[4]{0:T(128)} %add_convert_fusion.flags, f32[16,8,16,128]{3,2,1,0:T(8,128)} %get-tuple-element.40.corr_ref, f32[16,24,128]{2,1,0:T(8,128)} %copy-done.4, f32[16,24,128]{2,1,0:T(8,128)} %copy-done.5, f32[1056,128]{1,0:T(8,128)} %copy-done.6, ...), custom_call_target="tpu_custom_call" | custom-call | tf_op jit(solution)/shard_map/post/pallas_call | solution.py:29
  122.0 11.2 %gram.1 = (f32[48,128]{1,0:T(8,128)}, bf16[8,96,2048]{2,1,0:T(8,128)(2,1)}) custom-call(f32[2048,128]{1,0:T(8,128)} %bitcast.10, f32[2048,128]{1,0:T(8,128)} %bitcast.14, f32[2048,128]{1,0:T(8,128)} %bitcast.11, f32[2048,128]{1,0:T(8,128)} %bitcast.12, f32[2048,128]{1,0:T(8,128)} %bitcast.15, f32[2048,128]{1,0:T(8,128)} %bitcast.13), custom_call_target="tpu_custom_call" | custom-call | tf_op jit(solution)/shard_map/gram/pallas_call | solution.py:29
  133.2 9.7 %collective-permute-start.14 = (f32[48,128]{1,0:T(8,128)}, f32[48,128]{1,0:T(8,128)S(1)}, u32[]{:S(2)}, u32[]{:S(2)}) collective-permute-start(f32[48,128]{1,0:T(8,128)} %get-tuple-element.50), channel_id=1, source_target_pairs={{0,4},{4,0},{8,12},{12,8},{16,20},{20,16},{24,28},{28,24},{1,5},{5... | collective-permute-start | bytes 73736 | tf_op jit(solution)/shard_map/ppermute | solution.py:457
  145.0 2.9 %collective-permute-start.17 = (f32[48,128]{1,0:T(8,128)S(1)}, f32[48,128]{1,0:T(8,128)S(1)}, u32[]{:S(2)}, u32[]{:S(2)}) collective-permute-start(f32[48,128]{1,0:T(8,128)S(1)} %add.21), channel_id=1, source_target_pairs={{0,24},{4,28},{8,0},{12,4},{16,8},{20,12},{24,16},{28,20},{1,25},{... | collective-permute-start | bytes 73736 | tf_op jit(solution)/shard_map/ppermute | solution.py:457
  151.6 3.5 %collective-permute-start.20 = (f32[48,128]{1,0:T(8,128)S(1)}, f32[48,128]{1,0:T(8,128)S(1)}, u32[]{:S(2)}, u32[]{:S(2)}) collective-permute-start(f32[48,128]{1,0:T(8,128)S(1)} %add_add_fusion.1), channel_id=1, source_target_pairs={{0,3},{1,0},{2,1},{3,2},{4,7},{5,4},{6,5},{7,6},{8,11},{9,8},{10,9... | collective-permute-start | bytes 73736 | tf_op jit(solution)/shard_map/ppermute | solution.py:457
  157.5 12.3 %finish.1 = (f32[16,8,16,128]{3,2,1,0:T(8,128)}, f32[16,8,16,128]{3,2,1,0:T(8,128)}) custom-call(f32[48,128]{1,0:T(8,128)} %add_add_fusion.sums_ref, bf16[8,96,2048]{2,1,0:T(8,128)(2,1)} %get-tuple-element.51.s_ref), custom_call_target="tpu_custom_call" | custom-call | tf_op jit(solution)/shard_map/finish/pallas_call | solution.py:654
  (64 shorter events, 31.9 us)
Async XLA Ops:
  3.7 19.6 %collective-permute-start.2 = (f32[16,5,16,128]{3,2,1,0:T(8,128)}, f32[16,5,16,128]{3,2,1,0:T(8,128)S(1)}, u32[]{:S(2)}, u32[]{:S(2)}) collective-permute-start(f32[16,5,16,128]{3,2,1,0:T(8,128)} %get-tuple-element.29), channel_id=1, source_target_pairs={{0,4},{4,8},{8,12},{12,16},{16,20},{20,24},{24,28},{1,5},{5,9},{9,... | collective-permute-start | bytes 1966088 | tf_op jit(solution)/shard_map/ppermute | solution.py:423
  6.2 17.2 %collective-permute-start.3 = (f32[16,5,16,128]{3,2,1,0:T(8,128)}, f32[16,5,16,128]{3,2,1,0:T(8,128)S(1)}, u32[]{:S(2)}, u32[]{:S(2)}) collective-permute-start(f32[16,5,16,128]{3,2,1,0:T(8,128)} %get-tuple-element.30), channel_id=1, source_target_pairs={{4,0},{8,4},{12,8},{16,12},{20,16},{24,20},{28,24},{5,1},{9,5},{13... | collective-permute-start | bytes 1966088 | tf_op jit(solution)/shard_map/ppermute | solution.py:428
  7.5 11.3 %collective-permute-start = (f32[16,40,128]{2,1,0:T(8,128)}, f32[16,40,128]{2,1,0:T(8,128)S(1)}, u32[]{:S(2)}, u32[]{:S(2)}) collective-permute-start(f32[16,40,128]{2,1,0:T(8,128)} %get-tuple-element.27), channel_id=1, source_target_pairs={{0,1},{1,2},{2,3},{4,5},{5,6},{6,7},{8,9},{9,10},{10,11},{12,13},{... | collective-permute-start | bytes 983048 | tf_op jit(solution)/shard_map/ppermute | solution.py:423
  11.8 11.6 %collective-permute-start.1 = (f32[16,40,128]{2,1,0:T(8,128)}, f32[16,40,128]{2,1,0:T(8,128)S(1)}, u32[]{:S(2)}, u32[]{:S(2)}) collective-permute-start(f32[16,40,128]{2,1,0:T(8,128)} %get-tuple-element.28), channel_id=1, source_target_pairs={{1,0},{2,1},{3,2},{5,4},{6,5},{7,6},{9,8},{10,9},{11,10},{13,12},{... | collective-permute-start | bytes 983048 | tf_op jit(solution)/shard_map/ppermute | solution.py:428
  18.8 4.6 %copy-start.2 = (f32[16,40,128]{2,1,0:T(8,128)}, f32[16,40,128]{2,1,0:T(8,128)S(1)}, u32[]{:S(2)}) copy-start(f32[16,40,128]{2,1,0:T(8,128)S(1)} %collective-permute-done.ylo) | copy-start | bytes 983044
  30.0 21.0 %collective-permute-start.4 = (f32[16,32,128]{2,1,0:T(8,128)}, f32[16,32,128]{2,1,0:T(8,128)S(1)}, u32[]{:S(2)}, u32[]{:S(2)}) collective-permute-start(f32[16,32,128]{2,1,0:T(8,128)} %get-tuple-element.32), channel_id=1, source_target_pairs={{0,4},{4,8},{8,12},{12,16},{16,20},{20,24},{24,28},{1,5},{5,9},{9,... | collective-permute-start | bytes 786440 | tf_op jit(solution)/shard_map/ppermute | solution.py:423
  32.9 18.1 %collective-permute-start.5 = (f32[16,32,128]{2,1,0:T(8,128)}, f32[16,32,128]{2,1,0:T(8,128)S(1)}, u32[]{:S(2)}, u32[]{:S(2)}) collective-permute-start(f32[16,32,128]{2,1,0:T(8,128)} %get-tuple-element.33), channel_id=1, source_target_pairs={{4,0},{8,4},{12,8},{16,12},{20,16},{24,20},{28,24},{5,1},{9,5},{13... | collective-permute-start | bytes 786440 | tf_op jit(solution)/shard_map/ppermute | solution.py:428
  34.2 16.8 %all-to-all-start = ((f32[32,8,128]{2,1,0:T(8,128)}), f32[32,8,128]{2,1,0:T(8,128)S(1)}, u32[]{:S(2)}, u32[]{:S(2)}) async-start(f32[32,8,128]{2,1,0:T(8,128)} %get-tuple-element.31), calls=%async_computation | async-start | bytes 262144 | tf_op jit(solution)/shard_map/all_to_all | solution.py:600
  64.2 3.7 %collective-permute-start.6 = (f32[96,128]{1,0:T(8,128)}, f32[96,128]{1,0:T(8,128)S(1)}, u32[]{:S(2)}, u32[]{:S(2)}) collective-permute-start(f32[96,128]{1,0:T(8,128)} %get-tuple-element.35), channel_id=1, source_target_pairs={{0,1},{1,2},{2,3},{4,5},{5,6},{6,7},{8,9},{9,10},{10,11},{12,13},{... | collective-permute-start | bytes 147464 | tf_op jit(solution)/shard_map/ppermute | solution.py:423
  65.6 6.2 %collective-permute-start.7 = (f32[96,128]{1,0:T(8,128)}, f32[96,128]{1,0:T(8,128)S(1)}, u32[]{:S(2)}, u32[]{:S(2)}) collective-permute-start(f32[96,128]{1,0:T(8,128)} %get-tuple-element.36), channel_id=1, source_target_pairs={{1,0},{2,1},{3,2},{5,4},{6,5},{7,6},{9,8},{10,9},{11,10},{13,12},{... | collective-permute-start | bytes 147464 | tf_op jit(solution)/shard_map/ppermute | solution.py:428
  74.2 2.8 %collective-permute-start.8 = (f32[336,128]{1,0:T(8,128)}, f32[336,128]{1,0:T(8,128)S(1)}, u32[]{:S(2)}, u32[]{:S(2)}) collective-permute-start(f32[336,128]{1,0:T(8,128)} %get-tuple-element.37), channel_id=1, source_target_pairs={{0,4},{4,8},{8,12},{12,16},{16,20},{20,24},{24,28},{1,5},{5,9},{9,... | collective-permute-start | bytes 516104 | tf_op jit(solution)/shard_map/ppermute | solution.py:423
  75.7 4.6 %collective-permute-start.9 = (f32[336,128]{1,0:T(8,128)}, f32[336,128]{1,0:T(8,128)S(1)}, u32[]{:S(2)}, u32[]{:S(2)}) collective-permute-start(f32[336,128]{1,0:T(8,128)} %get-tuple-element.38), channel_id=1, source_target_pairs={{4,0},{8,4},{12,8},{16,12},{20,16},{24,20},{28,24},{5,1},{9,5},{13... | collective-permute-start | bytes 516104 | tf_op jit(solution)/shard_map/ppermute | solution.py:428
  86.6 6.4 %collective-permute-start.10 = (f32[16,24,128]{2,1,0:T(8,128)}, f32[16,24,128]{2,1,0:T(8,128)S(1)}, u32[]{:S(2)}, u32[]{:S(2)}) collective-permute-start(f32[16,24,128]{2,1,0:T(8,128)} %get-tuple-element.41), channel_id=1, source_target_pairs={{0,1},{1,2},{2,3},{4,5},{5,6},{6,7},{8,9},{9,10},{10,11},{12,13},{... | collective-permute-start | bytes 589832 | tf_op jit(solution)/shard_map/ppermute | solution.py:423
  89.6 7.8 %collective-permute-start.11 = (f32[16,24,128]{2,1,0:T(8,128)}, f32[16,24,128]{2,1,0:T(8,128)S(1)}, u32[]{:S(2)}, u32[]{:S(2)}) collective-permute-start(f32[16,24,128]{2,1,0:T(8,128)} %get-tuple-element.42), channel_id=1, source_target_pairs={{1,0},{2,1},{3,2},{5,4},{6,5},{7,6},{9,8},{10,9},{11,10},{13,12},{... | collective-permute-start | bytes 589832 | tf_op jit(solution)/shard_map/ppermute | solution.py:428
  93.0 4.3 %copy-start.4 = (f32[16,24,128]{2,1,0:T(8,128)}, f32[16,24,128]{2,1,0:T(8,128)S(1)}, u32[]{:S(2)}) copy-start(f32[16,24,128]{2,1,0:T(8,128)S(1)} %collective-permute-done.10.ylo) | copy-start | bytes 589828
  100.5 11.5 %collective-permute-start.12 = (f32[1056,128]{1,0:T(8,128)}, f32[1056,128]{1,0:T(8,128)S(1)}, u32[]{:S(2)}, u32[]{:S(2)}) collective-permute-start(f32[1056,128]{1,0:T(8,128)} %get-tuple-element.43), channel_id=1, source_target_pairs={{0,4},{4,8},{8,12},{12,16},{16,20},{20,24},{24,28},{1,5},{5,9},{9,... | collective-permute-start | bytes 1622024 | tf_op jit(solution)/shard_map/ppermute | solution.py:423
  104.9 7.1 %collective-permute-start.13 = (f32[1056,128]{1,0:T(8,128)}, f32[1056,128]{1,0:T(8,128)S(1)}, u32[]{:S(2)}, u32[]{:S(2)}) collective-permute-start(f32[1056,128]{1,0:T(8,128)} %get-tuple-element.44), channel_id=1, source_target_pairs={{4,0},{8,4},{12,8},{16,12},{20,16},{24,20},{28,24},{5,1},{9,5},{13... | collective-permute-start | bytes 1622024 | tf_op jit(solution)/shard_map/ppermute | solution.py:428
  133.2 10.7 %collective-permute-start.14 = (f32[48,128]{1,0:T(8,128)}, f32[48,128]{1,0:T(8,128)S(1)}, u32[]{:S(2)}, u32[]{:S(2)}) collective-permute-start(f32[48,128]{1,0:T(8,128)} %get-tuple-element.50), channel_id=1, source_target_pairs={{0,4},{4,0},{8,12},{12,8},{16,20},{20,16},{24,28},{28,24},{1,5},{5... | collective-permute-start | bytes 73736 | tf_op jit(solution)/shard_map/ppermute | solution.py:457
  144.7 3.8 %collective-permute-start.15 = (f32[48,128]{1,0:T(8,128)S(1)}, f32[48,128]{1,0:T(8,128)S(1)}, u32[]{:S(2)}, u32[]{:S(2)}) collective-permute-start(f32[48,128]{1,0:T(8,128)S(1)} %add.21), channel_id=1, source_target_pairs={{0,16},{4,20},{8,24},{12,28},{16,0},{20,4},{24,8},{28,12},{1,17},{... | collective-permute-start | bytes 73736 | tf_op jit(solution)/shard_map/ppermute | solution.py:457
  145.0 4.7 %collective-permute-start.16 = (f32[48,128]{1,0:T(8,128)S(1)}, f32[48,128]{1,0:T(8,128)S(1)}, u32[]{:S(2)}, u32[]{:S(2)}) collective-permute-start(f32[48,128]{1,0:T(8,128)S(1)} %add.21), channel_id=1, source_target_pairs={{0,8},{4,12},{8,16},{12,20},{16,24},{20,28},{24,0},{28,4},{1,9},{5... | collective-permute-start | bytes 73736 | tf_op jit(solution)/shard_map/ppermute | solution.py:457
  145.0 5.3 %collective-permute-start.17 = (f32[48,128]{1,0:T(8,128)S(1)}, f32[48,128]{1,0:T(8,128)S(1)}, u32[]{:S(2)}, u32[]{:S(2)}) collective-permute-start(f32[48,128]{1,0:T(8,128)S(1)} %add.21), channel_id=1, source_target_pairs={{0,24},{4,28},{8,0},{12,4},{16,8},{20,12},{24,16},{28,20},{1,25},{... | collective-permute-start | bytes 73736 | tf_op jit(solution)/shard_map/ppermute | solution.py:457
  150.2 4.8 %collective-permute-start.18 = (f32[48,128]{1,0:T(8,128)S(1)}, f32[48,128]{1,0:T(8,128)S(1)}, u32[]{:S(2)}, u32[]{:S(2)}) collective-permute-start(f32[48,128]{1,0:T(8,128)S(1)} %add_add_fusion.1), channel_id=1, source_target_pairs={{0,2},{1,3},{2,0},{3,1},{4,6},{5,7},{6,4},{7,5},{8,10},{9,11},{10,... | collective-permute-start | bytes 73736 | tf_op jit(solution)/shard_map/ppermute | solution.py:457
  151.2 5.6 %collective-permute-start.19 = (f32[48,128]{1,0:T(8,128)S(1)}, f32[48,128]{1,0:T(8,128)S(1)}, u32[]{:S(2)}, u32[]{:S(2)}) collective-permute-start(f32[48,128]{1,0:T(8,128)S(1)} %add_add_fusion.1), channel_id=1, source_target_pairs={{0,1},{1,2},{2,3},{3,0},{4,5},{5,6},{6,7},{7,4},{8,9},{9,10},{10,1... | collective-permute-start | bytes 73736 | tf_op jit(solution)/shard_map/ppermute | solution.py:457
  151.6 5.3 %collective-permute-start.20 = (f32[48,128]{1,0:T(8,128)S(1)}, f32[48,128]{1,0:T(8,128)S(1)}, u32[]{:S(2)}, u32[]{:S(2)}) collective-permute-start(f32[48,128]{1,0:T(8,128)S(1)} %add_add_fusion.1), channel_id=1, source_target_pairs={{0,3},{1,0},{2,1},{3,2},{4,7},{5,4},{6,5},{7,6},{8,11},{9,8},{10,9... | collective-permute-start | bytes 73736 | tf_op jit(solution)/shard_map/ppermute | solution.py:457
  (13 other events, 15.7 us)

commit v2 on v1

--- a/solution.py
+++ b/solution.py
@@ -15,13 +15,15 @@
 CO = 3
 PAD = 8
 
+GRANT = 20 << 20
+
 F32 = jnp.float32
 VMEM = pl.BlockSpec(memory_space=pltpu.VMEM)
 SMEM = pl.BlockSpec(memory_space=pltpu.SMEM)
 
 
 def shape(*dims):
-    return jax.ShapeDtypeStruct(dims, F32)
+    return pltpu.VMEM(dims, F32)
 
 
 def call(kernel, outs, scratch, args, name, smem=0):
@@ -32,6 +34,7 @@
         in_specs=specs,
         out_specs=[VMEM] * len(outs),
         scratch_shapes=scratch,
+        compiler_params=pltpu.CompilerParams(vmem_limit_bytes=GRANT),
         name=name,
     )(*args)
 
@@ -645,7 +648,7 @@
     nb = 3 * cols
     part, split = call(
         gram_kernel,
-        [shape(nb, 128), jax.ShapeDtypeStruct((nx, 2 * nb, ny * nz), BF16)],
+        [shape(nb, 128), pltpu.VMEM((nx, 2 * nb, ny * nz), BF16)],
         [work((2 * nb, ny * nz), BF16)],
         flat, "gram",
     )
@@ -653,13 +656,14 @@
     any_space = pl.BlockSpec(memory_space=pl.ANY)
     new_block, new_search = pl.pallas_call(
         functools.partial(finish_kernel, nx * ny * nz * devices),
-        out_shape=[shape(cols, nx, ny, nz)] * 2,
+        out_shape=[jax.ShapeDtypeStruct((cols, nx, ny, nz), F32)] * 2,
         in_specs=[VMEM, VMEM],
         out_specs=[any_space] * 2,
         scratch_shapes=[
             work((2, 2, cols, ny, nz), F32),
             pltpu.SemaphoreType.DMA((2, 2)),
         ],
+        compiler_params=pltpu.CompilerParams(vmem_limit_bytes=GRANT),
         name="finish",
     )(part, split)
     return (new_block, new_search)

time: 171 us -> 144 us (0.84)
  Pallas kernels: 67.8 us -> 42.4 us
  starting transfers between devices: 55.1 us -> 57.1 us
  other arithmetic: 2.02 us -> 0.1 us
  local copies, waits for them, and re-layouts: 6.21 us -> 4.4 us
    pallas_call x9, Pallas kernels: 55.5 us -> 32 us  [call(): pl.pallas_call(kernel, out_shape=outs, in_specs=specs, out_specs=[VMEM] *...]
    pallas_call x1, Pallas kernels: 12.3 us -> 10.4 us  [body(): pl.pallas_call(functools.partial(finish_kernel, nx * ny * nz * devices),...]
    ppermute x7, starting transfers between devices: 17.7 us -> 19.5 us  [sum_all(): parts.append(lax.ppermute(value, axis, pairs))]
    unnamed x30 -> x20, local copies, waits for them, and re-layouts: 6.21 us -> 4.4 us
  transfers between devices with their start and end apart: 22 -> 22, of which waited for: 13 -> 14; matrix products, arithmetic and copies ran while one was open for 0% -> 0% of each run, Pallas kernels for 3% -> 2%
where the time goes in v2:
time: 144 us
  starting transfers between devices  57.1 us (40%)
  Pallas kernels  42.4 us (29%)
  waiting for transfers between devices  38.9 us (27%)
  local copies, waits for them, and re-layouts  4.4 us (3%)
    pallas_call x9, Pallas kernels, call(): pl.pallas_call(kernel, out_shape=outs, in_specs=specs, out_specs=[VMEM] *...  32 us
    ppermute x7, starting transfers between devices, from_low(): return lax.ppermute(value, axis, [(i, i + 1) for i in range(count - 1)])  21.6 us
    ppermute x7, starting transfers between devices, sum_all(): parts.append(lax.ppermute(value, axis, pairs))  19.5 us
    ppermute x7, waiting for transfers between devices, from_high(): return lax.ppermute(value, axis, [(i + 1, i) for i in range(count - 1)])  17.8 us
    pallas_call x1, Pallas kernels, body(): pl.pallas_call(functools.partial(finish_kernel, nx * ny * nz * devices),...  10.4 us
    ppermute x7, starting transfers between devices, from_high(): return lax.ppermute(value, axis, [(i + 1, i) for i in range(count - 1)])  9.03 us
    all_to_all x1, waiting for transfers between devices, body(): sums = lax.all_to_all(sums, ('gx', 'gy'), 0, 0)  8.28 us
    ppermute x7, waiting for transfers between devices, from_low(): return lax.ppermute(value, axis, [(i, i + 1) for i in range(count - 1)])  7.83 us
  transfers between devices with their start and end apart: 22, of which 14 were waited for; matrix products, arithmetic and copies ran while one was open for 0% of the time, Pallas kernels for 2%

profile of v2, /device:TPU:0, one launch (start us, length us, event | category | flops | bytes accessed | tf_op | source)
XLA Modules:
  0.0 143.8 jit_solution(4676527623006256587)
XLA Ops:
  3.4 2.6 %collective-permute-start.2 = (f32[16,5,16,128]{3,2,1,0:T(8,128)S(1)}, f32[16,5,16,128]{3,2,1,0:T(8,128)S(1)}, u32[]{:S(2)}, u32[]{:S(2)}) collective-permute-start(f32[16,5,16,128]{3,2,1,0:T(8,128)S(1)} %get-tuple-element.29), channel_id=1, source_target_pairs={{0,4},{4,8},{8,12},{12,16},{16,20},{20,24},{24,28},{1,5},{5,9},{9,... | collective-permute-start | bytes 1966088 | tf_op jit(solution)/shard_map/ppermute | solution.py:426
  7.3 4.3 %collective-permute-start = (f32[16,40,128]{2,1,0:T(8,128)S(1)}, f32[16,40,128]{2,1,0:T(8,128)S(1)}, u32[]{:S(2)}, u32[]{:S(2)}) collective-permute-start(f32[16,40,128]{2,1,0:T(8,128)S(1)} %get-tuple-element.27), channel_id=1, source_target_pairs={{0,1},{1,2},{2,3},{4,5},{5,6},{6,7},{8,9},{9,10},{10,11},{12,13},{... | collective-permute-start | bytes 983048 | tf_op jit(solution)/shard_map/ppermute | solution.py:426
  12.9 5.4 %collective-permute-done.ylo = f32[16,40,128]{2,1,0:T(8,128)S(1)} collective-permute-done((f32[16,40,128]{2,1,0:T(8,128)S(1)}, f32[16,40,128]{2,1,0:T(8,128)S(1)}, u32[]{:S(2)}, u32[]{:S(2)}) %collective-permute-start) | collective-permute-done | bytes 327712 | tf_op jit(solution)/shard_map/ppermute | solution.py:426
  18.3 4.7 %collective-permute-done.1.yhi = f32[16,40,128]{2,1,0:T(8,128)S(1)} collective-permute-done((f32[16,40,128]{2,1,0:T(8,128)S(1)}, f32[16,40,128]{2,1,0:T(8,128)S(1)}, u32[]{:S(2)}, u32[]{:S(2)}) %collective-permute-start.1) | collective-permute-done | bytes 327712 | tf_op jit(solution)/shard_map/ppermute | solution.py:431
  23.0 3.0 %theta.1 = (f32[32,8,128]{2,1,0:T(8,128)}, f32[16,32,128]{2,1,0:T(8,128)}, f32[16,32,128]{2,1,0:T(8,128)}) custom-call(f32[16,8,16,128]{3,2,1,0:T(8,128)S(1)} %copy-done, f32[16,40,128]{2,1,0:T(8,128)S(1)} %collective-permute-done.ylo, f32[16,40,128]{2,1,0:T(8,128)S(1)} %collective-permute-done.1.yhi, f32[16,5,16,128]{3,2,1,0:T(8,128)S(1)} %collective-permute-done.2.xlo, ...), custom_call_target="tpu_custom_call" | custom-call | tf_op jit(solution)/shard_map/theta/pallas_call | solution.py:31
  25.9 4.3 %collective-permute-start.4 = (f32[16,32,128]{2,1,0:T(8,128)}, f32[16,32,128]{2,1,0:T(8,128)}, u32[]{:S(2)}, u32[]{:S(2)}) collective-permute-start(f32[16,32,128]{2,1,0:T(8,128)} %get-tuple-element.32), channel_id=1, source_target_pairs={{0,4},{4,8},{8,12},{12,16},{16,20},{20,24},{24,28},{1,5},{5,9},{9,... | collective-permute-start | bytes 786440 | tf_op jit(solution)/shard_map/ppermute | solution.py:426
  31.6 7.0 %all-to-all-start = ((f32[32,8,128]{2,1,0:T(8,128)}), f32[32,8,128]{2,1,0:T(8,128)S(1)}, u32[]{:S(2)}, u32[]{:S(2)}) async-start(f32[32,8,128]{2,1,0:T(8,128)} %get-tuple-element.31), calls=%async_computation | async-start | bytes 262144 | tf_op jit(solution)/shard_map/all_to_all | solution.py:603
  38.6 8.3 %all-to-all-done.sums = f32[32,8,128]{2,1,0:T(8,128)S(1)} async-done(((f32[32,8,128]{2,1,0:T(8,128)}), f32[32,8,128]{2,1,0:T(8,128)S(1)}, u32[]{:S(2)}, u32[]{:S(2)}) %all-to-all-start) | async-done | bytes 131104 | tf_op jit(solution)/shard_map/all_to_all | solution.py:603
  48.9 9.5 %pre.1 = (f32[16,12,24,128]{3,2,1,0:T(8,128)S(1)}, f32[16,8,16,128]{3,2,1,0:T(8,128)S(1)}, f32[8,4,8,128]{3,2,1,0:T(8,128)S(1)}, f32[96,128]{1,0:T(8,128)S(1)}, f32[96,128]{1,0:T(8,128)S(1)}) custom-call(s32[4]{0:T(128)S(1)} %add_convert_fusion.flags, f32[32,8,128]{2,1,0:T(8,128)S(1)} %all-to-all-done.sums, f32[16,8,16,128]{3,2,1,0:T(8,128)S(1)} %copy-done.1, ...), custom_call_target="tpu_custom_call" | custom-call | tf_op jit(solution)/shard_map/pre/pallas_call | solution.py:31
  61.7 4.1 %collective-permute-done.7.yhi = f32[96,128]{1,0:T(8,128)S(1)} collective-permute-done((f32[96,128]{1,0:T(8,128)S(1)}, f32[96,128]{1,0:T(8,128)S(1)}, u32[]{:S(2)}, u32[]{:S(2)}) %collective-permute-start.7) | collective-permute-done | bytes 49184 | tf_op jit(solution)/shard_map/ppermute | solution.py:431
  68.7 3.0 %collective-permute-done.9.xhi = f32[336,128]{1,0:T(8,128)S(1)} collective-permute-done((f32[336,128]{1,0:T(8,128)S(1)}, f32[336,128]{1,0:T(8,128)S(1)}, u32[]{:S(2)}, u32[]{:S(2)}) %collective-permute-start.9) | collective-permute-done | bytes 172064 | tf_op jit(solution)/shard_map/ppermute | solution.py:431
  71.8 3.6 %coarse.1 = (f32[16,8,16,128]{3,2,1,0:T(8,128)S(1)}, f32[16,24,128]{2,1,0:T(8,128)S(1)}, f32[16,24,128]{2,1,0:T(8,128)S(1)}) custom-call(s32[4]{0:T(128)S(1)} %add_convert_fusion.flags, f32[8,4,8,128]{3,2,1,0:T(8,128)S(1)} %get-tuple-element.34.c_ref, f32[96,128]{1,0:T(8,128)S(1)} %collective-permute-done.6.ylo, f32[96,128]{1,0:T(8,128)S(1)} %collective-permute-done.7.yhi, ...), custom_call_target="tpu_custom_call" | custom-call | tf_op jit(solution)/shard_map/coarse/pallas_call | solution.py:31
  75.4 2.9 %collective-permute-start.10 = (f32[16,24,128]{2,1,0:T(8,128)S(1)}, f32[16,24,128]{2,1,0:T(8,128)S(1)}, u32[]{:S(2)}, u32[]{:S(2)}) collective-permute-start(f32[16,24,128]{2,1,0:T(8,128)S(1)} %get-tuple-element.41), channel_id=1, source_target_pairs={{0,1},{1,2},{2,3},{4,5},{5,6},{6,7},{8,9},{9,10},{10,11},{12,13},{... | collective-permute-start | bytes 589832 | tf_op jit(solution)/shard_map/ppermute | solution.py:426
  79.6 1.9 %collective-permute-done.10.ylo = f32[16,24,128]{2,1,0:T(8,128)S(1)} collective-permute-done((f32[16,24,128]{2,1,0:T(8,128)S(1)}, f32[16,24,128]{2,1,0:T(8,128)S(1)}, u32[]{:S(2)}, u32[]{:S(2)}) %collective-permute-start.10) | collective-permute-done | bytes 196640 | tf_op jit(solution)/shard_map/ppermute | solution.py:426
  81.5 4.4 %collective-permute-done.11.yhi = f32[16,24,128]{2,1,0:T(8,128)S(1)} collective-permute-done((f32[16,24,128]{2,1,0:T(8,128)S(1)}, f32[16,24,128]{2,1,0:T(8,128)S(1)}, u32[]{:S(2)}, u32[]{:S(2)}) %collective-permute-start.11) | collective-permute-done | bytes 196640 | tf_op jit(solution)/shard_map/ppermute | solution.py:431
  86.1 4.4 %collective-permute-start.12 = (f32[1056,128]{1,0:T(8,128)S(1)}, f32[1056,128]{1,0:T(8,128)S(1)}, u32[]{:S(2)}, u32[]{:S(2)}) collective-permute-start(f32[1056,128]{1,0:T(8,128)S(1)} %get-tuple-element.43), channel_id=1, source_target_pairs={{0,4},{4,8},{8,12},{12,16},{16,20},{20,24},{24,28},{1,5},{5,9},{9,... | collective-permute-start | bytes 1622024 | tf_op jit(solution)/shard_map/ppermute | solution.py:426
  91.8 2.4 %image.1 = (f32[16,8,16,128]{3,2,1,0:T(8,128)S(1)}, f32[16,8,16,128]{3,2,1,0:T(8,128)S(1)}) custom-call(f32[16,8,16,128]{3,2,1,0:T(8,128)S(1)} %copy-done.1, f32[16,8,16,128]{3,2,1,0:T(8,128)S(1)} %copy-done.3, f32[16,40,128]{2,1,0:T(8,128)S(1)} %copy-done.6, f32[16,40,128]{2,1,0:T(8,128)S(1)} %copy-done.9, ...), custom_call_target="tpu_custom_call" | custom-call | tf_op jit(solution)/shard_map/image/pallas_call | solution.py:31
  95.8 5.8 %post.1 = (f32[16,8,16,128]{3,2,1,0:T(8,128)S(1)}, f32[16,8,16,128]{3,2,1,0:T(8,128)S(1)}) custom-call(s32[4]{0:T(128)S(1)} %add_convert_fusion.flags, f32[16,8,16,128]{3,2,1,0:T(8,128)S(1)} %get-tuple-element.40.corr_ref, f32[16,24,128]{2,1,0:T(8,128)S(1)} %collective-permute-done.10.ylo, f32[16,24,128]{2,1,0:T(8,128)S(1)} %collective-permute-done.11.yhi, ...), custom_call_target="tpu_custom_call" | custom-call | tf_op jit(solution)/shard_map/post/pallas_call | solution.py:31
  101.6 7.2 %gram.1 = (f32[48,128]{1,0:T(8,128)S(1)}, bf16[8,96,2048]{2,1,0:T(8,128)(2,1)S(1)}) custom-call(f32[2048,128]{1,0:T(8,128)S(1)} %bitcast.10, f32[2048,128]{1,0:T(8,128)S(1)} %bitcast.14, f32[2048,128]{1,0:T(8,128)S(1)} %bitcast.11, f32[2048,128]{1,0:T(8,128)S(1)} %bitcast.12, f32[2048,128]{1,0:T(8,128)S(1)} %bitcast.15, f32[2048,128]{1,0:T(8,128)S(1)} %bitcast.13), custom_call_target="tpu_custom_call" | custom-call | tf_op jit(solution)/shard_map/gram/pallas_call | solution.py:31
  108.8 11.5 %collective-permute-start.14 = (f32[48,128]{1,0:T(8,128)S(1)}, f32[48,128]{1,0:T(8,128)S(1)}, u32[]{:S(2)}, u32[]{:S(2)}) collective-permute-start(f32[48,128]{1,0:T(8,128)S(1)} %get-tuple-element.50), channel_id=1, source_target_pairs={{0,4},{4,0},{8,12},{12,8},{16,20},{20,16},{24,28},{28,24},{1,5},{5... | collective-permute-start | bytes 73736 | tf_op jit(solution)/shard_map/ppermute | solution.py:460
  121.5 2.9 %collective-permute-start.17 = (f32[48,128]{1,0:T(8,128)S(1)}, f32[48,128]{1,0:T(8,128)S(1)}, u32[]{:S(2)}, u32[]{:S(2)}) collective-permute-start(f32[48,128]{1,0:T(8,128)S(1)} %add.21), channel_id=1, source_target_pairs={{0,24},{4,28},{8,0},{12,4},{16,8},{20,12},{24,16},{28,20},{1,25},{... | collective-permute-start | bytes 73736 | tf_op jit(solution)/shard_map/ppermute | solution.py:460
  128.1 3.5 %collective-permute-start.20 = (f32[48,128]{1,0:T(8,128)S(1)}, f32[48,128]{1,0:T(8,128)S(1)}, u32[]{:S(2)}, u32[]{:S(2)}) collective-permute-start(f32[48,128]{1,0:T(8,128)S(1)} %add_add_fusion.1), channel_id=1, source_target_pairs={{0,3},{1,0},{2,1},{3,2},{4,7},{5,4},{6,5},{7,6},{8,11},{9,8},{10,9... | collective-permute-start | bytes 73736 | tf_op jit(solution)/shard_map/ppermute | solution.py:460
  131.5 1.8 %collective-permute-done.19 = f32[48,128]{1,0:T(8,128)S(1)} collective-permute-done((f32[48,128]{1,0:T(8,128)S(1)}, f32[48,128]{1,0:T(8,128)S(1)}, u32[]{:S(2)}, u32[]{:S(2)}) %collective-permute-start.19) | collective-permute-done | bytes 24608 | tf_op jit(solution)/shard_map/ppermute | solution.py:460
  133.4 10.4 %finish.1 = (f32[16,8,16,128]{3,2,1,0:T(8,128)}, f32[16,8,16,128]{3,2,1,0:T(8,128)}) custom-call(f32[48,128]{1,0:T(8,128)S(1)} %add_add_fusion.sums_ref, bf16[8,96,2048]{2,1,0:T(8,128)(2,1)S(1)} %get-tuple-element.51.s_ref), custom_call_target="tpu_custom_call" | custom-call | tf_op jit(solution)/shard_map/finish/pallas_call | solution.py:657
  (54 shorter events, 24.0 us)
Async XLA Ops:
  3.1 43.9 %copy-start.1 = (f32[16,8,16,128]{3,2,1,0:T(8,128)S(1)}, f32[16,8,16,128]{3,2,1,0:T(8,128)}, u32[]{:S(2)}) copy-start(f32[16,8,16,128]{3,2,1,0:T(8,128)} %x_ref.7) | copy-start | bytes 3145732
  3.4 19.6 %collective-permute-start.2 = (f32[16,5,16,128]{3,2,1,0:T(8,128)S(1)}, f32[16,5,16,128]{3,2,1,0:T(8,128)S(1)}, u32[]{:S(2)}, u32[]{:S(2)}) collective-permute-start(f32[16,5,16,128]{3,2,1,0:T(8,128)S(1)} %get-tuple-element.29), channel_id=1, source_target_pairs={{0,4},{4,8},{8,12},{12,16},{16,20},{20,24},{24,28},{1,5},{5,9},{9,... | collective-permute-start | bytes 1966088 | tf_op jit(solution)/shard_map/ppermute | solution.py:426
  6.0 17.0 %collective-permute-start.3 = (f32[16,5,16,128]{3,2,1,0:T(8,128)S(1)}, f32[16,5,16,128]{3,2,1,0:T(8,128)S(1)}, u32[]{:S(2)}, u32[]{:S(2)}) collective-permute-start(f32[16,5,16,128]{3,2,1,0:T(8,128)S(1)} %get-tuple-element.30), channel_id=1, source_target_pairs={{4,0},{8,4},{12,8},{16,12},{20,16},{24,20},{28,24},{5,1},{9,5},{13... | collective-permute-start | bytes 1966088 | tf_op jit(solution)/shard_map/ppermute | solution.py:431
  7.3 11.0 %collective-permute-start = (f32[16,40,128]{2,1,0:T(8,128)S(1)}, f32[16,40,128]{2,1,0:T(8,128)S(1)}, u32[]{:S(2)}, u32[]{:S(2)}) collective-permute-start(f32[16,40,128]{2,1,0:T(8,128)S(1)} %get-tuple-element.27), channel_id=1, source_target_pairs={{0,1},{1,2},{2,3},{4,5},{5,6},{6,7},{8,9},{9,10},{10,11},{12,13},{... | collective-permute-start | bytes 983048 | tf_op jit(solution)/shard_map/ppermute | solution.py:426
  11.6 11.4 %collective-permute-start.1 = (f32[16,40,128]{2,1,0:T(8,128)S(1)}, f32[16,40,128]{2,1,0:T(8,128)S(1)}, u32[]{:S(2)}, u32[]{:S(2)}) collective-permute-start(f32[16,40,128]{2,1,0:T(8,128)S(1)} %get-tuple-element.28), channel_id=1, source_target_pairs={{1,0},{2,1},{3,2},{5,4},{6,5},{7,6},{9,8},{10,9},{11,10},{13,12},{... | collective-permute-start | bytes 983048 | tf_op jit(solution)/shard_map/ppermute | solution.py:431
  25.9 21.0 %collective-permute-start.4 = (f32[16,32,128]{2,1,0:T(8,128)}, f32[16,32,128]{2,1,0:T(8,128)}, u32[]{:S(2)}, u32[]{:S(2)}) collective-permute-start(f32[16,32,128]{2,1,0:T(8,128)} %get-tuple-element.32), channel_id=1, source_target_pairs={{0,4},{4,8},{8,12},{12,16},{16,20},{20,24},{24,28},{1,5},{5,9},{9,... | collective-permute-start | bytes 786440 | tf_op jit(solution)/shard_map/ppermute | solution.py:426
  30.3 16.6 %collective-permute-start.5 = (f32[16,32,128]{2,1,0:T(8,128)}, f32[16,32,128]{2,1,0:T(8,128)}, u32[]{:S(2)}, u32[]{:S(2)}) collective-permute-start(f32[16,32,128]{2,1,0:T(8,128)} %get-tuple-element.33), channel_id=1, source_target_pairs={{4,0},{8,4},{12,8},{16,12},{20,16},{24,20},{28,24},{5,1},{9,5},{13... | collective-permute-start | bytes 786440 | tf_op jit(solution)/shard_map/ppermute | solution.py:431
  31.6 15.4 %all-to-all-start = ((f32[32,8,128]{2,1,0:T(8,128)}), f32[32,8,128]{2,1,0:T(8,128)S(1)}, u32[]{:S(2)}, u32[]{:S(2)}) async-start(f32[32,8,128]{2,1,0:T(8,128)} %get-tuple-element.31), calls=%async_computation | async-start | bytes 262144 | tf_op jit(solution)/shard_map/all_to_all | solution.py:603
  38.6 53.2 %copy-start.3 = (f32[16,8,16,128]{3,2,1,0:T(8,128)S(1)}, f32[16,8,16,128]{3,2,1,0:T(8,128)}, u32[]{:S(2)}) copy-start(f32[16,8,16,128]{3,2,1,0:T(8,128)} %p_ref.3) | copy-start | bytes 3145732
  58.4 3.4 %collective-permute-start.6 = (f32[96,128]{1,0:T(8,128)S(1)}, f32[96,128]{1,0:T(8,128)S(1)}, u32[]{:S(2)}, u32[]{:S(2)}) collective-permute-start(f32[96,128]{1,0:T(8,128)S(1)} %get-tuple-element.35), channel_id=1, source_target_pairs={{0,1},{1,2},{2,3},{4,5},{5,6},{6,7},{8,9},{9,10},{10,11},{12,13},{... | collective-permute-start | bytes 147464 | tf_op jit(solution)/shard_map/ppermute | solution.py:426
  59.8 6.0 %collective-permute-start.7 = (f32[96,128]{1,0:T(8,128)S(1)}, f32[96,128]{1,0:T(8,128)S(1)}, u32[]{:S(2)}, u32[]{:S(2)}) collective-permute-start(f32[96,128]{1,0:T(8,128)S(1)} %get-tuple-element.36), channel_id=1, source_target_pairs={{1,0},{2,1},{3,2},{5,4},{6,5},{7,6},{9,8},{10,9},{11,10},{13,12},{... | collective-permute-start | bytes 147464 | tf_op jit(solution)/shard_map/ppermute | solution.py:431
  65.9 2.8 %collective-permute-start.8 = (f32[336,128]{1,0:T(8,128)S(1)}, f32[336,128]{1,0:T(8,128)S(1)}, u32[]{:S(2)}, u32[]{:S(2)}) collective-permute-start(f32[336,128]{1,0:T(8,128)S(1)} %get-tuple-element.37), channel_id=1, source_target_pairs={{0,4},{4,8},{8,12},{12,16},{16,20},{20,24},{24,28},{1,5},{5,9},{9,... | collective-permute-start | bytes 516104 | tf_op jit(solution)/shard_map/ppermute | solution.py:426
  67.4 4.4 %collective-permute-start.9 = (f32[336,128]{1,0:T(8,128)S(1)}, f32[336,128]{1,0:T(8,128)S(1)}, u32[]{:S(2)}, u32[]{:S(2)}) collective-permute-start(f32[336,128]{1,0:T(8,128)S(1)} %get-tuple-element.38), channel_id=1, source_target_pairs={{4,0},{8,4},{12,8},{16,12},{20,16},{24,20},{28,24},{5,1},{9,5},{13... | collective-permute-start | bytes 516104 | tf_op jit(solution)/shard_map/ppermute | solution.py:431
  75.4 6.1 %collective-permute-start.10 = (f32[16,24,128]{2,1,0:T(8,128)S(1)}, f32[16,24,128]{2,1,0:T(8,128)S(1)}, u32[]{:S(2)}, u32[]{:S(2)}) collective-permute-start(f32[16,24,128]{2,1,0:T(8,128)S(1)} %get-tuple-element.41), channel_id=1, source_target_pairs={{0,1},{1,2},{2,3},{4,5},{5,6},{6,7},{8,9},{9,10},{10,11},{12,13},{... | collective-permute-start | bytes 589832 | tf_op jit(solution)/shard_map/ppermute | solution.py:426
  78.3 7.6 %collective-permute-start.11 = (f32[16,24,128]{2,1,0:T(8,128)S(1)}, f32[16,24,128]{2,1,0:T(8,128)S(1)}, u32[]{:S(2)}, u32[]{:S(2)}) collective-permute-start(f32[16,24,128]{2,1,0:T(8,128)S(1)} %get-tuple-element.42), channel_id=1, source_target_pairs={{1,0},{2,1},{3,2},{5,4},{6,5},{7,6},{9,8},{10,9},{11,10},{13,12},{... | collective-permute-start | bytes 589832 | tf_op jit(solution)/shard_map/ppermute | solution.py:431
  86.1 8.1 %collective-permute-start.12 = (f32[1056,128]{1,0:T(8,128)S(1)}, f32[1056,128]{1,0:T(8,128)S(1)}, u32[]{:S(2)}, u32[]{:S(2)}) collective-permute-start(f32[1056,128]{1,0:T(8,128)S(1)} %get-tuple-element.43), channel_id=1, source_target_pairs={{0,4},{4,8},{8,12},{12,16},{16,20},{20,24},{24,28},{1,5},{5,9},{9,... | collective-permute-start | bytes 1622024 | tf_op jit(solution)/shard_map/ppermute | solution.py:426
  90.5 5.3 %collective-permute-start.13 = (f32[1056,128]{1,0:T(8,128)S(1)}, f32[1056,128]{1,0:T(8,128)S(1)}, u32[]{:S(2)}, u32[]{:S(2)}) collective-permute-start(f32[1056,128]{1,0:T(8,128)S(1)} %get-tuple-element.44), channel_id=1, source_target_pairs={{4,0},{8,4},{12,8},{16,12},{20,16},{24,20},{28,24},{5,1},{9,5},{13... | collective-permute-start | bytes 1622024 | tf_op jit(solution)/shard_map/ppermute | solution.py:431
  108.8 12.3 %collective-permute-start.14 = (f32[48,128]{1,0:T(8,128)S(1)}, f32[48,128]{1,0:T(8,128)S(1)}, u32[]{:S(2)}, u32[]{:S(2)}) collective-permute-start(f32[48,128]{1,0:T(8,128)S(1)} %get-tuple-element.50), channel_id=1, source_target_pairs={{0,4},{4,0},{8,12},{12,8},{16,20},{20,16},{24,28},{28,24},{1,5},{5... | collective-permute-start | bytes 73736 | tf_op jit(solution)/shard_map/ppermute | solution.py:460
  121.2 3.8 %collective-permute-start.15 = (f32[48,128]{1,0:T(8,128)S(1)}, f32[48,128]{1,0:T(8,128)S(1)}, u32[]{:S(2)}, u32[]{:S(2)}) collective-permute-start(f32[48,128]{1,0:T(8,128)S(1)} %add.21), channel_id=1, source_target_pairs={{0,16},{4,20},{8,24},{12,28},{16,0},{20,4},{24,8},{28,12},{1,17},{... | collective-permute-start | bytes 73736 | tf_op jit(solution)/shard_map/ppermute | solution.py:460
  121.5 4.7 %collective-permute-start.16 = (f32[48,128]{1,0:T(8,128)S(1)}, f32[48,128]{1,0:T(8,128)S(1)}, u32[]{:S(2)}, u32[]{:S(2)}) collective-permute-start(f32[48,128]{1,0:T(8,128)S(1)} %add.21), channel_id=1, source_target_pairs={{0,8},{4,12},{8,16},{12,20},{16,24},{20,28},{24,0},{28,4},{1,9},{5... | collective-permute-start | bytes 73736 | tf_op jit(solution)/shard_map/ppermute | solution.py:460
  121.5 5.2 %collective-permute-start.17 = (f32[48,128]{1,0:T(8,128)S(1)}, f32[48,128]{1,0:T(8,128)S(1)}, u32[]{:S(2)}, u32[]{:S(2)}) collective-permute-start(f32[48,128]{1,0:T(8,128)S(1)} %add.21), channel_id=1, source_target_pairs={{0,24},{4,28},{8,0},{12,4},{16,8},{20,12},{24,16},{28,20},{1,25},{... | collective-permute-start | bytes 73736 | tf_op jit(solution)/shard_map/ppermute | solution.py:460
  126.7 4.8 %collective-permute-start.18 = (f32[48,128]{1,0:T(8,128)S(1)}, f32[48,128]{1,0:T(8,128)S(1)}, u32[]{:S(2)}, u32[]{:S(2)}) collective-permute-start(f32[48,128]{1,0:T(8,128)S(1)} %add_add_fusion.1), channel_id=1, source_target_pairs={{0,2},{1,3},{2,0},{3,1},{4,6},{5,7},{6,4},{7,5},{8,10},{9,11},{10,... | collective-permute-start | bytes 73736 | tf_op jit(solution)/shard_map/ppermute | solution.py:460
  127.7 5.6 %collective-permute-start.19 = (f32[48,128]{1,0:T(8,128)S(1)}, f32[48,128]{1,0:T(8,128)S(1)}, u32[]{:S(2)}, u32[]{:S(2)}) collective-permute-start(f32[48,128]{1,0:T(8,128)S(1)} %add_add_fusion.1), channel_id=1, source_target_pairs={{0,1},{1,2},{2,3},{3,0},{4,5},{5,6},{6,7},{7,4},{8,9},{9,10},{10,1... | collective-permute-start | bytes 73736 | tf_op jit(solution)/shard_map/ppermute | solution.py:460
  128.1 5.3 %collective-permute-start.20 = (f32[48,128]{1,0:T(8,128)S(1)}, f32[48,128]{1,0:T(8,128)S(1)}, u32[]{:S(2)}, u32[]{:S(2)}) collective-permute-start(f32[48,128]{1,0:T(8,128)S(1)} %add_add_fusion.1), channel_id=1, source_target_pairs={{0,3},{1,0},{2,1},{3,2},{4,7},{5,4},{6,5},{7,6},{8,11},{9,8},{10,9... | collective-permute-start | bytes 73736 | tf_op jit(solution)/shard_map/ppermute | solution.py:460
  (8 other events, 113.6 us)

commit v3 on v2

--- a/solution.py
+++ b/solution.py
@@ -7,12 +7,14 @@
 from jax.experimental.pallas import tpu as pltpu
 from jax.sharding import PartitionSpec as P
 
+
 RELAX = 1.0 / 9.0
 COARSE_RELAX = 1.0 / 36.0
 SHIFT = 13.0
 DEEP = 4
 POST = 3
 CO = 3
+CP = 2
 PAD = 8
 
 GRANT = 20 << 20
@@ -26,7 +28,7 @@
     return pltpu.VMEM(dims, F32)
 
 
-def call(kernel, outs, scratch, args, name, smem=0):
+def call(kernel, outs, scratch, args, smem=0):
     specs = [SMEM] * smem + [VMEM] * (len(args) - smem)
     return pl.pallas_call(
         kernel,
@@ -35,7 +37,6 @@
         out_specs=[VMEM] * len(outs),
         scratch_shapes=scratch,
         compiler_params=pltpu.CompilerParams(vmem_limit_bytes=GRANT),
-        name=name,
     )(*args)
 
 
@@ -63,8 +64,9 @@
     return lax.broadcasted_iota(jnp.int32, (rows, 128), 1)
 
 
-def pack_kernel(x_ref, p_ref, ylo, yhi, xlo, xhi):
+def pack_kernel(flags, x_ref, p_ref, ylo, yhi, xa, xb):
     cols, nx, ny, _ = x_ref.shape
+    even = flags[4]
 
     def body(f, carry):
         for i in range(nx):
@@ -72,25 +74,25 @@
             yhi[f, pl.ds(i * DEEP, DEEP), :] = x_ref[f, i, pl.ds(ny - DEEP, DEEP), :]
             ylo[f, pl.ds(nx * DEEP + i, 1), :] = p_ref[f, i, pl.ds(0, 1), :]
             yhi[f, pl.ds(nx * DEEP + i, 1), :] = p_ref[f, i, pl.ds(ny - 1, 1), :]
-        for i in range(DEEP):
-            xlo[f, i] = x_ref[f, i]
-            xhi[f, i] = x_ref[f, nx - DEEP + i]
-        xlo[f, DEEP] = p_ref[f, 0]
-        xhi[f, DEEP] = p_ref[f, nx - 1]
+        for out, high in ((xa, even), (xb, 1 - even)):
+            for i in range(DEEP):
+                out[f, i] = x_ref[f, high * (nx - DEEP) + i]
+            out[f, DEEP] = p_ref[f, high * (nx - 1)]
         return carry
 
     lax.fori_loop(0, cols, body, 0)
 
 
-def theta_kernel(x_ref, ylo, yhi, xlo, xhi, out_ref, clo, chi, work, parts):
+def theta_kernel(flags, x_ref, ylo, yhi, xa, xb, out_ref, ca, cb, work, parts):
     cols, nx, ny, _ = x_ref.shape
     lanes = lane_index(ny)
     half = nx // 2 * DEEP
+    even = flags[4]
     parts[pl.ds(2 * cols * 8, 128 * 8 - 2 * cols * 8), :] = jnp.ones((128 * 8 - 2 * cols * 8, 128), F32)
 
     def body(f, carry):
-        work[0, pl.ds(PAD, ny), :] = xlo[f, DEEP - 1]
-        work[nx + 1, pl.ds(PAD, ny), :] = xhi[f, 0]
+        for buf, high in ((xa, even), (xb, 1 - even)):
+            work[high * (nx + 1), pl.ds(PAD, ny), :] = buf[f, (1 - high) * (DEEP - 1)]
         for i in range(nx):
             work[i + 1, pl.ds(PAD, ny), :] = x_ref[f, i]
             work[i + 1, pl.ds(PAD - 1, 1), :] = ylo[f, pl.ds(i * DEEP + DEEP - 1, 1), :]
@@ -107,10 +109,10 @@
             before, center = center, after
         parts[pl.ds(pl.multiple_of(f * 8, 8), 8), :] = numer[0:8] + numer[8:16]
         parts[pl.ds(pl.multiple_of((cols + f) * 8, 8), 8), :] = denom[0:8] + denom[8:16]
-        clo[f, pl.ds(0, half), :] = ylo[f, pl.ds(0, half), :]
-        clo[f, pl.ds(half, half), :] = yhi[f, pl.ds(0, half), :]
-        chi[f, pl.ds(0, half), :] = ylo[f, pl.ds(half, half), :]
-        chi[f, pl.ds(half, half), :] = yhi[f, pl.ds(half, half), :]
+        for out, high in ((ca, even), (cb, 1 - even)):
+            rows = pl.ds(pl.multiple_of(high * half, half), half)
+            out[f, pl.ds(0, half), :] = ylo[f, rows, :]
+            out[f, pl.ds(half, half), :] = yhi[f, rows, :]
         return carry
 
     lax.fori_loop(0, cols, body, 0)
@@ -127,8 +129,8 @@
 
 
 def pre_kernel(
-    flags, sums, x_ref, ylo, yhi, xlo, xhi, clo, chi,
-    r_ref, e_ref, c_ref, slo, shi,
+    flags, sums, x_ref, ylo, yhi, xa, xb, ca, cb,
+    r_ref, e_ref, c_ref, slo, shi, elo, ehi,
     work, other, rhs, small, coarse,
 ):
     cols, nx, ny, _ = x_ref.shape
@@ -148,6 +150,7 @@
             return mask_y * has[1]
         return mask_y
 
+    even = flags[4]
     total = sums[0]
     for k in range(1, sums.shape[0]):
         total = total + sums[k]
@@ -166,10 +169,10 @@
     def body(f, carry):
         th = jnp.sum(jnp.where(spot == f, theta, 0.0)) * 0.125
         for i in range(DEEP):
-            lo, hi = i, nx + DEEP + i
-            work[lo, pl.ds(PAD + DEEP, ny), :] = xlo[f, i]
-            work[hi, pl.ds(PAD + DEEP, ny), :] = xhi[f, i]
-            for plane, buf in ((lo, clo), (hi, chi)):
+            for buf, corner, high in ((xa, ca, even), (xb, cb, 1 - even)):
+                plane = high * (nx + DEEP) + i
+                work[plane, pl.ds(PAD + DEEP, ny), :] = buf[f, i]
+                buf = corner
                 work[plane, pl.ds(PAD, DEEP), :] = buf[f, pl.ds(i * DEEP, DEEP), :]
                 work[plane, pl.ds(PAD + DEEP + ny, DEEP), :] = buf[
                     f, pl.ds(DEEP * DEEP + i * DEEP, DEEP), :
@@ -205,7 +208,10 @@
             after = src[i + 1, own_rows, :]
             near = beside(src, i, PAD + DEEP, ny, center, before, after, own)
             rest = rhs[i, pl.ds(DEEP, ny), :] - 6.0 * center + near
-            e_ref[f, i - DEEP] = center
+            k = i - DEEP
+            e_ref[f, k] = center
+            elo[f, pl.ds(k * POST, POST), :] = e_ref[f, k, pl.ds(0, POST), :]
+            ehi[f, pl.ds(k * POST, POST), :] = e_ref[f, k, pl.ds(ny - POST, POST), :]
             if held is None:
                 held = rest
             else:
@@ -234,30 +240,29 @@
             shi[pl.ds(at, CO), :] = small[pl.ds(cy - CO, CO), :]
 
 
-def coarse_pack_kernel(c_ref, ylo, yhi, xlo, xhi):
+def coarse_pack_kernel(deep, flags, c_ref, ylo, yhi, xa, xb):
     half, cx, cy, _ = c_ref.shape
-    tall = cy + 2 * CO
+    even = flags[4]
+    tall = cy + 2 * deep
     for g in range(half):
-        for out, first in ((xlo, 0), (xhi, cx - CO)):
-            for i in range(CO):
-                at = (g * CO + i) * tall
-                src = (g * cx + first + i) * CO
-                out[pl.ds(at, CO), :] = ylo[pl.ds(src, CO), :]
-                out[pl.ds(at + CO, cy), :] = c_ref[g, first + i]
-                out[pl.ds(at + CO + cy, CO), :] = yhi[pl.ds(src, CO), :]
+        for out, first in ((xa, even * (cx - deep)), (xb, (1 - even) * (cx - deep))):
+            for i in range(deep):
+                at = (g * deep + i) * tall
+                src = (g * cx + first + i) * deep
+                out[pl.ds(at, deep), :] = ylo[pl.ds(src, deep), :]
+                out[pl.ds(at + deep, cy), :] = c_ref[g, first + i]
+                out[pl.ds(at + deep + cy, deep), :] = yhi[pl.ds(src, deep), :]
 
 
 def coarse_kernel(
-    flags, c_ref, ylo, yhi, xlo, xhi, e_ref, corr_ref, slo, shi, work, other, rhs, small
+    flags, c_ref, ylo, yhi, xa, xb, corr_ref, slo, shi, work, other, rhs
 ):
     half, cx, cy, _ = c_ref.shape
-    cols, nx, ny, _ = e_ref.shape
     tall = cy + 2 * CO
     full = 16
     wide = cx + 2 * CO
+    even = flags[4]
     lanes = lane_index(full)
-    spot = lane_index(8)
-    odd = spot % 2 == 1
     has = [flags[k].astype(F32) for k in range(4)]
     row = lax.broadcasted_iota(jnp.int32, (full, 128), 0)
     mask_y = COARSE_RELAX * jnp.where(row < CO, has[2], jnp.where(row >= cy + CO, has[3], 1.0))
@@ -279,8 +284,9 @@
 
     def body(g, carry):
         for i in range(CO):
-            rhs[i, pl.ds(0, tall), :] = xlo[pl.ds((g * CO + i) * tall, tall), :]
-            rhs[cx + CO + i, pl.ds(0, tall), :] = xhi[pl.ds((g * CO + i) * tall, tall), :]
+            for buf, high in ((xa, even), (xb, 1 - even)):
+                plane = high * (cx + CO) + i
+                rhs[plane, pl.ds(0, tall), :] = buf[pl.ds((g * CO + i) * tall, tall), :]
         for i in range(cx):
             at = pl.ds((g * cx + i) * CO, CO)
             rhs[i + CO, pl.ds(0, CO), :] = ylo[at, :]
@@ -299,28 +305,22 @@
                 before, center = center, after
             src, dst = dst, src
         for i in range(cx):
-            both = src[i + CO, pl.ds(PAD + CO, cy), :]
-            first = jnp.where(odd, pltpu.roll(both, 1, 1), both)
-            second = jnp.where(odd, both, pltpu.roll(both, 127, 1))
-            for f, value in ((g, first), (g + half, second)):
-                small[pl.ds(0, cy, stride=2), :] = value
-                small[pl.ds(1, cy, stride=2), :] = value
-                for k in (2 * i, 2 * i + 1):
-                    corr = e_ref[f, k] + small[...]
-                    corr_ref[f, k] = corr
-                    slo[f, pl.ds(k * POST, POST), :] = corr_ref[f, k, pl.ds(0, POST), :]
-                    shi[f, pl.ds(k * POST, POST), :] = corr_ref[f, k, pl.ds(ny - POST, POST), :]
+            corr_ref[g, i] = src[i + CO, pl.ds(PAD + CO, cy), :]
+            at = pl.ds((g * cx + i) * CP, CP)
+            slo[at, :] = src[i + CO, pl.ds(PAD + CO, CP), :]
+            shi[at, :] = src[i + CO, pl.ds(PAD + CO + cy - CP, CP), :]
         return carry
 
     lax.fori_loop(0, half, body, 0)
 
 
-def post_pack_kernel(corr_ref, ylo, yhi, xlo, xhi):
+def post_pack_kernel(flags, corr_ref, ylo, yhi, xa, xb):
     cols, nx, ny, _ = corr_ref.shape
+    even = flags[4]
     tall = ny + 2 * POST
 
     def body(f, carry):
-        for out, first in ((xlo, 0), (xhi, nx - POST)):
+        for out, first in ((xa, even * (nx - POST)), (xb, (1 - even) * (nx - POST))):
             for i in range(POST):
                 at = (f * POST + i) * tall
                 src = pl.ds((first + i) * POST, POST)
@@ -333,13 +333,19 @@
 
 
 def post_kernel(
-    flags, corr_ref, ylo, yhi, xlo, xhi, r_ref, w_ref, image_ref, work, other
+    flags, e_ref, ylo, yhi, xa, xb, c_ref, cylo, cyhi, cxa, cxb, r_ref,
+    w_ref, image_ref, work, other, coarse, small,
 ):
-    cols, nx, ny, _ = corr_ref.shape
+    cols, nx, ny, _ = e_ref.shape
+    half, cx, cy, _ = c_ref.shape
+    ctall = cy + 2 * CP
+    parity = lane_index(16) % 2
+    coarse[:, pl.ds(8, 8), :] = jnp.zeros((cx + 2 * CP, 8, 128), F32)
     tall = ny + 2 * DEEP
     wide = nx + 2 * POST
     span = ny + 2 * POST
     gap = DEEP - POST
+    even = flags[4]
     lanes = lane_index(tall)
     own = lane_index(ny)
     has = [flags[k].astype(F32) for k in range(4)]
@@ -361,15 +367,36 @@
     data = pl.ds(PAD, tall)
 
     def body(f, carry):
+        g = lax.rem(f, half)
+        for i in range(CP):
+            at = pl.ds((g * CP + i) * ctall, ctall)
+            for buf, high in ((cxa, even), (cxb, 1 - even)):
+                coarse[high * (cx + CP) + i, pl.ds(0, ctall), :] = buf[at, :]
+        for i in range(cx):
+            at = pl.ds((g * cx + i) * CP, CP)
+            coarse[i + CP, pl.ds(0, CP), :] = cylo[at, :]
+            coarse[i + CP, pl.ds(CP, cy), :] = c_ref[g, i]
+            coarse[i + CP, pl.ds(CP + cy, CP), :] = cyhi[at, :]
         for i in range(POST):
             at = pl.ds((f * POST + i) * span, span)
-            work[i, pl.ds(PAD + gap, span), :] = xlo[at, :]
-            work[nx + POST + i, pl.ds(PAD + gap, span), :] = xhi[at, :]
+            for buf, high in ((xa, even), (xb, 1 - even)):
+                work[high * (nx + POST) + i, pl.ds(PAD + gap, span), :] = buf[at, :]
         for i in range(nx):
             at = pl.ds(i * POST, POST)
             work[i + POST, pl.ds(PAD + gap, POST), :] = ylo[f, at, :]
-            work[i + POST, pl.ds(PAD + DEEP, ny), :] = corr_ref[f, i]
+            work[i + POST, pl.ds(PAD + DEEP, ny), :] = e_ref[f, i]
             work[i + POST, pl.ds(PAD + DEEP + ny, POST), :] = yhi[f, at, :]
+        upper = jnp.where(f >= half, 1, 0)
+        for m in range(cx + 2 * CP):
+            both = coarse[m]
+            moved = jnp.where(parity == 1, pltpu.roll(both, 1, 1), pltpu.roll(both, 127, 1))
+            value = jnp.where(parity == upper, both, moved)
+            small[m % 2, pl.ds(0, 16, stride=2), :] = value
+            small[m % 2, pl.ds(1, 16, stride=2), :] = value
+            up = small[m % 2, pl.ds(0, tall), :]
+            for i in (2 * m - 1, 2 * m):
+                if 0 <= i < wide:
+                    work[i, data, :] = work[i, data, :] + up
         src, dst = work, other
         for depth in (1, 2):
             before = src[depth - 1, data, :]
@@ -394,17 +421,19 @@
     lax.fori_loop(0, cols, body, 0)
 
 
-def image_kernel(x_ref, p_ref, ylo, yhi, xlo, xhi, ax_ref, ap_ref, work):
+def image_kernel(flags, x_ref, p_ref, ylo, yhi, xa, xb, ax_ref, ap_ref, work):
     cols, nx, ny, _ = x_ref.shape
+    even = flags[4]
     lanes = lane_index(ny)
 
     def body(f, carry):
-        for ref, out, lo, hi, base, deep in (
-            (x_ref, ax_ref, DEEP - 1, 0, 0, DEEP),
-            (p_ref, ap_ref, DEEP, DEEP, nx * DEEP, 1),
+        for ref, out, first, base, deep in (
+            (x_ref, ax_ref, 0, 0, DEEP),
+            (p_ref, ap_ref, DEEP, nx * DEEP, 1),
         ):
-            work[0, pl.ds(PAD, ny), :] = xlo[f, lo]
-            work[nx + 1, pl.ds(PAD, ny), :] = xhi[f, hi]
+            for buf, high in ((xa, even), (xb, 1 - even)):
+                plane = first + (1 - high) * (deep - 1)
+                work[high * (nx + 1), pl.ds(PAD, ny), :] = buf[f, plane]
             for i in range(nx):
                 work[i + 1, pl.ds(PAD, ny), :] = ref[f, i]
                 work[i + 1, pl.ds(PAD - 1, 1), :] = ylo[f, pl.ds(base + i * deep + deep - 1, 1), :]
@@ -429,6 +458,15 @@
 def from_high(value, axis):
     count = lax.axis_size(axis)
     return lax.ppermute(value, axis, [(i + 1, i) for i in range(count - 1)])
+
+
+def swap(one, two, axis):
+    count = lax.axis_size(axis)
+    pairs = [[], []]
+    for i in range(count - 1):
+        pairs[i % 2] += [(i, i + 1), (i + 1, i)]
+    two = lax.ppermute(two, axis, pairs[1])
+    return lax.ppermute(one, axis, pairs[0]), two
 
 
 def radices(count):
@@ -548,17 +586,13 @@
         terms += [high, (part - high.astype(F32)).astype(BF16)]
     terms = jnp.concatenate(terms, axis=0)
 
-    def copies(c, slot):
+    def copies(c):
         return [
-            pltpu.make_async_copy(bufs.at[slot, k], ref.at[:, c], sems.at[slot, k])
+            pltpu.make_async_copy(bufs.at[c, k], ref.at[:, c], sems.at[c, k])
             for k, ref in enumerate((block_ref, search_ref))
         ]
 
     for c in range(chunks):
-        slot = c % 2
-        if c >= 2:
-            for copy in copies(c - 2, slot):
-                copy.wait()
         for y in range(0, ny, 2):
             got = jnp.dot(
                 terms, s_ref[c, :, pl.ds(y * 128, 256)], preferred_element_type=F32
@@ -567,19 +601,20 @@
             block = search + (got[:cols] + got[cols : 2 * cols])
             for k, value in enumerate((block, search)):
                 for j in range(2):
-                    bufs[slot, k, :, y + j, :] = value[:, j * 128 : (j + 1) * 128]
-        for copy in copies(c, slot):
+                    flat = bufs.at[c, k].reshape(cols * ny, 128)
+                    flat[pl.ds(y + j, cols, stride=ny), :] = value[:, j * 128 : (j + 1) * 128]
+        for copy in copies(c):
             copy.start()
-    for c in range(max(chunks - 2, 0), chunks):
-        for copy in copies(c, c % 2):
+    for c in range(chunks):
+        for copy in copies(c):
             copy.wait()
 
 
-def body(x, p):
+def step(x, p):
     cols, nx, ny, nz = x.shape
     ngx, ngy = lax.axis_size("gx"), lax.axis_size("gy")
     ix, iy = lax.axis_index("gx"), lax.axis_index("gy")
-    flags = jnp.stack([ix > 0, ix < ngx - 1, iy > 0, iy < ngy - 1]).astype(jnp.int32)
+    flags = jnp.stack([ix > 0, ix < ngx - 1, iy > 0, iy < ngy - 1, ix % 2 == 0]).astype(jnp.int32)
     half, cx, cy = cols // 2, nx // 2, ny // 2
     work = pltpu.VMEM
 
@@ -587,61 +622,69 @@
     to_ylo, to_yhi, to_xlo, to_xhi = call(
         pack_kernel,
         [shape(cols, yrows, nz)] * 2 + [shape(cols, DEEP + 1, ny, nz)] * 2,
-        [], (x, p), "pack",
+        [], (flags, x, p), smem=1,
     )
     ylo, yhi = from_low(to_yhi, "gy"), from_high(to_ylo, "gy")
-    xlo, xhi = from_low(to_xhi, "gx"), from_high(to_xlo, "gx")
+    xlo, xhi = swap(to_xlo, to_xhi, "gx")
 
     devices = ngx * ngy
     sums, to_clo, to_chi = call(
         theta_kernel,
         [shape(devices, 8, 128)] + [shape(cols, nx * DEEP, nz)] * 2,
         [work((nx + 2, PAD + ny + 8, nz), F32), work((128 * 8, nz), F32)],
-        (x, ylo, yhi, xlo, xhi), "theta",
-    )
-    clo, chi = from_low(to_chi, "gx"), from_high(to_clo, "gx")
+        (flags, x, ylo, yhi, xlo, xhi), smem=1,
+    )
+    clo, chi = swap(to_clo, to_chi, "gx")
     sums = lax.all_to_all(sums, ("gx", "gy"), 0, 0)
 
     tall, wide = ny + 2 * DEEP, nx + 2 * DEEP
     plane = PAD + tall + 8
-    r, e, c, to_ylo, to_yhi = call(
+    r, e, c, to_ylo, to_yhi, to_eylo, to_eyhi = call(
         pre_kernel,
         [shape(cols, wide - 4, tall, nz), shape(cols, nx, ny, nz), shape(half, cx, cy, nz)]
-        + [shape(half * cx * CO, nz)] * 2,
+        + [shape(half * cx * CO, nz)] * 2
+        + [shape(cols, nx * POST, nz)] * 2,
         [work((wide, plane, nz), F32)] * 2
         + [work((wide, tall, nz), F32), work((ny, nz), F32), work((cols, cx, cy, nz), F32)],
-        (flags, sums, x, ylo, yhi, xlo, xhi, clo, chi), "pre", smem=1,
+        (flags, sums, x, ylo, yhi, xlo, xhi, clo, chi), smem=1,
     )
 
     cylo, cyhi = from_low(to_yhi, "gy"), from_high(to_ylo, "gy")
+    eylo, eyhi = from_low(to_eyhi, "gy"), from_high(to_eylo, "gy")
     to_xlo, to_xhi = call(
-        coarse_pack_kernel, [shape(half * CO * (cy + 2 * CO), nz)] * 2, [], (c, cylo, cyhi), "cpack"
-    )
-    cxlo, cxhi = from_low(to_xhi, "gx"), from_high(to_xlo, "gx")
+        functools.partial(coarse_pack_kernel, CO),
+        [shape(half * CO * (cy + 2 * CO), nz)] * 2, [], (flags, c, cylo, cyhi), smem=1,
+    )
+    cxlo, cxhi = swap(to_xlo, to_xhi, "gx")
+    to_exlo, to_exhi = call(
+        post_pack_kernel, [shape(cols * POST * (ny + 2 * POST), nz)] * 2, [],
+        (flags, e, eylo, eyhi), smem=1,
+    )
+    exlo, exhi = swap(to_exlo, to_exhi, "gx")
     cwide = cx + 2 * CO
-    corr, to_ylo, to_yhi = call(
+    d, to_ylo, to_yhi = call(
         coarse_kernel,
-        [shape(cols, nx, ny, nz)] + [shape(cols, nx * POST, nz)] * 2,
-        [work((cwide, PAD + 16 + 8, nz), F32)] * 2
-        + [work((cwide, 16, nz), F32), work((ny, nz), F32)],
-        (flags, c, cylo, cyhi, cxlo, cxhi, e), "coarse", smem=1,
-    )
-
-    eylo, eyhi = from_low(to_yhi, "gy"), from_high(to_ylo, "gy")
+        [shape(half, cx, cy, nz)] + [shape(half * cx * CP, nz)] * 2,
+        [work((cwide, PAD + 16 + 8, nz), F32)] * 2 + [work((cwide, 16, nz), F32)],
+        (flags, c, cylo, cyhi, cxlo, cxhi), smem=1,
+    )
+    dylo, dyhi = from_low(to_yhi, "gy"), from_high(to_ylo, "gy")
     to_xlo, to_xhi = call(
-        post_pack_kernel, [shape(cols * POST * (ny + 2 * POST), nz)] * 2, [], (corr, eylo, eyhi), "ppack"
-    )
-    exlo, exhi = from_low(to_xhi, "gx"), from_high(to_xlo, "gx")
+        functools.partial(coarse_pack_kernel, CP),
+        [shape(half * CP * (cy + 2 * CP), nz)] * 2, [], (flags, d, dylo, dyhi), smem=1,
+    )
+    dxlo, dxhi = swap(to_xlo, to_xhi, "gx")
 
     image_x, image_p = call(
         image_kernel, [shape(cols, nx, ny, nz)] * 2,
         [work((nx + 2, PAD + ny + 8, nz), F32)],
-        (x, p, ylo, yhi, xlo, xhi), "image",
+        (flags, x, p, ylo, yhi, xlo, xhi), smem=1,
     )
     w, image_w = call(
         post_kernel, [shape(cols, nx, ny, nz)] * 2,
-        [work((nx + 2 * POST, plane, nz), F32)] * 2,
-        (flags, corr, eylo, eyhi, exlo, exhi, r), "post", smem=1,
+        [work((nx + 2 * POST, plane, nz), F32)] * 2
+        + [work((cx + 2 * CP, 16, nz), F32), work((2, 32, nz), F32)],
+        (flags, e, eylo, eyhi, exlo, exhi, d, dylo, dyhi, dxlo, dxhi, r), smem=1,
     )
 
     flat = [v.reshape(cols * nx * ny, nz) for v in (x, w, p, image_x, image_w, image_p)]
@@ -650,7 +693,7 @@
         gram_kernel,
         [shape(nb, 128), pltpu.VMEM((nx, 2 * nb, ny * nz), BF16)],
         [work((2 * nb, ny * nz), BF16)],
-        flat, "gram",
+        flat,
     )
     part = sum_all(part)
     any_space = pl.BlockSpec(memory_space=pl.ANY)
@@ -660,8 +703,8 @@
         in_specs=[VMEM, VMEM],
         out_specs=[any_space] * 2,
         scratch_shapes=[
-            work((2, 2, cols, ny, nz), F32),
-            pltpu.SemaphoreType.DMA((2, 2)),
+            work((nx, 2, cols, ny, nz), F32),
+            pltpu.SemaphoreType.DMA((nx, 2)),
         ],
         compiler_params=pltpu.CompilerParams(vmem_limit_bytes=GRANT),
         name="finish",
@@ -672,5 +715,5 @@
 def solution(mesh):
     spec = P(None, "gx", "gy", None)
     return jax.shard_map(
-        body, mesh=mesh, in_specs=(spec, spec), out_specs=(spec, spec), check_vma=False
-    )
+        step, mesh=mesh, in_specs=(spec, spec), out_specs=(spec, spec), check_vma=False
+    )

time: 144 us -> 141 us (0.979)
  blocking collectives: 0 us -> 17.6 us
  starting transfers between devices: 57.1 us -> 45.1 us
  waiting for transfers between devices: 38.9 us -> 31.5 us
  local copies, waits for them, and re-layouts: 4.4 us -> 2.57 us
    all_to_all x0 -> x1, blocking collectives: none -> 17.6 us  [step(): sums = lax.all_to_all(sums, ('gx', 'gy'), 0, 0)]
    ppermute x0 -> x10, starting transfers between devices: none -> 13.5 us  [the longest x5 10.1 us: swap(): return (lax.ppermute(one, axis, pairs[0]), two)]
    ppermute x7 -> x4, starting transfers between devices: 21.6 us -> 11.5 us  [from_low(): return lax.ppermute(value, axis, [(i, i + 1) for i in range(count - 1)])]
    all_to_all x1 -> x0, waiting for transfers between devices: 8.28 us -> none  [body(): sums = lax.all_to_all(sums, ('gx', 'gy'), 0, 0)]
    all_to_all x1 -> x0, starting transfers between devices: 6.97 us -> none  [body(): sums = lax.all_to_all(sums, ('gx', 'gy'), 0, 0)]
    ppermute x7, starting transfers between devices: 19.5 us -> 14.9 us  [sum_all(): parts.append(lax.ppermute(value, axis, pairs))]
    ppermute x7 -> x4, starting transfers between devices: 9.03 us -> 5.17 us  [from_high(): return lax.ppermute(value, axis, [(i + 1, i) for i in range(count - 1)])]
    pallas_call x9 -> x10, Pallas kernels: 32 us -> 34.8 us  [call(): pl.pallas_call(kernel, out_shape=outs, in_specs=specs, out_specs=[VMEM] *...]
  transfers between devices with their start and end apart: 22 -> 25, of which waited for: 14 -> 13; matrix products, arithmetic and copies ran while one was open for 0% -> 0% of each run, Pallas kernels for 2% -> 5%
where the time goes in v3:
time: 141 us; the launch traced here: 140 us
  starting transfers between devices  45.1 us (32%)
  Pallas kernels  42.6 us (30%)
  waiting for transfers between devices  31.5 us (22%)
  blocking collectives  17.6 us (12%)
  local copies, waits for them, and re-layouts  2.57 us (2%)
    pallas_call x10, Pallas kernels, call(): pl.pallas_call(kernel, out_shape=outs, in_specs=specs, out_specs=[VMEM] *...  34.8 us
    all_to_all x1, blocking collectives, step(): sums = lax.all_to_all(sums, ('gx', 'gy'), 0, 0)  17.6 us
    ppermute x4, waiting for transfers between devices, from_high(): return lax.ppermute(value, axis, [(i + 1, i) for i in range(count - 1)])  17.3 us
    ppermute x7, starting transfers between devices, sum_all(): parts.append(lax.ppermute(value, axis, pairs))  14.9 us
    ppermute x4, starting transfers between devices, from_low(): return lax.ppermute(value, axis, [(i, i + 1) for i in range(count - 1)])  11.5 us
    ppermute x5, starting transfers between devices, swap(): return (lax.ppermute(one, axis, pairs[0]), two)  10.1 us
    ppermute x4, waiting for transfers between devices, from_low(): return lax.ppermute(value, axis, [(i, i + 1) for i in range(count - 1)])  9.37 us
    pallas_call x1, Pallas kernels, step(): pl.pallas_call(functools.partial(finish_kernel, nx * ny * nz * devices),...  7.82 us
  transfers between devices with their start and end apart: 25, of which 13 were waited for; matrix products, arithmetic and copies ran while one was open for 0% of the time, Pallas kernels for 5%

profile of v3, /device:TPU:0, one launch (start us, length us, event | category | flops | bytes accessed | tf_op | source)
XLA Modules:
  0.0 140.2 jit_solution(5692304622259336972)
XLA Ops:
  5.3 4.5 %collective-permute-start = (f32[16,40,128]{2,1,0:T(8,128)S(1)}, f32[16,40,128]{2,1,0:T(8,128)S(1)}, u32[]{:S(2)}, u32[]{:S(2)}) collective-permute-start(f32[16,40,128]{2,1,0:T(8,128)S(1)} %get-tuple-element.31), channel_id=1, source_target_pairs={{0,1},{1,2},{2,3},{4,5},{5,6},{6,7},{8,9},{9,10},{10,11},{12,13},{... | collective-permute-start | bytes 983048 | tf_op jit(solution)/shard_map/ppermute | solution.py:455
  11.1 4.9 %collective-permute-done.ylo = f32[16,40,128]{2,1,0:T(8,128)S(1)} collective-permute-done((f32[16,40,128]{2,1,0:T(8,128)S(1)}, f32[16,40,128]{2,1,0:T(8,128)S(1)}, u32[]{:S(2)}, u32[]{:S(2)}) %collective-permute-start) | collective-permute-done | bytes 327712 | tf_op jit(solution)/shard_map/ppermute | solution.py:455
  16.1 4.7 %collective-permute-done.1.yhi = f32[16,40,128]{2,1,0:T(8,128)S(1)} collective-permute-done((f32[16,40,128]{2,1,0:T(8,128)S(1)}, f32[16,40,128]{2,1,0:T(8,128)S(1)}, u32[]{:S(2)}, u32[]{:S(2)}) %collective-permute-start.1) | collective-permute-done | bytes 327712 | tf_op jit(solution)/shard_map/ppermute | solution.py:460
  20.8 2.8 %shard_map.42 = (f32[32,8,128]{2,1,0:T(8,128)S(1)}, f32[16,32,128]{2,1,0:T(8,128)S(1)}, f32[16,32,128]{2,1,0:T(8,128)S(1)}) custom-call(s32[5]{0:T(128)S(1)} %convert_element_type.3.flags, f32[16,8,16,128]{3,2,1,0:T(8,128)S(1)} %copy-done, f32[16,40,128]{2,1,0:T(8,128)S(1)} %collective-permute-done.ylo, f32[16,40,128]{2,1,0:T(8,128)S(1)} %collective-permute-done.1.yhi, ...), custom_call_target="tpu_custom_call" | custom-call | tf_op jit(solution)/shard_map/pallas_call | solution.py:33
  23.5 2.8 %collective-permute-start.4 = (f32[16,32,128]{2,1,0:T(8,128)S(1)}, f32[16,32,128]{2,1,0:T(8,128)S(1)}, u32[]{:S(2)}, u32[]{:S(2)}) collective-permute-start(f32[16,32,128]{2,1,0:T(8,128)S(1)} %get-tuple-element.36), channel_id=1, source_target_pairs={{0,4},{4,0},{8,12},{12,8},{16,20},{20,16},{24,28},{28,24},{1,5},{5... | collective-permute-start | bytes 786440 | tf_op jit(solution)/shard_map/ppermute | solution.py:469
  27.0 17.6 %all_to_all.5.sums = f32[32,8,128]{2,1,0:T(8,128)S(1)} all-to-all(f32[32,8,128]{2,1,0:T(8,128)S(1)} %get-tuple-element.35), channel_id=1, replica_groups=mesh['gx'=8,'gy'=4] {'gx','gy'}, dimensions={0} | all-to-all | bytes 262144 | tf_op jit(solution)/shard_map/all_to_all | solution.py:638
  44.6 9.2 %shard_map.43 = (f32[16,12,24,128]{3,2,1,0:T(8,128)S(1)}, f32[16,8,16,128]{3,2,1,0:T(8,128)S(1)}, f32[8,4,8,128]{3,2,1,0:T(8,128)S(1)}, f32[96,128]{1,0:T(8,128)...) custom-call(s32[5]{0:T(128)S(1)} %convert_element_type.3.flags, ...), custom_call_target="tpu_custom_call" | custom-call | tf_op jit(solution)/shard_map/pallas_call | solution.py:33
  56.5 3.7 %collective-permute-done.6.ylo = f32[16,24,128]{2,1,0:T(8,128)S(1)} collective-permute-done((f32[16,24,128]{2,1,0:T(8,128)S(1)}, f32[16,24,128]{2,1,0:T(8,128)S(1)}, u32[]{:S(2)}, u32[]{:S(2)}) %collective-permute-start.6) | collective-permute-done | bytes 196640 | tf_op jit(solution)/shard_map/ppermute | solution.py:455
  60.3 4.1 %collective-permute-done.7.yhi = f32[16,24,128]{2,1,0:T(8,128)S(1)} collective-permute-done((f32[16,24,128]{2,1,0:T(8,128)S(1)}, f32[16,24,128]{2,1,0:T(8,128)S(1)}, u32[]{:S(2)}, u32[]{:S(2)}) %collective-permute-start.7) | collective-permute-done | bytes 196640 | tf_op jit(solution)/shard_map/ppermute | solution.py:460
  65.9 2.6 %collective-permute-start.10 = (f32[96,128]{1,0:T(8,128)S(1)}, f32[96,128]{1,0:T(8,128)S(1)}, u32[]{:S(2)}, u32[]{:S(2)}) collective-permute-start(f32[96,128]{1,0:T(8,128)S(1)} %get-tuple-element.44), channel_id=1, source_target_pairs={{0,1},{1,2},{2,3},{4,5},{5,6},{6,7},{8,9},{9,10},{10,11},{12,13},{... | collective-permute-start | bytes 147464 | tf_op jit(solution)/shard_map/ppermute | solution.py:455
  70.3 4.3 %collective-permute-done.11.yhi = f32[96,128]{1,0:T(8,128)S(1)} collective-permute-done((f32[96,128]{1,0:T(8,128)S(1)}, f32[96,128]{1,0:T(8,128)S(1)}, u32[]{:S(2)}, u32[]{:S(2)}) %collective-permute-start.11) | collective-permute-done | bytes 49184 | tf_op jit(solution)/shard_map/ppermute | solution.py:460
  76.9 2.7 %shard_map.46 = (f32[8,4,8,128]{3,2,1,0:T(8,128)S(1)}, f32[64,128]{1,0:T(8,128)S(1)}, f32[64,128]{1,0:T(8,128)S(1)}) custom-call(s32[5]{0:T(128)S(1)} %convert_element_type.3.flags, f32[8,4,8,128]{3,2,1,0:T(8,128)S(1)} %get-tuple-element.43.c_ref, f32[96,128]{1,0:T(8,128)S(1)} %collective-permute-done.10.ylo, f32[96,128]{1,0:T(8,128)S(1)} %collective-permute-done.11.yhi, ...), custom_call_target="tpu_custom_call" | custom-call | tf_op jit(solution)/shard_map/pallas_call | solution.py:33
  79.6 2.9 %collective-permute-start.14 = (f32[64,128]{1,0:T(8,128)S(1)}, f32[64,128]{1,0:T(8,128)S(1)}, u32[]{:S(2)}, u32[]{:S(2)}) collective-permute-start(f32[64,128]{1,0:T(8,128)S(1)} %get-tuple-element.49), channel_id=1, source_target_pairs={{0,1},{1,2},{2,3},{4,5},{5,6},{6,7},{8,9},{9,10},{10,11},{12,13},{... | collective-permute-start | bytes 98312 | tf_op jit(solution)/shard_map/ppermute | solution.py:455
  84.1 4.2 %collective-permute-done.15.yhi.cyhi = f32[64,128]{1,0:T(8,128)S(1)} collective-permute-done((f32[64,128]{1,0:T(8,128)S(1)}, f32[64,128]{1,0:T(8,128)S(1)}, u32[]{:S(2)}, u32[]{:S(2)}) %collective-permute-start.15) | collective-permute-done | bytes 32800 | tf_op jit(solution)/shard_map/ppermute | solution.py:460
  88.9 6.0 %collective-permute-start.16 = (f32[192,128]{1,0:T(8,128)S(1)}, f32[192,128]{1,0:T(8,128)S(1)}, u32[]{:S(2)}, u32[]{:S(2)}) collective-permute-start(f32[192,128]{1,0:T(8,128)S(1)} %get-tuple-element.51), channel_id=1, source_target_pairs={{0,4},{4,0},{8,12},{12,8},{16,20},{20,16},{24,28},{28,24},{1,5},{5... | collective-permute-start | bytes 294920 | tf_op jit(solution)/shard_map/ppermute | solution.py:469
  95.6 2.9 %shard_map.49 = (f32[16,8,16,128]{3,2,1,0:T(8,128)S(1)}, f32[16,8,16,128]{3,2,1,0:T(8,128)S(1)}) custom-call(s32[5]{0:T(128)S(1)} %convert_element_type.3.flags, f32[16,8,16,128]{3,2,1,0:T(8,128)S(1)} %copy-done.1, f32[16,8,16,128]{3,2,1,0:T(8,128)S(1)} %copy-done.3, f32[16,40,128]{2,1,0:T(8,128)S(1)} %collective-permute-done.ylo, ...), custom_call_target="tpu_custom_call" | custom-call | tf_op jit(solution)/shard_map/pallas_call | solution.py:33
  98.6 7.2 %shard_map.48 = (f32[16,8,16,128]{3,2,1,0:T(8,128)S(1)}, f32[16,8,16,128]{3,2,1,0:T(8,128)S(1)}) custom-call(s32[5]{0:T(128)S(1)} %convert_element_type.3.flags, f32[16,8,16,128]{3,2,1,0:T(8,128)S(1)} %get-tuple-element.38.corr_ref.e_ref, f32[16,24,128]{2,1,0:T(8,128)S(1)} %collective-permute-done.6.ylo, f32[16,24,128]{2,1,0:T(8,128)S(1)} %collective-permute-done.7.yhi, ...), custom_call_target="tpu_custom_call" | custom-call | tf_op jit(solution)/shard_map/pallas_call | solution.py:33
  105.8 7.2 %shard_map.50 = (f32[48,128]{1,0:T(8,128)S(1)}, bf16[8,96,2048]{2,1,0:T(8,128)(2,1)S(1)}) custom-call(f32[2048,128]{1,0:T(8,128)S(1)} %bitcast.11, f32[2048,128]{1,0:T(8,128)S(1)} %bitcast.15, f32[2048,128]{1,0:T(8,128)S(1)} %bitcast.12, f32[2048,128]{1,0:T(8,128)S(1)} %bitcast.13, f32[2048,128]{1,0:T(8,128)S(1)} %bitcast.16, f32[2048,128]{1,0:T(8,128)S(1)} %bitcast.14), custom_call_target="tpu_custom_call" | custom-call | tf_op jit(solution)/shard_map/pallas_call | solution.py:33
  113.0 4.4 %collective-permute-start.18 = (f32[48,128]{1,0:T(8,128)S(1)}, f32[48,128]{1,0:T(8,128)S(1)}, u32[]{:S(2)}, u32[]{:S(2)}) collective-permute-start(f32[48,128]{1,0:T(8,128)S(1)} %get-tuple-element.58), channel_id=1, source_target_pairs={{0,4},{4,0},{8,12},{12,8},{16,20},{20,16},{24,28},{28,24},{1,5},{5... | collective-permute-start | bytes 73736 | tf_op jit(solution)/shard_map/ppermute | solution.py:498
  118.3 3.2 %collective-permute-start.19 = (f32[48,128]{1,0:T(8,128)S(1)}, f32[48,128]{1,0:T(8,128)S(1)}, u32[]{:S(2)}, u32[]{:S(2)}) collective-permute-start(f32[48,128]{1,0:T(8,128)S(1)} %add.26), channel_id=1, source_target_pairs={{0,16},{4,20},{8,24},{12,28},{16,0},{20,4},{24,8},{28,12},{1,17},{... | collective-permute-start | bytes 73736 | tf_op jit(solution)/shard_map/ppermute | solution.py:498
  121.7 2.7 %collective-permute-start.21 = (f32[48,128]{1,0:T(8,128)S(1)}, f32[48,128]{1,0:T(8,128)S(1)}, u32[]{:S(2)}, u32[]{:S(2)}) collective-permute-start(f32[48,128]{1,0:T(8,128)S(1)} %add.26), channel_id=1, source_target_pairs={{0,24},{4,28},{8,0},{12,4},{16,8},{20,12},{24,16},{28,20},{1,25},{... | collective-permute-start | bytes 73736 | tf_op jit(solution)/shard_map/ppermute | solution.py:498
  124.4 1.8 %collective-permute-done.20 = f32[48,128]{1,0:T(8,128)S(1)} collective-permute-done((f32[48,128]{1,0:T(8,128)S(1)}, f32[48,128]{1,0:T(8,128)S(1)}, u32[]{:S(2)}, u32[]{:S(2)}) %collective-permute-start.20) | collective-permute-done | bytes 24608 | tf_op jit(solution)/shard_map/ppermute | solution.py:498
  127.4 3.2 %collective-permute-start.24 = (f32[48,128]{1,0:T(8,128)S(1)}, f32[48,128]{1,0:T(8,128)S(1)}, u32[]{:S(2)}, u32[]{:S(2)}) collective-permute-start(f32[48,128]{1,0:T(8,128)S(1)} %add_add_fusion.1), channel_id=1, source_target_pairs={{0,3},{1,0},{2,1},{3,2},{4,7},{5,4},{6,5},{7,6},{8,11},{9,8},{10,9... | collective-permute-start | bytes 73736 | tf_op jit(solution)/shard_map/ppermute | solution.py:498
  132.4 7.8 %finish.1 = (f32[16,8,16,128]{3,2,1,0:T(8,128)}, f32[16,8,16,128]{3,2,1,0:T(8,128)}) custom-call(f32[48,128]{1,0:T(8,128)S(1)} %add_add_fusion.sums_ref, bf16[8,96,2048]{2,1,0:T(8,128)(2,1)S(1)} %get-tuple-element.59.s_ref), custom_call_target="tpu_custom_call" | custom-call | tf_op jit(solution)/shard_map/finish/pallas_call | solution.py:700
  (51 shorter events, 21.9 us)
Async XLA Ops:
  4.1 16.7 %collective-permute-start.2 = (f32[16,5,16,128]{3,2,1,0:T(8,128)S(1)}, f32[16,5,16,128]{3,2,1,0:T(8,128)S(1)}, u32[]{:S(2)}, u32[]{:S(2)}) collective-permute-start(f32[16,5,16,128]{3,2,1,0:T(8,128)S(1)} %get-tuple-element.33), channel_id=1, source_target_pairs={{0,4},{4,0},{8,12},{12,8},{16,20},{20,16},{24,28},{28,24},{1,5},{5... | collective-permute-start | bytes 1966088 | tf_op jit(solution)/shard_map/ppermute | solution.py:469
  4.6 16.1 %collective-permute-start.3 = (f32[16,5,16,128]{3,2,1,0:T(8,128)S(1)}, f32[16,5,16,128]{3,2,1,0:T(8,128)S(1)}, u32[]{:S(2)}, u32[]{:S(2)}) collective-permute-start(f32[16,5,16,128]{3,2,1,0:T(8,128)S(1)} %get-tuple-element.34), channel_id=1, source_target_pairs={{4,8},{8,4},{12,16},{16,12},{20,24},{24,20},{5,9},{9,5},{13,17},{1... | collective-permute-start | bytes 1966088 | tf_op jit(solution)/shard_map/ppermute | solution.py:468
  5.3 10.7 %collective-permute-start = (f32[16,40,128]{2,1,0:T(8,128)S(1)}, f32[16,40,128]{2,1,0:T(8,128)S(1)}, u32[]{:S(2)}, u32[]{:S(2)}) collective-permute-start(f32[16,40,128]{2,1,0:T(8,128)S(1)} %get-tuple-element.31), channel_id=1, source_target_pairs={{0,1},{1,2},{2,3},{4,5},{5,6},{6,7},{8,9},{9,10},{10,11},{12,13},{... | collective-permute-start | bytes 983048 | tf_op jit(solution)/shard_map/ppermute | solution.py:455
  9.8 10.9 %collective-permute-start.1 = (f32[16,40,128]{2,1,0:T(8,128)S(1)}, f32[16,40,128]{2,1,0:T(8,128)S(1)}, u32[]{:S(2)}, u32[]{:S(2)}) collective-permute-start(f32[16,40,128]{2,1,0:T(8,128)S(1)} %get-tuple-element.32), channel_id=1, source_target_pairs={{1,0},{2,1},{3,2},{5,4},{6,5},{7,6},{9,8},{10,9},{11,10},{13,12},{... | collective-permute-start | bytes 983048 | tf_op jit(solution)/shard_map/ppermute | solution.py:460
  23.5 21.1 %collective-permute-start.4 = (f32[16,32,128]{2,1,0:T(8,128)S(1)}, f32[16,32,128]{2,1,0:T(8,128)S(1)}, u32[]{:S(2)}, u32[]{:S(2)}) collective-permute-start(f32[16,32,128]{2,1,0:T(8,128)S(1)} %get-tuple-element.36), channel_id=1, source_target_pairs={{0,4},{4,0},{8,12},{12,8},{16,20},{20,16},{24,28},{28,24},{1,5},{5... | collective-permute-start | bytes 786440 | tf_op jit(solution)/shard_map/ppermute | solution.py:469
  26.3 18.3 %collective-permute-start.5 = (f32[16,32,128]{2,1,0:T(8,128)S(1)}, f32[16,32,128]{2,1,0:T(8,128)S(1)}, u32[]{:S(2)}, u32[]{:S(2)}) collective-permute-start(f32[16,32,128]{2,1,0:T(8,128)S(1)} %get-tuple-element.37), channel_id=1, source_target_pairs={{4,8},{8,4},{12,16},{16,12},{20,24},{24,20},{5,9},{9,5},{13,17},{1... | collective-permute-start | bytes 786440 | tf_op jit(solution)/shard_map/ppermute | solution.py:468
  53.8 6.5 %collective-permute-start.6 = (f32[16,24,128]{2,1,0:T(8,128)S(1)}, f32[16,24,128]{2,1,0:T(8,128)S(1)}, u32[]{:S(2)}, u32[]{:S(2)}) collective-permute-start(f32[16,24,128]{2,1,0:T(8,128)S(1)} %get-tuple-element.39), channel_id=1, source_target_pairs={{0,1},{1,2},{2,3},{4,5},{5,6},{6,7},{8,9},{9,10},{10,11},{12,13},{... | collective-permute-start | bytes 589832 | tf_op jit(solution)/shard_map/ppermute | solution.py:455
  55.2 9.2 %collective-permute-start.7 = (f32[16,24,128]{2,1,0:T(8,128)S(1)}, f32[16,24,128]{2,1,0:T(8,128)S(1)}, u32[]{:S(2)}, u32[]{:S(2)}) collective-permute-start(f32[16,24,128]{2,1,0:T(8,128)S(1)} %get-tuple-element.40), channel_id=1, source_target_pairs={{1,0},{2,1},{3,2},{5,4},{6,5},{7,6},{9,8},{10,9},{11,10},{13,12},{... | collective-permute-start | bytes 589832 | tf_op jit(solution)/shard_map/ppermute | solution.py:460
  65.2 33.4 %collective-permute-start.8 = (f32[1056,128]{1,0:T(8,128)S(1)}, f32[1056,128]{1,0:T(8,128)S(1)}, u32[]{:S(2)}, u32[]{:S(2)}) collective-permute-start(f32[1056,128]{1,0:T(8,128)S(1)} %get-tuple-element.41), channel_id=1, source_target_pairs={{0,4},{4,0},{8,12},{12,8},{16,20},{20,16},{24,28},{28,24},{1,5},{5... | collective-permute-start | bytes 1622024 | tf_op jit(solution)/shard_map/ppermute | solution.py:469
  65.2 33.3 %collective-permute-start.9 = (f32[1056,128]{1,0:T(8,128)S(1)}, f32[1056,128]{1,0:T(8,128)S(1)}, u32[]{:S(2)}, u32[]{:S(2)}) collective-permute-start(f32[1056,128]{1,0:T(8,128)S(1)} %get-tuple-element.42), channel_id=1, source_target_pairs={{4,8},{8,4},{12,16},{16,12},{20,24},{24,20},{5,9},{9,5},{13,17},{1... | collective-permute-start | bytes 1622024 | tf_op jit(solution)/shard_map/ppermute | solution.py:468
  65.9 4.4 %collective-permute-start.10 = (f32[96,128]{1,0:T(8,128)S(1)}, f32[96,128]{1,0:T(8,128)S(1)}, u32[]{:S(2)}, u32[]{:S(2)}) collective-permute-start(f32[96,128]{1,0:T(8,128)S(1)} %get-tuple-element.44), channel_id=1, source_target_pairs={{0,1},{1,2},{2,3},{4,5},{5,6},{6,7},{8,9},{9,10},{10,11},{12,13},{... | collective-permute-start | bytes 147464 | tf_op jit(solution)/shard_map/ppermute | solution.py:455
  68.6 6.0 %collective-permute-start.11 = (f32[96,128]{1,0:T(8,128)S(1)}, f32[96,128]{1,0:T(8,128)S(1)}, u32[]{:S(2)}, u32[]{:S(2)}) collective-permute-start(f32[96,128]{1,0:T(8,128)S(1)} %get-tuple-element.45), channel_id=1, source_target_pairs={{1,0},{2,1},{3,2},{5,4},{6,5},{7,6},{9,8},{10,9},{11,10},{13,12},{... | collective-permute-start | bytes 147464 | tf_op jit(solution)/shard_map/ppermute | solution.py:460
  75.2 1.7 %collective-permute-start.12 = (f32[336,128]{1,0:T(8,128)S(1)}, f32[336,128]{1,0:T(8,128)S(1)}, u32[]{:S(2)}, u32[]{:S(2)}) collective-permute-start(f32[336,128]{1,0:T(8,128)S(1)} %get-tuple-element.46), channel_id=1, source_target_pairs={{0,4},{4,0},{8,12},{12,8},{16,20},{20,16},{24,28},{28,24},{1,5},{5... | collective-permute-start | bytes 516104 | tf_op jit(solution)/shard_map/ppermute | solution.py:469
  79.6 4.5 %collective-permute-start.14 = (f32[64,128]{1,0:T(8,128)S(1)}, f32[64,128]{1,0:T(8,128)S(1)}, u32[]{:S(2)}, u32[]{:S(2)}) collective-permute-start(f32[64,128]{1,0:T(8,128)S(1)} %get-tuple-element.49), channel_id=1, source_target_pairs={{0,1},{1,2},{2,3},{4,5},{5,6},{6,7},{8,9},{9,10},{10,11},{12,13},{... | collective-permute-start | bytes 98312 | tf_op jit(solution)/shard_map/ppermute | solution.py:455
  82.5 5.8 %collective-permute-start.15 = (f32[64,128]{1,0:T(8,128)S(1)}, f32[64,128]{1,0:T(8,128)S(1)}, u32[]{:S(2)}, u32[]{:S(2)}) collective-permute-start(f32[64,128]{1,0:T(8,128)S(1)} %get-tuple-element.50), channel_id=1, source_target_pairs={{1,0},{2,1},{3,2},{5,4},{6,5},{7,6},{9,8},{10,9},{11,10},{13,12},{... | collective-permute-start | bytes 98312 | tf_op jit(solution)/shard_map/ppermute | solution.py:460
  88.9 9.6 %collective-permute-start.16 = (f32[192,128]{1,0:T(8,128)S(1)}, f32[192,128]{1,0:T(8,128)S(1)}, u32[]{:S(2)}, u32[]{:S(2)}) collective-permute-start(f32[192,128]{1,0:T(8,128)S(1)} %get-tuple-element.51), channel_id=1, source_target_pairs={{0,4},{4,0},{8,12},{12,8},{16,20},{20,16},{24,28},{28,24},{1,5},{5... | collective-permute-start | bytes 294920 | tf_op jit(solution)/shard_map/ppermute | solution.py:469
  94.9 3.6 %collective-permute-start.17 = (f32[192,128]{1,0:T(8,128)S(1)}, f32[192,128]{1,0:T(8,128)S(1)}, u32[]{:S(2)}, u32[]{:S(2)}) collective-permute-start(f32[192,128]{1,0:T(8,128)S(1)} %get-tuple-element.52), channel_id=1, source_target_pairs={{4,8},{8,4},{12,16},{16,12},{20,24},{24,20},{5,9},{9,5},{13,17},{1... | collective-permute-start | bytes 294920 | tf_op jit(solution)/shard_map/ppermute | solution.py:468
  113.0 5.3 %collective-permute-start.18 = (f32[48,128]{1,0:T(8,128)S(1)}, f32[48,128]{1,0:T(8,128)S(1)}, u32[]{:S(2)}, u32[]{:S(2)}) collective-permute-start(f32[48,128]{1,0:T(8,128)S(1)} %get-tuple-element.58), channel_id=1, source_target_pairs={{0,4},{4,0},{8,12},{12,8},{16,20},{20,16},{24,28},{28,24},{1,5},{5... | collective-permute-start | bytes 73736 | tf_op jit(solution)/shard_map/ppermute | solution.py:498
  118.3 6.1 %collective-permute-start.19 = (f32[48,128]{1,0:T(8,128)S(1)}, f32[48,128]{1,0:T(8,128)S(1)}, u32[]{:S(2)}, u32[]{:S(2)}) collective-permute-start(f32[48,128]{1,0:T(8,128)S(1)} %add.26), channel_id=1, source_target_pairs={{0,16},{4,20},{8,24},{12,28},{16,0},{20,4},{24,8},{28,12},{1,17},{... | collective-permute-start | bytes 73736 | tf_op jit(solution)/shard_map/ppermute | solution.py:498
  121.4 4.7 %collective-permute-start.20 = (f32[48,128]{1,0:T(8,128)S(1)}, f32[48,128]{1,0:T(8,128)S(1)}, u32[]{:S(2)}, u32[]{:S(2)}) collective-permute-start(f32[48,128]{1,0:T(8,128)S(1)} %add.26), channel_id=1, source_target_pairs={{0,8},{4,12},{8,16},{12,20},{16,24},{20,28},{24,0},{28,4},{1,9},{5... | collective-permute-start | bytes 73736 | tf_op jit(solution)/shard_map/ppermute | solution.py:498
  121.7 4.5 %collective-permute-start.21 = (f32[48,128]{1,0:T(8,128)S(1)}, f32[48,128]{1,0:T(8,128)S(1)}, u32[]{:S(2)}, u32[]{:S(2)}) collective-permute-start(f32[48,128]{1,0:T(8,128)S(1)} %add.26), channel_id=1, source_target_pairs={{0,24},{4,28},{8,0},{12,4},{16,8},{20,12},{24,16},{28,20},{1,25},{... | collective-permute-start | bytes 73736 | tf_op jit(solution)/shard_map/ppermute | solution.py:498
  126.2 4.8 %collective-permute-start.22 = (f32[48,128]{1,0:T(8,128)S(1)}, f32[48,128]{1,0:T(8,128)S(1)}, u32[]{:S(2)}, u32[]{:S(2)}) collective-permute-start(f32[48,128]{1,0:T(8,128)S(1)} %add_add_fusion.1), channel_id=1, source_target_pairs={{0,2},{1,3},{2,0},{3,1},{4,6},{5,7},{6,4},{7,5},{8,10},{9,11},{10,... | collective-permute-start | bytes 73736 | tf_op jit(solution)/shard_map/ppermute | solution.py:498
  126.8 5.6 %collective-permute-start.23 = (f32[48,128]{1,0:T(8,128)S(1)}, f32[48,128]{1,0:T(8,128)S(1)}, u32[]{:S(2)}, u32[]{:S(2)}) collective-permute-start(f32[48,128]{1,0:T(8,128)S(1)} %add_add_fusion.1), channel_id=1, source_target_pairs={{0,1},{1,2},{2,3},{3,0},{4,5},{5,6},{6,7},{7,4},{8,9},{9,10},{10,1... | collective-permute-start | bytes 73736 | tf_op jit(solution)/shard_map/ppermute | solution.py:498
  127.4 5.0 %collective-permute-start.24 = (f32[48,128]{1,0:T(8,128)S(1)}, f32[48,128]{1,0:T(8,128)S(1)}, u32[]{:S(2)}, u32[]{:S(2)}) collective-permute-start(f32[48,128]{1,0:T(8,128)S(1)} %add_add_fusion.1), channel_id=1, source_target_pairs={{0,3},{1,0},{2,1},{3,2},{4,7},{5,4},{6,5},{7,6},{8,11},{9,8},{10,9... | collective-permute-start | bytes 73736 | tf_op jit(solution)/shard_map/ppermute | solution.py:498
  (5 other events, 140.6 us)

commit v4 on v3

--- a/solution.py
+++ b/solution.py
@@ -58,6 +58,15 @@
         a, b, (((1,), (1,)), ((), ())),
         precision=lax.Precision.HIGHEST, preferred_element_type=F32,
     )
+
+
+def by_pairs(cols, one):
+    def body(h, carry):
+        for u in range(2):
+            one(h + u * (cols // 2), u)
+        return carry
+
+    lax.fori_loop(0, cols // 2, body, 0)
 
 
 def lane_index(rows):
@@ -83,14 +92,15 @@
     lax.fori_loop(0, cols, body, 0)
 
 
-def theta_kernel(flags, x_ref, ylo, yhi, xa, xb, out_ref, ca, cb, work, parts):
+def theta_kernel(flags, x_ref, ylo, yhi, xa, xb, out_ref, ca, cb, works, parts):
     cols, nx, ny, _ = x_ref.shape
     lanes = lane_index(ny)
     half = nx // 2 * DEEP
     even = flags[4]
     parts[pl.ds(2 * cols * 8, 128 * 8 - 2 * cols * 8), :] = jnp.ones((128 * 8 - 2 * cols * 8, 128), F32)
 
-    def body(f, carry):
+    def one(f, u):
+        work = works.at[u]
         for buf, high in ((xa, even), (xb, 1 - even)):
             work[high * (nx + 1), pl.ds(PAD, ny), :] = buf[f, (1 - high) * (DEEP - 1)]
         for i in range(nx):
@@ -113,9 +123,8 @@
             rows = pl.ds(pl.multiple_of(high * half, half), half)
             out[f, pl.ds(0, half), :] = ylo[f, rows, :]
             out[f, pl.ds(half, half), :] = yhi[f, rows, :]
-        return carry
-
-    lax.fori_loop(0, cols, body, 0)
+
+    by_pairs(cols, one)
     total = parts[pl.ds(0, 128, stride=8), :]
     for k in range(1, 8):
         total = total + parts[pl.ds(k, 128, stride=8), :]
@@ -131,7 +140,7 @@
 def pre_kernel(
     flags, sums, x_ref, ylo, yhi, xa, xb, ca, cb,
     r_ref, e_ref, c_ref, slo, shi, elo, ehi,
-    work, other, rhs, small, coarse,
+    works, others, rhss, smalls, coarse,
 ):
     cols, nx, ny, _ = x_ref.shape
     tall = ny + 2 * DEEP
@@ -160,13 +169,15 @@
     def _():
         zero = jnp.zeros((8, 128), F32)
         for i in range(wide):
-            for buf in (work, other):
-                buf[i, pl.ds(0, PAD), :] = zero
-                buf[i, pl.ds(PAD + tall, 8), :] = zero
+            for buf in (works, others):
+                for u in range(2):
+                    buf[u, i, pl.ds(0, PAD), :] = zero
+                    buf[u, i, pl.ds(PAD + tall, 8), :] = zero
 
     data = pl.ds(PAD, tall)
 
-    def body(f, carry):
+    def one(f, u):
+        work, other, rhs, small = works.at[u], others.at[u], rhss.at[u], smalls.at[u]
         th = jnp.sum(jnp.where(spot == f, theta, 0.0)) * 0.125
         for i in range(DEEP):
             for buf, corner, high in ((xa, ca, even), (xb, cb, 1 - even)):
@@ -225,9 +236,9 @@
             before, center = center, after
         for i in range(2, wide - 2):
             r_ref[f, i - 2] = rhs[i]
-        return carry
-
-    lax.fori_loop(0, cols, body, 0)
+
+    by_pairs(cols, one)
+    small = smalls.at[0]
     half, cx, cy = cols // 2, nx // 2, ny // 2
     even = spot % 2 == 0
     for g in range(half):
@@ -334,13 +345,13 @@
 
 def post_kernel(
     flags, e_ref, ylo, yhi, xa, xb, c_ref, cylo, cyhi, cxa, cxb, r_ref,
-    w_ref, image_ref, work, other, coarse, small,
+    w_ref, image_ref, works, others, coarses, smalls,
 ):
     cols, nx, ny, _ = e_ref.shape
-    half, cx, cy, _ = c_ref.shape
+    _, cx, cy, _ = c_ref.shape
     ctall = cy + 2 * CP
     parity = lane_index(16) % 2
-    coarse[:, pl.ds(8, 8), :] = jnp.zeros((cx + 2 * CP, 8, 128), F32)
+    coarses[:, :, pl.ds(8, 8), :] = jnp.zeros((2, cx + 2 * CP, 8, 128), F32)
     tall = ny + 2 * DEEP
     wide = nx + 2 * POST
     span = ny + 2 * POST
@@ -353,9 +364,10 @@
     mask_y = RELAX * jnp.where(row < DEEP, has[2], jnp.where(row >= ny + DEEP, has[3], 1.0))
     zero = jnp.zeros((PAD + 8, 128), F32)
     for i in range(wide):
-        for buf in (work, other):
-            buf[i, pl.ds(0, PAD + 8), :] = zero
-            buf[i, pl.ds(PAD + tall - 8, 16), :] = zero
+        for buf in (works, others):
+            for u in range(2):
+                buf[u, i, pl.ds(0, PAD + 8), :] = zero
+                buf[u, i, pl.ds(PAD + tall - 8, 16), :] = zero
 
     def relax_of(i):
         if i < POST:
@@ -366,17 +378,19 @@
 
     data = pl.ds(PAD, tall)
 
-    def body(f, carry):
-        g = lax.rem(f, half)
-        for i in range(CP):
-            at = pl.ds((g * CP + i) * ctall, ctall)
-            for buf, high in ((cxa, even), (cxb, 1 - even)):
-                coarse[high * (cx + CP) + i, pl.ds(0, ctall), :] = buf[at, :]
-        for i in range(cx):
-            at = pl.ds((g * cx + i) * CP, CP)
-            coarse[i + CP, pl.ds(0, CP), :] = cylo[at, :]
-            coarse[i + CP, pl.ds(CP, cy), :] = c_ref[g, i]
-            coarse[i + CP, pl.ds(CP + cy, CP), :] = cyhi[at, :]
+    def one(f, u):
+        work, other, coarse, small = works.at[u], others.at[u], coarses.at[0], smalls.at[u]
+        if u == 0:
+            g = f
+            for i in range(CP):
+                at = pl.ds((g * CP + i) * ctall, ctall)
+                for buf, high in ((cxa, even), (cxb, 1 - even)):
+                    coarse[high * (cx + CP) + i, pl.ds(0, ctall), :] = buf[at, :]
+            for i in range(cx):
+                at = pl.ds((g * cx + i) * CP, CP)
+                coarse[i + CP, pl.ds(0, CP), :] = cylo[at, :]
+                coarse[i + CP, pl.ds(CP, cy), :] = c_ref[g, i]
+                coarse[i + CP, pl.ds(CP + cy, CP), :] = cyhi[at, :]
         for i in range(POST):
             at = pl.ds((f * POST + i) * span, span)
             for buf, high in ((xa, even), (xb, 1 - even)):
@@ -386,11 +400,9 @@
             work[i + POST, pl.ds(PAD + gap, POST), :] = ylo[f, at, :]
             work[i + POST, pl.ds(PAD + DEEP, ny), :] = e_ref[f, i]
             work[i + POST, pl.ds(PAD + DEEP + ny, POST), :] = yhi[f, at, :]
-        upper = jnp.where(f >= half, 1, 0)
         for m in range(cx + 2 * CP):
             both = coarse[m]
-            moved = jnp.where(parity == 1, pltpu.roll(both, 1, 1), pltpu.roll(both, 127, 1))
-            value = jnp.where(parity == upper, both, moved)
+            value = jnp.where(parity == u, both, pltpu.roll(both, 127 if u else 1, 1))
             small[m % 2, pl.ds(0, 16, stride=2), :] = value
             small[m % 2, pl.ds(1, 16, stride=2), :] = value
             up = small[m % 2, pl.ds(0, tall), :]
@@ -413,23 +425,23 @@
         for i in range(POST, nx + POST):
             after = src[i + 1, own_rows, :]
             near = beside(src, i, PAD + DEEP, ny, center, before, after, own)
-            w_ref[f, i - POST] = center
-            image_ref[f, i - POST] = 6.0 * center - near
+            rows = pl.ds((i - POST) * ny * cols + f, ny, stride=cols)
+            w_ref[rows, :] = center
+            image_ref[rows, :] = 6.0 * center - near
             before, center = center, after
-        return carry
-
-    lax.fori_loop(0, cols, body, 0)
-
-
-def image_kernel(flags, x_ref, p_ref, ylo, yhi, xa, xb, ax_ref, ap_ref, work):
+
+    by_pairs(cols, one)
+
+
+def image_kernel(flags, x_ref, p_ref, ylo, yhi, xa, xb, tx_ref, tp_ref, ax_ref, ap_ref, work):
     cols, nx, ny, _ = x_ref.shape
     even = flags[4]
     lanes = lane_index(ny)
 
     def body(f, carry):
-        for ref, out, first, base, deep in (
-            (x_ref, ax_ref, 0, 0, DEEP),
-            (p_ref, ap_ref, DEEP, nx * DEEP, 1),
+        for ref, same, out, first, base, deep in (
+            (x_ref, tx_ref, ax_ref, 0, 0, DEEP),
+            (p_ref, tp_ref, ap_ref, DEEP, nx * DEEP, 1),
         ):
             for buf, high in ((xa, even), (xb, 1 - even)):
                 plane = first + (1 - high) * (deep - 1)
@@ -443,7 +455,9 @@
             for i in range(nx):
                 after = work[i + 2, pl.ds(PAD, ny), :]
                 near = beside(work, i + 1, PAD, ny, center, before, after, lanes)
-                out[f, i] = 6.0 * center - near
+                rows = pl.ds(i * ny * cols + f, ny, stride=cols)
+                same[rows, :] = center
+                out[rows, :] = 6.0 * center - near
                 before, center = center, after
         return carry
 
@@ -516,12 +530,11 @@
     chunks, rows, wide = s_ref.shape
     cols = rows // 6
     ny = wide // 128
-    stride = x_ref.shape[0] // cols
 
     def body(c, carry):
         for k, (b_ref, a_ref) in enumerate(((x_ref, ax_ref), (w_ref, aw_ref), (p_ref, ap_ref))):
             for y in range(ny):
-                pick = pl.ds(c * ny + y, cols, stride=stride)
+                pick = pl.ds(pl.multiple_of((c * ny + y) * cols, cols), cols)
                 at = pl.ds(y * 128, 128)
                 for ref, put in (
                     (b_ref, lambda r, v: s_ref.__setitem__((c, r, at), v)),
@@ -548,18 +561,29 @@
 
 def eliminate(left, right, first):
     size = left.shape[0]
-    row = lax.broadcasted_iota(jnp.int32, (size, 1), 0)
-    scale = jnp.zeros((size, 1), F32)
+    tiles = size // 8
+    lefts = [left[8 * t : 8 * t + 8] for t in range(tiles)]
+    rights = [right[8 * t : 8 * t + 8] for t in range(tiles)]
+    row = lax.broadcasted_iota(jnp.int32, (8, 1), 0)
+    scales = [jnp.zeros((8, 1), F32) for _ in range(tiles)]
     for k in range(size):
-        pivot = left[k : k + 1, first + k : first + k + 1]
-        column = left[:, first + k : first + k + 1]
-        factor = jnp.where(row > k, column / pivot, 0.0)
-        scale = jnp.where(row == k, pivot, scale)
-        line, other = left[k : k + 1], right[k : k + 1]
-        left = left - factor * line
-        right = right - factor * other
-    scale = lax.rsqrt(scale)
-    return left * scale, right * scale
+        own, at = k // 8, k % 8
+        line, other = lefts[own][at : at + 1], rights[own][at : at + 1]
+        pivot = line[:, first + k : first + k + 1]
+        inverse = 1.0 / pivot
+        line, other = line * inverse, other * inverse
+        scales[own] = jnp.where(row == at, pivot, scales[own])
+        for t in range(own, tiles):
+            column = lefts[t][:, first + k : first + k + 1]
+            if t == own:
+                column = jnp.where(row > at, column, 0.0)
+            lefts[t] = lefts[t] - column * line
+            rights[t] = rights[t] - column * other
+    scales = [lax.rsqrt(scale) for scale in scales]
+    return (
+        jnp.concatenate([v * scale for v, scale in zip(lefts, scales)], axis=0),
+        jnp.concatenate([v * scale for v, scale in zip(rights, scales)], axis=0),
+    )
 
 
 def finish_kernel(ncells, sums_ref, s_ref, block_ref, search_ref, bufs, sems):
@@ -592,7 +616,7 @@
             for k, ref in enumerate((block_ref, search_ref))
         ]
 
-    for c in range(chunks):
+    def chunk(c, carry):
         for y in range(0, ny, 2):
             got = jnp.dot(
                 terms, s_ref[c, :, pl.ds(y * 128, 256)], preferred_element_type=F32
@@ -605,9 +629,15 @@
                     flat[pl.ds(y + j, cols, stride=ny), :] = value[:, j * 128 : (j + 1) * 128]
         for copy in copies(c):
             copy.start()
-    for c in range(chunks):
+        return carry
+
+    def finish(c, carry):
         for copy in copies(c):
             copy.wait()
+        return carry
+
+    lax.fori_loop(0, chunks, chunk, 0, unroll=4 if chunks % 4 == 0 else 1)
+    lax.fori_loop(0, chunks, finish, 0)
 
 
 def step(x, p):
@@ -631,7 +661,7 @@
     sums, to_clo, to_chi = call(
         theta_kernel,
         [shape(devices, 8, 128)] + [shape(cols, nx * DEEP, nz)] * 2,
-        [work((nx + 2, PAD + ny + 8, nz), F32), work((128 * 8, nz), F32)],
+        [work((2, nx + 2, PAD + ny + 8, nz), F32), work((128 * 8, nz), F32)],
         (flags, x, ylo, yhi, xlo, xhi), smem=1,
     )
     clo, chi = swap(to_clo, to_chi, "gx")
@@ -644,8 +674,8 @@
         [shape(cols, wide - 4, tall, nz), shape(cols, nx, ny, nz), shape(half, cx, cy, nz)]
         + [shape(half * cx * CO, nz)] * 2
         + [shape(cols, nx * POST, nz)] * 2,
-        [work((wide, plane, nz), F32)] * 2
-        + [work((wide, tall, nz), F32), work((ny, nz), F32), work((cols, cx, cy, nz), F32)],
+        [work((2, wide, plane, nz), F32)] * 2
+        + [work((2, wide, tall, nz), F32), work((2, ny, nz), F32), work((cols, cx, cy, nz), F32)],
         (flags, sums, x, ylo, yhi, xlo, xhi, clo, chi), smem=1,
     )
 
@@ -675,19 +705,19 @@
     )
     dxlo, dxhi = swap(to_xlo, to_xhi, "gx")
 
-    image_x, image_p = call(
-        image_kernel, [shape(cols, nx, ny, nz)] * 2,
+    flat_x, flat_p, image_x, image_p = call(
+        image_kernel, [shape(nx * ny * cols, nz)] * 4,
         [work((nx + 2, PAD + ny + 8, nz), F32)],
         (flags, x, p, ylo, yhi, xlo, xhi), smem=1,
     )
     w, image_w = call(
-        post_kernel, [shape(cols, nx, ny, nz)] * 2,
-        [work((nx + 2 * POST, plane, nz), F32)] * 2
-        + [work((cx + 2 * CP, 16, nz), F32), work((2, 32, nz), F32)],
+        post_kernel, [shape(nx * ny * cols, nz)] * 2,
+        [work((2, nx + 2 * POST, plane, nz), F32)] * 2
+        + [work((2, cx + 2 * CP, 16, nz), F32), work((2, 2, 32, nz), F32)],
         (flags, e, eylo, eyhi, exlo, exhi, d, dylo, dyhi, dxlo, dxhi, r), smem=1,
     )
 
-    flat = [v.reshape(cols * nx * ny, nz) for v in (x, w, p, image_x, image_w, image_p)]
+    flat = (flat_x, w, flat_p, image_x, image_w, image_p)
     nb = 3 * cols
     part, split = call(
         gram_kernel,

time: 141 us -> 136 us (0.965)
  Pallas kernels: 42.6 us -> 37.6 us
  waiting for transfers between devices: 31.5 us -> 35.2 us
  starting transfers between devices: 45.1 us -> 41.7 us
    pallas_call x10, Pallas kernels: 34.8 us -> 29.9 us  [call(): pl.pallas_call(kernel, out_shape=outs, in_specs=specs, out_specs=[VMEM] *...]
    ppermute x7, waiting for transfers between devices: 4.45 us -> 8.1 us  [sum_all(): parts.append(lax.ppermute(value, axis, pairs))]
    ppermute x7, starting transfers between devices: 14.9 us -> 11.5 us  [sum_all(): parts.append(lax.ppermute(value, axis, pairs))]
  transfers between devices with their start and end apart: 25 -> 25, of which waited for: 13 -> 14; matrix products, arithmetic and copies ran while one was open for 0% -> 0% of each run, Pallas kernels for 5% -> 6%
where the time goes in v4:
time: 136 us; the launch traced here: 135 us
  starting transfers between devices  41.7 us (31%)
  Pallas kernels  37.6 us (28%)
  waiting for transfers between devices  35.2 us (26%)
  blocking collectives  17.6 us (13%)
  local copies, waits for them, and re-layouts  2.57 us (2%)
    pallas_call x10, Pallas kernels, call(): pl.pallas_call(kernel, out_shape=outs, in_specs=specs, out_specs=[VMEM] *...  29.9 us
    all_to_all x1, blocking collectives, step(): sums = lax.all_to_all(sums, ('gx', 'gy'), 0, 0)  17.6 us
    ppermute x4, waiting for transfers between devices, from_high(): return lax.ppermute(value, axis, [(i + 1, i) for i in range(count - 1)])  17.3 us
    ppermute x4, starting transfers between devices, from_low(): return lax.ppermute(value, axis, [(i, i + 1) for i in range(count - 1)])  11.5 us
    ppermute x7, starting transfers between devices, sum_all(): parts.append(lax.ppermute(value, axis, pairs))  11.5 us
    ppermute x5, starting transfers between devices, swap(): return (lax.ppermute(one, axis, pairs[0]), two)  10.1 us
    ppermute x4, waiting for transfers between devices, from_low(): return lax.ppermute(value, axis, [(i, i + 1) for i in range(count - 1)])  9.37 us
    ppermute x7, waiting for transfers between devices, sum_all(): parts.append(lax.ppermute(value, axis, pairs))  8.1 us
  transfers between devices with their start and end apart: 25, of which 14 were waited for; matrix products, arithmetic and copies ran while one was open for 0% of the time, Pallas kernels for 6%

profile of v4, /device:TPU:0, one launch (start us, length us, event | category | flops | bytes accessed | tf_op | source)
XLA Modules:
  0.0 135.5 jit_solution(18413406979166804842)
XLA Ops:
  5.3 4.5 %collective-permute-start = (f32[16,40,128]{2,1,0:T(8,128)S(1)}, f32[16,40,128]{2,1,0:T(8,128)S(1)}, u32[]{:S(2)}, u32[]{:S(2)}) collective-permute-start(f32[16,40,128]{2,1,0:T(8,128)S(1)} %get-tuple-element.33), channel_id=1, source_target_pairs={{0,1},{1,2},{2,3},{4,5},{5,6},{6,7},{8,9},{9,10},{10,11},{12,13},{... | collective-permute-start | bytes 983048 | tf_op jit(solution)/shard_map/ppermute | solution.py:469
  11.1 4.9 %collective-permute-done.ylo = f32[16,40,128]{2,1,0:T(8,128)S(1)} collective-permute-done((f32[16,40,128]{2,1,0:T(8,128)S(1)}, f32[16,40,128]{2,1,0:T(8,128)S(1)}, u32[]{:S(2)}, u32[]{:S(2)}) %collective-permute-start) | collective-permute-done | bytes 327712 | tf_op jit(solution)/shard_map/ppermute | solution.py:469
  16.1 4.7 %collective-permute-done.1.yhi = f32[16,40,128]{2,1,0:T(8,128)S(1)} collective-permute-done((f32[16,40,128]{2,1,0:T(8,128)S(1)}, f32[16,40,128]{2,1,0:T(8,128)S(1)}, u32[]{:S(2)}, u32[]{:S(2)}) %collective-permute-start.1) | collective-permute-done | bytes 327712 | tf_op jit(solution)/shard_map/ppermute | solution.py:474
  20.8 2.2 %shard_map.43 = (f32[32,8,128]{2,1,0:T(8,128)S(1)}, f32[16,32,128]{2,1,0:T(8,128)S(1)}, f32[16,32,128]{2,1,0:T(8,128)S(1)}) custom-call(s32[5]{0:T(128)S(1)} %convert_element_type.3.flags, f32[16,8,16,128]{3,2,1,0:T(8,128)S(1)} %copy-done, f32[16,40,128]{2,1,0:T(8,128)S(1)} %collective-permute-done.ylo, f32[16,40,128]{2,1,0:T(8,128)S(1)} %collective-permute-done.1.yhi, ...), custom_call_target="tpu_custom_call" | custom-call | tf_op jit(solution)/shard_map/pallas_call | solution.py:33
  23.0 2.8 %collective-permute-start.4 = (f32[16,32,128]{2,1,0:T(8,128)S(1)}, f32[16,32,128]{2,1,0:T(8,128)S(1)}, u32[]{:S(2)}, u32[]{:S(2)}) collective-permute-start(f32[16,32,128]{2,1,0:T(8,128)S(1)} %get-tuple-element.39), channel_id=1, source_target_pairs={{0,4},{4,0},{8,12},{12,8},{16,20},{20,16},{24,28},{28,24},{1,5},{5... | collective-permute-start | bytes 786440 | tf_op jit(solution)/shard_map/ppermute | solution.py:483
  26.5 17.6 %all_to_all.5.sums = f32[32,8,128]{2,1,0:T(8,128)S(1)} all-to-all(f32[32,8,128]{2,1,0:T(8,128)S(1)} %get-tuple-element.38), channel_id=1, replica_groups=mesh['gx'=8,'gy'=4] {'gx','gy'}, dimensions={0} | all-to-all | bytes 262144 | tf_op jit(solution)/shard_map/all_to_all | solution.py:668
  44.0 8.3 %shard_map.44 = (f32[16,12,24,128]{3,2,1,0:T(8,128)S(1)}, f32[16,8,16,128]{3,2,1,0:T(8,128)S(1)}, f32[8,4,8,128]{3,2,1,0:T(8,128)S(1)}, f32[96,128]{1,0:T(8,128)...) custom-call(s32[5]{0:T(128)S(1)} %convert_element_type.3.flags, ...), custom_call_target="tpu_custom_call" | custom-call | tf_op jit(solution)/shard_map/pallas_call | solution.py:33
  55.1 3.7 %collective-permute-done.6.ylo = f32[16,24,128]{2,1,0:T(8,128)S(1)} collective-permute-done((f32[16,24,128]{2,1,0:T(8,128)S(1)}, f32[16,24,128]{2,1,0:T(8,128)S(1)}, u32[]{:S(2)}, u32[]{:S(2)}) %collective-permute-start.6) | collective-permute-done | bytes 196640 | tf_op jit(solution)/shard_map/ppermute | solution.py:469
  58.9 4.1 %collective-permute-done.7.yhi = f32[16,24,128]{2,1,0:T(8,128)S(1)} collective-permute-done((f32[16,24,128]{2,1,0:T(8,128)S(1)}, f32[16,24,128]{2,1,0:T(8,128)S(1)}, u32[]{:S(2)}, u32[]{:S(2)}) %collective-permute-start.7) | collective-permute-done | bytes 196640 | tf_op jit(solution)/shard_map/ppermute | solution.py:474
  64.5 2.6 %collective-permute-start.10 = (f32[96,128]{1,0:T(8,128)S(1)}, f32[96,128]{1,0:T(8,128)S(1)}, u32[]{:S(2)}, u32[]{:S(2)}) collective-permute-start(f32[96,128]{1,0:T(8,128)S(1)} %get-tuple-element.47), channel_id=1, source_target_pairs={{0,1},{1,2},{2,3},{4,5},{5,6},{6,7},{8,9},{9,10},{10,11},{12,13},{... | collective-permute-start | bytes 147464 | tf_op jit(solution)/shard_map/ppermute | solution.py:469
  68.9 4.3 %collective-permute-done.11.yhi = f32[96,128]{1,0:T(8,128)S(1)} collective-permute-done((f32[96,128]{1,0:T(8,128)S(1)}, f32[96,128]{1,0:T(8,128)S(1)}, u32[]{:S(2)}, u32[]{:S(2)}) %collective-permute-start.11) | collective-permute-done | bytes 49184 | tf_op jit(solution)/shard_map/ppermute | solution.py:474
  75.5 2.7 %shard_map.47 = (f32[8,4,8,128]{3,2,1,0:T(8,128)S(1)}, f32[64,128]{1,0:T(8,128)S(1)}, f32[64,128]{1,0:T(8,128)S(1)}) custom-call(s32[5]{0:T(128)S(1)} %convert_element_type.3.flags, f32[8,4,8,128]{3,2,1,0:T(8,128)S(1)} %get-tuple-element.46.c_ref, f32[96,128]{1,0:T(8,128)S(1)} %collective-permute-done.10.ylo, f32[96,128]{1,0:T(8,128)S(1)} %collective-permute-done.11.yhi, ...), custom_call_target="tpu_custom_call" | custom-call | tf_op jit(solution)/shard_map/pallas_call | solution.py:33
  78.2 2.9 %collective-permute-start.14 = (f32[64,128]{1,0:T(8,128)S(1)}, f32[64,128]{1,0:T(8,128)S(1)}, u32[]{:S(2)}, u32[]{:S(2)}) collective-permute-start(f32[64,128]{1,0:T(8,128)S(1)} %get-tuple-element.52), channel_id=1, source_target_pairs={{0,1},{1,2},{2,3},{4,5},{5,6},{6,7},{8,9},{9,10},{10,11},{12,13},{... | collective-permute-start | bytes 98312 | tf_op jit(solution)/shard_map/ppermute | solution.py:469
  82.7 4.2 %collective-permute-done.15.yhi.cyhi = f32[64,128]{1,0:T(8,128)S(1)} collective-permute-done((f32[64,128]{1,0:T(8,128)S(1)}, f32[64,128]{1,0:T(8,128)S(1)}, u32[]{:S(2)}, u32[]{:S(2)}) %collective-permute-start.15) | collective-permute-done | bytes 32800 | tf_op jit(solution)/shard_map/ppermute | solution.py:474
  87.5 6.0 %collective-permute-start.16 = (f32[192,128]{1,0:T(8,128)S(1)}, f32[192,128]{1,0:T(8,128)S(1)}, u32[]{:S(2)}, u32[]{:S(2)}) collective-permute-start(f32[192,128]{1,0:T(8,128)S(1)} %get-tuple-element.54), channel_id=1, source_target_pairs={{0,4},{4,0},{8,12},{12,8},{16,20},{20,16},{24,28},{28,24},{1,5},{5... | collective-permute-start | bytes 294920 | tf_op jit(solution)/shard_map/ppermute | solution.py:483
  94.2 3.6 %shard_map.42 = (f32[2048,128]{1,0:T(8,128)S(1)}, f32[2048,128]{1,0:T(8,128)S(1)}, f32[2048,128]{1,0:T(8,128)S(1)}, f32[2048,128]{1,0:T(8,128)S(1)}) custom-call(s32[5]{0:T(128)S(1)} %convert_element_type.3.flags, f32[16,8,16,128]{3,2,1,0:T(8,128)S(1)} %copy-done.1, f32[16,8,16,128]{3,2,1,0:T(8,128)S(1)} %copy-done.3, ...), custom_call_target="tpu_custom_call" | custom-call | tf_op jit(solution)/shard_map/pallas_call | solution.py:33
  97.9 6.2 %shard_map.49 = (f32[2048,128]{1,0:T(8,128)S(1)}, f32[2048,128]{1,0:T(8,128)S(1)}) custom-call(s32[5]{0:T(128)S(1)} %convert_element_type.3.flags, f32[16,8,16,128]{3,2,1,0:T(8,128)S(1)} %get-tuple-element.41.corr_ref.e_ref, f32[16,24,128]{2,1,0:T(8,128)S(1)} %collective-permute-done.6.ylo, f32[16,24,128]{2,1,0:T(8,128)S(1)} %collective-permute-done.7.yhi, ...), custom_call_target="tpu_custom_call" | custom-call | tf_op jit(solution)/shard_map/pallas_call | solution.py:33
  104.0 4.1 %shard_map.50 = (f32[48,128]{1,0:T(8,128)S(1)}, bf16[8,96,2048]{2,1,0:T(8,128)(2,1)S(1)}) custom-call(f32[2048,128]{1,0:T(8,128)S(1)} %get-tuple-element.37.x_ref, f32[2048,128]{1,0:T(8,128)S(1)} %get-tuple-element.57.w_ref, f32[2048,128]{1,0:T(8,128)S(1)} %get-tuple-element.58.p_ref, f32[2048,128]{1,0:T(8,128)S(1)} %get-tuple-element.59.ax_ref, ...), custom_call_target="tpu_custom_call" | custom-call | tf_op jit(solution)/shard_map/pallas_call | solution.py:33
  108.2 4.4 %collective-permute-start.18 = (f32[48,128]{1,0:T(8,128)S(1)}, f32[48,128]{1,0:T(8,128)S(1)}, u32[]{:S(2)}, u32[]{:S(2)}) collective-permute-start(f32[48,128]{1,0:T(8,128)S(1)} %get-tuple-element.62), channel_id=1, source_target_pairs={{0,4},{4,0},{8,12},{12,8},{16,20},{20,16},{24,28},{28,24},{1,5},{5... | collective-permute-start | bytes 73736 | tf_op jit(solution)/shard_map/ppermute | solution.py:512
  113.4 2.8 %collective-permute-start.21 = (f32[48,128]{1,0:T(8,128)S(1)}, f32[48,128]{1,0:T(8,128)S(1)}, u32[]{:S(2)}, u32[]{:S(2)}) collective-permute-start(f32[48,128]{1,0:T(8,128)S(1)} %add.26), channel_id=1, source_target_pairs={{0,24},{4,28},{8,0},{12,4},{16,8},{20,12},{24,16},{28,20},{1,25},{... | collective-permute-start | bytes 73736 | tf_op jit(solution)/shard_map/ppermute | solution.py:512
  116.2 1.7 %collective-permute-start.19 = (f32[48,128]{1,0:T(8,128)S(1)}, f32[48,128]{1,0:T(8,128)S(1)}, u32[]{:S(2)}, u32[]{:S(2)}) collective-permute-start(f32[48,128]{1,0:T(8,128)S(1)} %add.26), channel_id=1, source_target_pairs={{0,16},{4,20},{8,24},{12,28},{16,0},{20,4},{24,8},{28,12},{1,17},{... | collective-permute-start | bytes 73736 | tf_op jit(solution)/shard_map/ppermute | solution.py:512
  117.9 3.0 %collective-permute-done.20 = f32[48,128]{1,0:T(8,128)S(1)} collective-permute-done((f32[48,128]{1,0:T(8,128)S(1)}, f32[48,128]{1,0:T(8,128)S(1)}, u32[]{:S(2)}, u32[]{:S(2)}) %collective-permute-start.20) | collective-permute-done | bytes 24608 | tf_op jit(solution)/shard_map/ppermute | solution.py:512
  121.0 2.0 %collective-permute-start.23 = (f32[48,128]{1,0:T(8,128)S(1)}, f32[48,128]{1,0:T(8,128)S(1)}, u32[]{:S(2)}, u32[]{:S(2)}) collective-permute-start(f32[48,128]{1,0:T(8,128)S(1)} %add_add_fusion.1), channel_id=1, source_target_pairs={{0,1},{1,2},{2,3},{3,0},{4,5},{5,6},{6,7},{7,4},{8,9},{9,10},{10,1... | collective-permute-start | bytes 73736 | tf_op jit(solution)/shard_map/ppermute | solution.py:512
  127.8 7.7 %finish.1 = (f32[16,8,16,128]{3,2,1,0:T(8,128)}, f32[16,8,16,128]{3,2,1,0:T(8,128)}) custom-call(f32[48,128]{1,0:T(8,128)S(1)} %add_add_fusion.sums_ref, bf16[8,96,2048]{2,1,0:T(8,128)(2,1)S(1)} %get-tuple-element.63.s_ref), custom_call_target="tpu_custom_call" | custom-call | tf_op jit(solution)/shard_map/finish/pallas_call | solution.py:730
  (51 shorter events, 23.4 us)
Async XLA Ops:
  4.1 16.7 %collective-permute-start.2 = (f32[16,5,16,128]{3,2,1,0:T(8,128)S(1)}, f32[16,5,16,128]{3,2,1,0:T(8,128)S(1)}, u32[]{:S(2)}, u32[]{:S(2)}) collective-permute-start(f32[16,5,16,128]{3,2,1,0:T(8,128)S(1)} %get-tuple-element.35), channel_id=1, source_target_pairs={{0,4},{4,0},{8,12},{12,8},{16,20},{20,16},{24,28},{28,24},{1,5},{5... | collective-permute-start | bytes 1966088 | tf_op jit(solution)/shard_map/ppermute | solution.py:483
  4.6 16.1 %collective-permute-start.3 = (f32[16,5,16,128]{3,2,1,0:T(8,128)S(1)}, f32[16,5,16,128]{3,2,1,0:T(8,128)S(1)}, u32[]{:S(2)}, u32[]{:S(2)}) collective-permute-start(f32[16,5,16,128]{3,2,1,0:T(8,128)S(1)} %get-tuple-element.36), channel_id=1, source_target_pairs={{4,8},{8,4},{12,16},{16,12},{20,24},{24,20},{5,9},{9,5},{13,17},{1... | collective-permute-start | bytes 1966088 | tf_op jit(solution)/shard_map/ppermute | solution.py:482
  5.3 10.7 %collective-permute-start = (f32[16,40,128]{2,1,0:T(8,128)S(1)}, f32[16,40,128]{2,1,0:T(8,128)S(1)}, u32[]{:S(2)}, u32[]{:S(2)}) collective-permute-start(f32[16,40,128]{2,1,0:T(8,128)S(1)} %get-tuple-element.33), channel_id=1, source_target_pairs={{0,1},{1,2},{2,3},{4,5},{5,6},{6,7},{8,9},{9,10},{10,11},{12,13},{... | collective-permute-start | bytes 983048 | tf_op jit(solution)/shard_map/ppermute | solution.py:469
  9.8 10.9 %collective-permute-start.1 = (f32[16,40,128]{2,1,0:T(8,128)S(1)}, f32[16,40,128]{2,1,0:T(8,128)S(1)}, u32[]{:S(2)}, u32[]{:S(2)}) collective-permute-start(f32[16,40,128]{2,1,0:T(8,128)S(1)} %get-tuple-element.34), channel_id=1, source_target_pairs={{1,0},{2,1},{3,2},{5,4},{6,5},{7,6},{9,8},{10,9},{11,10},{13,12},{... | collective-permute-start | bytes 983048 | tf_op jit(solution)/shard_map/ppermute | solution.py:474
  23.0 21.1 %collective-permute-start.4 = (f32[16,32,128]{2,1,0:T(8,128)S(1)}, f32[16,32,128]{2,1,0:T(8,128)S(1)}, u32[]{:S(2)}, u32[]{:S(2)}) collective-permute-start(f32[16,32,128]{2,1,0:T(8,128)S(1)} %get-tuple-element.39), channel_id=1, source_target_pairs={{0,4},{4,0},{8,12},{12,8},{16,20},{20,16},{24,28},{28,24},{1,5},{5... | collective-permute-start | bytes 786440 | tf_op jit(solution)/shard_map/ppermute | solution.py:483
  25.8 18.3 %collective-permute-start.5 = (f32[16,32,128]{2,1,0:T(8,128)S(1)}, f32[16,32,128]{2,1,0:T(8,128)S(1)}, u32[]{:S(2)}, u32[]{:S(2)}) collective-permute-start(f32[16,32,128]{2,1,0:T(8,128)S(1)} %get-tuple-element.40), channel_id=1, source_target_pairs={{4,8},{8,4},{12,16},{16,12},{20,24},{24,20},{5,9},{9,5},{13,17},{1... | collective-permute-start | bytes 786440 | tf_op jit(solution)/shard_map/ppermute | solution.py:482
  52.4 6.5 %collective-permute-start.6 = (f32[16,24,128]{2,1,0:T(8,128)S(1)}, f32[16,24,128]{2,1,0:T(8,128)S(1)}, u32[]{:S(2)}, u32[]{:S(2)}) collective-permute-start(f32[16,24,128]{2,1,0:T(8,128)S(1)} %get-tuple-element.42), channel_id=1, source_target_pairs={{0,1},{1,2},{2,3},{4,5},{5,6},{6,7},{8,9},{9,10},{10,11},{12,13},{... | collective-permute-start | bytes 589832 | tf_op jit(solution)/shard_map/ppermute | solution.py:469
  53.8 9.2 %collective-permute-start.7 = (f32[16,24,128]{2,1,0:T(8,128)S(1)}, f32[16,24,128]{2,1,0:T(8,128)S(1)}, u32[]{:S(2)}, u32[]{:S(2)}) collective-permute-start(f32[16,24,128]{2,1,0:T(8,128)S(1)} %get-tuple-element.43), channel_id=1, source_target_pairs={{1,0},{2,1},{3,2},{5,4},{6,5},{7,6},{9,8},{10,9},{11,10},{13,12},{... | collective-permute-start | bytes 589832 | tf_op jit(solution)/shard_map/ppermute | solution.py:474
  63.7 34.1 %collective-permute-start.8 = (f32[1056,128]{1,0:T(8,128)S(1)}, f32[1056,128]{1,0:T(8,128)S(1)}, u32[]{:S(2)}, u32[]{:S(2)}) collective-permute-start(f32[1056,128]{1,0:T(8,128)S(1)} %get-tuple-element.44), channel_id=1, source_target_pairs={{0,4},{4,0},{8,12},{12,8},{16,20},{20,16},{24,28},{28,24},{1,5},{5... | collective-permute-start | bytes 1622024 | tf_op jit(solution)/shard_map/ppermute | solution.py:483
  63.8 34.0 %collective-permute-start.9 = (f32[1056,128]{1,0:T(8,128)S(1)}, f32[1056,128]{1,0:T(8,128)S(1)}, u32[]{:S(2)}, u32[]{:S(2)}) collective-permute-start(f32[1056,128]{1,0:T(8,128)S(1)} %get-tuple-element.45), channel_id=1, source_target_pairs={{4,8},{8,4},{12,16},{16,12},{20,24},{24,20},{5,9},{9,5},{13,17},{1... | collective-permute-start | bytes 1622024 | tf_op jit(solution)/shard_map/ppermute | solution.py:482
  64.5 4.4 %collective-permute-start.10 = (f32[96,128]{1,0:T(8,128)S(1)}, f32[96,128]{1,0:T(8,128)S(1)}, u32[]{:S(2)}, u32[]{:S(2)}) collective-permute-start(f32[96,128]{1,0:T(8,128)S(1)} %get-tuple-element.47), channel_id=1, source_target_pairs={{0,1},{1,2},{2,3},{4,5},{5,6},{6,7},{8,9},{9,10},{10,11},{12,13},{... | collective-permute-start | bytes 147464 | tf_op jit(solution)/shard_map/ppermute | solution.py:469
  67.2 6.0 %collective-permute-start.11 = (f32[96,128]{1,0:T(8,128)S(1)}, f32[96,128]{1,0:T(8,128)S(1)}, u32[]{:S(2)}, u32[]{:S(2)}) collective-permute-start(f32[96,128]{1,0:T(8,128)S(1)} %get-tuple-element.48), channel_id=1, source_target_pairs={{1,0},{2,1},{3,2},{5,4},{6,5},{7,6},{9,8},{10,9},{11,10},{13,12},{... | collective-permute-start | bytes 147464 | tf_op jit(solution)/shard_map/ppermute | solution.py:474
  73.7 1.7 %collective-permute-start.12 = (f32[336,128]{1,0:T(8,128)S(1)}, f32[336,128]{1,0:T(8,128)S(1)}, u32[]{:S(2)}, u32[]{:S(2)}) collective-permute-start(f32[336,128]{1,0:T(8,128)S(1)} %get-tuple-element.49), channel_id=1, source_target_pairs={{0,4},{4,0},{8,12},{12,8},{16,20},{20,16},{24,28},{28,24},{1,5},{5... | collective-permute-start | bytes 516104 | tf_op jit(solution)/shard_map/ppermute | solution.py:483
  78.2 4.5 %collective-permute-start.14 = (f32[64,128]{1,0:T(8,128)S(1)}, f32[64,128]{1,0:T(8,128)S(1)}, u32[]{:S(2)}, u32[]{:S(2)}) collective-permute-start(f32[64,128]{1,0:T(8,128)S(1)} %get-tuple-element.52), channel_id=1, source_target_pairs={{0,1},{1,2},{2,3},{4,5},{5,6},{6,7},{8,9},{9,10},{10,11},{12,13},{... | collective-permute-start | bytes 98312 | tf_op jit(solution)/shard_map/ppermute | solution.py:469
  81.1 5.8 %collective-permute-start.15 = (f32[64,128]{1,0:T(8,128)S(1)}, f32[64,128]{1,0:T(8,128)S(1)}, u32[]{:S(2)}, u32[]{:S(2)}) collective-permute-start(f32[64,128]{1,0:T(8,128)S(1)} %get-tuple-element.53), channel_id=1, source_target_pairs={{1,0},{2,1},{3,2},{5,4},{6,5},{7,6},{9,8},{10,9},{11,10},{13,12},{... | collective-permute-start | bytes 98312 | tf_op jit(solution)/shard_map/ppermute | solution.py:474
  87.5 10.3 %collective-permute-start.16 = (f32[192,128]{1,0:T(8,128)S(1)}, f32[192,128]{1,0:T(8,128)S(1)}, u32[]{:S(2)}, u32[]{:S(2)}) collective-permute-start(f32[192,128]{1,0:T(8,128)S(1)} %get-tuple-element.54), channel_id=1, source_target_pairs={{0,4},{4,0},{8,12},{12,8},{16,20},{20,16},{24,28},{28,24},{1,5},{5... | collective-permute-start | bytes 294920 | tf_op jit(solution)/shard_map/ppermute | solution.py:483
  93.5 4.3 %collective-permute-start.17 = (f32[192,128]{1,0:T(8,128)S(1)}, f32[192,128]{1,0:T(8,128)S(1)}, u32[]{:S(2)}, u32[]{:S(2)}) collective-permute-start(f32[192,128]{1,0:T(8,128)S(1)} %get-tuple-element.55), channel_id=1, source_target_pairs={{4,8},{8,4},{12,16},{16,12},{20,24},{24,20},{5,9},{9,5},{13,17},{1... | collective-permute-start | bytes 294920 | tf_op jit(solution)/shard_map/ppermute | solution.py:482
  108.2 5.3 %collective-permute-start.18 = (f32[48,128]{1,0:T(8,128)S(1)}, f32[48,128]{1,0:T(8,128)S(1)}, u32[]{:S(2)}, u32[]{:S(2)}) collective-permute-start(f32[48,128]{1,0:T(8,128)S(1)} %get-tuple-element.62), channel_id=1, source_target_pairs={{0,4},{4,0},{8,12},{12,8},{16,20},{20,16},{24,28},{28,24},{1,5},{5... | collective-permute-start | bytes 73736 | tf_op jit(solution)/shard_map/ppermute | solution.py:512
  113.4 4.5 %collective-permute-start.21 = (f32[48,128]{1,0:T(8,128)S(1)}, f32[48,128]{1,0:T(8,128)S(1)}, u32[]{:S(2)}, u32[]{:S(2)}) collective-permute-start(f32[48,128]{1,0:T(8,128)S(1)} %add.26), channel_id=1, source_target_pairs={{0,24},{4,28},{8,0},{12,4},{16,8},{20,12},{24,16},{28,20},{1,25},{... | collective-permute-start | bytes 73736 | tf_op jit(solution)/shard_map/ppermute | solution.py:512
  116.2 4.7 %collective-permute-start.20 = (f32[48,128]{1,0:T(8,128)S(1)}, f32[48,128]{1,0:T(8,128)S(1)}, u32[]{:S(2)}, u32[]{:S(2)}) collective-permute-start(f32[48,128]{1,0:T(8,128)S(1)} %add.26), channel_id=1, source_target_pairs={{0,8},{4,12},{8,16},{12,20},{16,24},{20,28},{24,0},{28,4},{1,9},{5... | collective-permute-start | bytes 73736 | tf_op jit(solution)/shard_map/ppermute | solution.py:512
  116.2 4.7 %collective-permute-start.19 = (f32[48,128]{1,0:T(8,128)S(1)}, f32[48,128]{1,0:T(8,128)S(1)}, u32[]{:S(2)}, u32[]{:S(2)}) collective-permute-start(f32[48,128]{1,0:T(8,128)S(1)} %add.26), channel_id=1, source_target_pairs={{0,16},{4,20},{8,24},{12,28},{16,0},{20,4},{24,8},{28,12},{1,17},{... | collective-permute-start | bytes 73736 | tf_op jit(solution)/shard_map/ppermute | solution.py:512
  121.0 4.1 %collective-permute-start.24 = (f32[48,128]{1,0:T(8,128)S(1)}, f32[48,128]{1,0:T(8,128)S(1)}, u32[]{:S(2)}, u32[]{:S(2)}) collective-permute-start(f32[48,128]{1,0:T(8,128)S(1)} %add_add_fusion.1), channel_id=1, source_target_pairs={{0,3},{1,0},{2,1},{3,2},{4,7},{5,4},{6,5},{7,6},{8,11},{9,8},{10,9... | collective-permute-start | bytes 73736 | tf_op jit(solution)/shard_map/ppermute | solution.py:512
  121.0 5.7 %collective-permute-start.23 = (f32[48,128]{1,0:T(8,128)S(1)}, f32[48,128]{1,0:T(8,128)S(1)}, u32[]{:S(2)}, u32[]{:S(2)}) collective-permute-start(f32[48,128]{1,0:T(8,128)S(1)} %add_add_fusion.1), channel_id=1, source_target_pairs={{0,1},{1,2},{2,3},{3,0},{4,5},{5,6},{6,7},{7,4},{8,9},{9,10},{10,1... | collective-permute-start | bytes 73736 | tf_op jit(solution)/shard_map/ppermute | solution.py:512
  123.1 4.7 %collective-permute-start.22 = (f32[48,128]{1,0:T(8,128)S(1)}, f32[48,128]{1,0:T(8,128)S(1)}, u32[]{:S(2)}, u32[]{:S(2)}) collective-permute-start(f32[48,128]{1,0:T(8,128)S(1)} %add_add_fusion.1), channel_id=1, source_target_pairs={{0,2},{1,3},{2,0},{3,1},{4,6},{5,7},{6,4},{7,5},{8,10},{9,11},{10,... | collective-permute-start | bytes 73736 | tf_op jit(solution)/shard_map/ppermute | solution.py:512
  (5 other events, 138.9 us)

commit v5 on v4

--- a/solution.py
+++ b/solution.py
@@ -266,7 +266,7 @@
 
 
 def coarse_kernel(
-    flags, c_ref, ylo, yhi, xa, xb, corr_ref, slo, shi, work, other, rhs
+    flags, c_ref, ylo, yhi, xa, xb, corr_ref, slo, shi, works, others, rhss
 ):
     half, cx, cy, _ = c_ref.shape
     tall = cy + 2 * CO
@@ -279,10 +279,11 @@
     mask_y = COARSE_RELAX * jnp.where(row < CO, has[2], jnp.where(row >= cy + CO, has[3], 1.0))
     zero = jnp.zeros((8, 128), F32)
     for i in range(wide):
-        rhs[i, pl.ds(8, 8), :] = zero
-        for buf in (work, other):
-            buf[i, pl.ds(0, PAD), :] = zero
-            buf[i, pl.ds(PAD + full, 8), :] = zero
+        for u in range(2):
+            rhss[u, i, pl.ds(8, 8), :] = zero
+            for buf in (works, others):
+                buf[u, i, pl.ds(0, PAD), :] = zero
+                buf[u, i, pl.ds(PAD + full, 8), :] = zero
 
     def relax_of(i):
         if i < CO:
@@ -293,7 +294,8 @@
 
     data = pl.ds(PAD, full)
 
-    def body(g, carry):
+    def one(g, u):
+        work, other, rhs = works.at[u], others.at[u], rhss.at[u]
         for i in range(CO):
             for buf, high in ((xa, even), (xb, 1 - even)):
                 plane = high * (cx + CO) + i
@@ -320,9 +322,8 @@
             at = pl.ds((g * cx + i) * CP, CP)
             slo[at, :] = src[i + CO, pl.ds(PAD + CO, CP), :]
             shi[at, :] = src[i + CO, pl.ds(PAD + CO + cy - CP, CP), :]
-        return carry
-
-    lax.fori_loop(0, half, body, 0)
+
+    by_pairs(half, one)
 
 
 def post_pack_kernel(flags, corr_ref, ylo, yhi, xa, xb):
@@ -497,7 +498,7 @@
 
 
 def sum_all(value):
-    for axis in ("gx", "gy"):
+    for axis in ("gy", "gx"):
         count = lax.axis_size(axis)
         stride = 1
         for radix in radices(count):
@@ -695,7 +696,7 @@
     d, to_ylo, to_yhi = call(
         coarse_kernel,
         [shape(half, cx, cy, nz)] + [shape(half * cx * CP, nz)] * 2,
-        [work((cwide, PAD + 16 + 8, nz), F32)] * 2 + [work((cwide, 16, nz), F32)],
+        [work((2, cwide, PAD + 16 + 8, nz), F32)] * 2 + [work((2, cwide, 16, nz), F32)],
         (flags, c, cylo, cyhi, cxlo, cxhi), smem=1,
     )
     dylo, dyhi = from_low(to_yhi, "gy"), from_high(to_ylo, "gy")

time: 136 us -> 135 us (level)
  transfers between devices with their start and end apart: 25 -> 25, of which waited for: 14 -> 14; matrix products, arithmetic and copies ran while one was open for 0% -> 0% of each run, Pallas kernels for 6% -> 5%
where the time goes in v5:
time: 135 us
  starting transfers between devices  42.4 us (31%)
  Pallas kernels  36.6 us (27%)
  waiting for transfers between devices  34.5 us (26%)
  blocking collectives  17.6 us (13%)
  local copies, waits for them, and re-layouts  2.57 us (2%)
    pallas_call x10, Pallas kernels, call(): pl.pallas_call(kernel, out_shape=outs, in_specs=specs, out_specs=[VMEM] *...  29 us
    all_to_all x1, blocking collectives, step(): sums = lax.all_to_all(sums, ('gx', 'gy'), 0, 0)  17.6 us
    ppermute x4, waiting for transfers between devices, from_high(): return lax.ppermute(value, axis, [(i + 1, i) for i in range(count - 1)])  17.3 us
    ppermute x7, starting transfers between devices, sum_all(): parts.append(lax.ppermute(value, axis, pairs))  12.2 us
    ppermute x4, starting transfers between devices, from_low(): return lax.ppermute(value, axis, [(i, i + 1) for i in range(count - 1)])  11.5 us
    ppermute x5, starting transfers between devices, swap(): return (lax.ppermute(one, axis, pairs[0]), two)  10.1 us
    ppermute x4, waiting for transfers between devices, from_low(): return lax.ppermute(value, axis, [(i, i + 1) for i in range(count - 1)])  9.37 us
    pallas_call x1, Pallas kernels, step(): pl.pallas_call(functools.partial(finish_kernel, nx * ny * nz * devices),...  7.67 us
  transfers between devices with their start and end apart: 25, of which 14 were waited for; matrix products, arithmetic and copies ran while one was open for 0% of the time, Pallas kernels for 5%

profile of v5, /device:TPU:0, one launch (start us, length us, event | category | flops | bytes accessed | tf_op | source)
XLA Modules:
  0.0 134.5 jit_solution(1120215455038356057)
XLA Ops:
  5.3 4.5 %collective-permute-start = (f32[16,40,128]{2,1,0:T(8,128)S(1)}, f32[16,40,128]{2,1,0:T(8,128)S(1)}, u32[]{:S(2)}, u32[]{:S(2)}) collective-permute-start(f32[16,40,128]{2,1,0:T(8,128)S(1)} %get-tuple-element.33), channel_id=1, source_target_pairs={{0,1},{1,2},{2,3},{4,5},{5,6},{6,7},{8,9},{9,10},{10,11},{12,13},{... | collective-permute-start | bytes 983048 | tf_op jit(solution)/shard_map/ppermute | solution.py:470
  11.1 4.9 %collective-permute-done.ylo = f32[16,40,128]{2,1,0:T(8,128)S(1)} collective-permute-done((f32[16,40,128]{2,1,0:T(8,128)S(1)}, f32[16,40,128]{2,1,0:T(8,128)S(1)}, u32[]{:S(2)}, u32[]{:S(2)}) %collective-permute-start) | collective-permute-done | bytes 327712 | tf_op jit(solution)/shard_map/ppermute | solution.py:470
  16.1 4.7 %collective-permute-done.1.yhi = f32[16,40,128]{2,1,0:T(8,128)S(1)} collective-permute-done((f32[16,40,128]{2,1,0:T(8,128)S(1)}, f32[16,40,128]{2,1,0:T(8,128)S(1)}, u32[]{:S(2)}, u32[]{:S(2)}) %collective-permute-start.1) | collective-permute-done | bytes 327712 | tf_op jit(solution)/shard_map/ppermute | solution.py:475
  20.8 2.2 %shard_map.43 = (f32[32,8,128]{2,1,0:T(8,128)S(1)}, f32[16,32,128]{2,1,0:T(8,128)S(1)}, f32[16,32,128]{2,1,0:T(8,128)S(1)}) custom-call(s32[5]{0:T(128)S(1)} %convert_element_type.3.flags, f32[16,8,16,128]{3,2,1,0:T(8,128)S(1)} %copy-done, f32[16,40,128]{2,1,0:T(8,128)S(1)} %collective-permute-done.ylo, f32[16,40,128]{2,1,0:T(8,128)S(1)} %collective-permute-done.1.yhi, ...), custom_call_target="tpu_custom_call" | custom-call | tf_op jit(solution)/shard_map/pallas_call | solution.py:33
  23.0 2.8 %collective-permute-start.4 = (f32[16,32,128]{2,1,0:T(8,128)S(1)}, f32[16,32,128]{2,1,0:T(8,128)S(1)}, u32[]{:S(2)}, u32[]{:S(2)}) collective-permute-start(f32[16,32,128]{2,1,0:T(8,128)S(1)} %get-tuple-element.39), channel_id=1, source_target_pairs={{0,4},{4,0},{8,12},{12,8},{16,20},{20,16},{24,28},{28,24},{1,5},{5... | collective-permute-start | bytes 786440 | tf_op jit(solution)/shard_map/ppermute | solution.py:484
  26.5 17.6 %all_to_all.5.sums = f32[32,8,128]{2,1,0:T(8,128)S(1)} all-to-all(f32[32,8,128]{2,1,0:T(8,128)S(1)} %get-tuple-element.38), channel_id=1, replica_groups=mesh['gx'=8,'gy'=4] {'gx','gy'}, dimensions={0} | all-to-all | bytes 262144 | tf_op jit(solution)/shard_map/all_to_all | solution.py:669
  44.0 8.3 %shard_map.44 = (f32[16,12,24,128]{3,2,1,0:T(8,128)S(1)}, f32[16,8,16,128]{3,2,1,0:T(8,128)S(1)}, f32[8,4,8,128]{3,2,1,0:T(8,128)S(1)}, f32[96,128]{1,0:T(8,128)...) custom-call(s32[5]{0:T(128)S(1)} %convert_element_type.3.flags, ...), custom_call_target="tpu_custom_call" | custom-call | tf_op jit(solution)/shard_map/pallas_call | solution.py:33
  55.1 3.7 %collective-permute-done.6.ylo = f32[16,24,128]{2,1,0:T(8,128)S(1)} collective-permute-done((f32[16,24,128]{2,1,0:T(8,128)S(1)}, f32[16,24,128]{2,1,0:T(8,128)S(1)}, u32[]{:S(2)}, u32[]{:S(2)}) %collective-permute-start.6) | collective-permute-done | bytes 196640 | tf_op jit(solution)/shard_map/ppermute | solution.py:470
  58.9 4.1 %collective-permute-done.7.yhi = f32[16,24,128]{2,1,0:T(8,128)S(1)} collective-permute-done((f32[16,24,128]{2,1,0:T(8,128)S(1)}, f32[16,24,128]{2,1,0:T(8,128)S(1)}, u32[]{:S(2)}, u32[]{:S(2)}) %collective-permute-start.7) | collective-permute-done | bytes 196640 | tf_op jit(solution)/shard_map/ppermute | solution.py:475
  64.5 2.6 %collective-permute-start.10 = (f32[96,128]{1,0:T(8,128)S(1)}, f32[96,128]{1,0:T(8,128)S(1)}, u32[]{:S(2)}, u32[]{:S(2)}) collective-permute-start(f32[96,128]{1,0:T(8,128)S(1)} %get-tuple-element.47), channel_id=1, source_target_pairs={{0,1},{1,2},{2,3},{4,5},{5,6},{6,7},{8,9},{9,10},{10,11},{12,13},{... | collective-permute-start | bytes 147464 | tf_op jit(solution)/shard_map/ppermute | solution.py:470
  68.9 4.3 %collective-permute-done.11.yhi = f32[96,128]{1,0:T(8,128)S(1)} collective-permute-done((f32[96,128]{1,0:T(8,128)S(1)}, f32[96,128]{1,0:T(8,128)S(1)}, u32[]{:S(2)}, u32[]{:S(2)}) %collective-permute-start.11) | collective-permute-done | bytes 49184 | tf_op jit(solution)/shard_map/ppermute | solution.py:475
  75.5 1.8 %shard_map.47 = (f32[8,4,8,128]{3,2,1,0:T(8,128)S(1)}, f32[64,128]{1,0:T(8,128)S(1)}, f32[64,128]{1,0:T(8,128)S(1)}) custom-call(s32[5]{0:T(128)S(1)} %convert_element_type.3.flags, f32[8,4,8,128]{3,2,1,0:T(8,128)S(1)} %get-tuple-element.46.c_ref, f32[96,128]{1,0:T(8,128)S(1)} %collective-permute-done.10.ylo, f32[96,128]{1,0:T(8,128)S(1)} %collective-permute-done.11.yhi, ...), custom_call_target="tpu_custom_call" | custom-call | tf_op jit(solution)/shard_map/pallas_call | solution.py:33
  77.3 2.9 %collective-permute-start.14 = (f32[64,128]{1,0:T(8,128)S(1)}, f32[64,128]{1,0:T(8,128)S(1)}, u32[]{:S(2)}, u32[]{:S(2)}) collective-permute-start(f32[64,128]{1,0:T(8,128)S(1)} %get-tuple-element.52), channel_id=1, source_target_pairs={{0,1},{1,2},{2,3},{4,5},{5,6},{6,7},{8,9},{9,10},{10,11},{12,13},{... | collective-permute-start | bytes 98312 | tf_op jit(solution)/shard_map/ppermute | solution.py:470
  81.7 4.2 %collective-permute-done.15.yhi.cyhi = f32[64,128]{1,0:T(8,128)S(1)} collective-permute-done((f32[64,128]{1,0:T(8,128)S(1)}, f32[64,128]{1,0:T(8,128)S(1)}, u32[]{:S(2)}, u32[]{:S(2)}) %collective-permute-start.15) | collective-permute-done | bytes 32800 | tf_op jit(solution)/shard_map/ppermute | solution.py:475
  86.6 6.0 %collective-permute-start.16 = (f32[192,128]{1,0:T(8,128)S(1)}, f32[192,128]{1,0:T(8,128)S(1)}, u32[]{:S(2)}, u32[]{:S(2)}) collective-permute-start(f32[192,128]{1,0:T(8,128)S(1)} %get-tuple-element.54), channel_id=1, source_target_pairs={{0,4},{4,0},{8,12},{12,8},{16,20},{20,16},{24,28},{28,24},{1,5},{5... | collective-permute-start | bytes 294920 | tf_op jit(solution)/shard_map/ppermute | solution.py:484
  93.2 3.6 %shard_map.42 = (f32[2048,128]{1,0:T(8,128)S(1)}, f32[2048,128]{1,0:T(8,128)S(1)}, f32[2048,128]{1,0:T(8,128)S(1)}, f32[2048,128]{1,0:T(8,128)S(1)}) custom-call(s32[5]{0:T(128)S(1)} %convert_element_type.3.flags, f32[16,8,16,128]{3,2,1,0:T(8,128)S(1)} %copy-done.1, f32[16,8,16,128]{3,2,1,0:T(8,128)S(1)} %copy-done.3, ...), custom_call_target="tpu_custom_call" | custom-call | tf_op jit(solution)/shard_map/pallas_call | solution.py:33
  96.9 6.2 %shard_map.49 = (f32[2048,128]{1,0:T(8,128)S(1)}, f32[2048,128]{1,0:T(8,128)S(1)}) custom-call(s32[5]{0:T(128)S(1)} %convert_element_type.3.flags, f32[16,8,16,128]{3,2,1,0:T(8,128)S(1)} %get-tuple-element.41.corr_ref.e_ref, f32[16,24,128]{2,1,0:T(8,128)S(1)} %collective-permute-done.6.ylo, f32[16,24,128]{2,1,0:T(8,128)S(1)} %collective-permute-done.7.yhi, ...), custom_call_target="tpu_custom_call" | custom-call | tf_op jit(solution)/shard_map/pallas_call | solution.py:33
  103.1 4.1 %shard_map.50 = (f32[48,128]{1,0:T(8,128)S(1)}, bf16[8,96,2048]{2,1,0:T(8,128)(2,1)S(1)}) custom-call(f32[2048,128]{1,0:T(8,128)S(1)} %get-tuple-element.37.x_ref, f32[2048,128]{1,0:T(8,128)S(1)} %get-tuple-element.57.w_ref, f32[2048,128]{1,0:T(8,128)S(1)} %get-tuple-element.58.p_ref, f32[2048,128]{1,0:T(8,128)S(1)} %get-tuple-element.59.ax_ref, ...), custom_call_target="tpu_custom_call" | custom-call | tf_op jit(solution)/shard_map/pallas_call | solution.py:33
  111.0 3.0 %collective-permute-done.19 = f32[48,128]{1,0:T(8,128)S(1)} collective-permute-done((f32[48,128]{1,0:T(8,128)S(1)}, f32[48,128]{1,0:T(8,128)S(1)}, u32[]{:S(2)}, u32[]{:S(2)}) %collective-permute-start.19) | collective-permute-done | bytes 24608 | tf_op jit(solution)/shard_map/ppermute | solution.py:513
  114.2 2.5 %collective-permute-start.21 = (f32[48,128]{1,0:T(8,128)S(1)}, f32[48,128]{1,0:T(8,128)S(1)}, u32[]{:S(2)}, u32[]{:S(2)}) collective-permute-start(f32[48,128]{1,0:T(8,128)S(1)} %add_add_fusion.1), channel_id=1, source_target_pairs={{0,4},{4,0},{8,12},{12,8},{16,20},{20,16},{24,28},{28,24},{1,5},{5... | collective-permute-start | bytes 73736 | tf_op jit(solution)/shard_map/ppermute | solution.py:513
  117.6 4.5 %collective-permute-start.24 = (f32[48,128]{1,0:T(8,128)S(1)}, f32[48,128]{1,0:T(8,128)S(1)}, u32[]{:S(2)}, u32[]{:S(2)}) collective-permute-start(f32[48,128]{1,0:T(8,128)S(1)} %add.29), channel_id=1, source_target_pairs={{0,24},{4,28},{8,0},{12,4},{16,8},{20,12},{24,16},{28,20},{1,25},{... | collective-permute-start | bytes 73736 | tf_op jit(solution)/shard_map/ppermute | solution.py:513
  122.1 1.7 %collective-permute-start.22 = (f32[48,128]{1,0:T(8,128)S(1)}, f32[48,128]{1,0:T(8,128)S(1)}, u32[]{:S(2)}, u32[]{:S(2)}) collective-permute-start(f32[48,128]{1,0:T(8,128)S(1)} %add.29), channel_id=1, source_target_pairs={{0,16},{4,20},{8,24},{12,28},{16,0},{20,4},{24,8},{28,12},{1,17},{... | collective-permute-start | bytes 73736 | tf_op jit(solution)/shard_map/ppermute | solution.py:513
  123.8 3.0 %collective-permute-done.23 = f32[48,128]{1,0:T(8,128)S(1)} collective-permute-done((f32[48,128]{1,0:T(8,128)S(1)}, f32[48,128]{1,0:T(8,128)S(1)}, u32[]{:S(2)}, u32[]{:S(2)}) %collective-permute-start.23) | collective-permute-done | bytes 24608 | tf_op jit(solution)/shard_map/ppermute | solution.py:513
  126.8 7.7 %finish.1 = (f32[16,8,16,128]{3,2,1,0:T(8,128)}, f32[16,8,16,128]{3,2,1,0:T(8,128)}) custom-call(f32[48,128]{1,0:T(8,128)S(1)} %add_add_fusion.sums_ref, bf16[8,96,2048]{2,1,0:T(8,128)(2,1)S(1)} %get-tuple-element.63.s_ref), custom_call_target="tpu_custom_call" | custom-call | tf_op jit(solution)/shard_map/finish/pallas_call | solution.py:731
  (51 shorter events, 22.6 us)
Async XLA Ops:
  4.1 16.7 %collective-permute-start.2 = (f32[16,5,16,128]{3,2,1,0:T(8,128)S(1)}, f32[16,5,16,128]{3,2,1,0:T(8,128)S(1)}, u32[]{:S(2)}, u32[]{:S(2)}) collective-permute-start(f32[16,5,16,128]{3,2,1,0:T(8,128)S(1)} %get-tuple-element.35), channel_id=1, source_target_pairs={{0,4},{4,0},{8,12},{12,8},{16,20},{20,16},{24,28},{28,24},{1,5},{5... | collective-permute-start | bytes 1966088 | tf_op jit(solution)/shard_map/ppermute | solution.py:484
  4.6 16.1 %collective-permute-start.3 = (f32[16,5,16,128]{3,2,1,0:T(8,128)S(1)}, f32[16,5,16,128]{3,2,1,0:T(8,128)S(1)}, u32[]{:S(2)}, u32[]{:S(2)}) collective-permute-start(f32[16,5,16,128]{3,2,1,0:T(8,128)S(1)} %get-tuple-element.36), channel_id=1, source_target_pairs={{4,8},{8,4},{12,16},{16,12},{20,24},{24,20},{5,9},{9,5},{13,17},{1... | collective-permute-start | bytes 1966088 | tf_op jit(solution)/shard_map/ppermute | solution.py:483
  5.3 10.7 %collective-permute-start = (f32[16,40,128]{2,1,0:T(8,128)S(1)}, f32[16,40,128]{2,1,0:T(8,128)S(1)}, u32[]{:S(2)}, u32[]{:S(2)}) collective-permute-start(f32[16,40,128]{2,1,0:T(8,128)S(1)} %get-tuple-element.33), channel_id=1, source_target_pairs={{0,1},{1,2},{2,3},{4,5},{5,6},{6,7},{8,9},{9,10},{10,11},{12,13},{... | collective-permute-start | bytes 983048 | tf_op jit(solution)/shard_map/ppermute | solution.py:470
  9.8 10.9 %collective-permute-start.1 = (f32[16,40,128]{2,1,0:T(8,128)S(1)}, f32[16,40,128]{2,1,0:T(8,128)S(1)}, u32[]{:S(2)}, u32[]{:S(2)}) collective-permute-start(f32[16,40,128]{2,1,0:T(8,128)S(1)} %get-tuple-element.34), channel_id=1, source_target_pairs={{1,0},{2,1},{3,2},{5,4},{6,5},{7,6},{9,8},{10,9},{11,10},{13,12},{... | collective-permute-start | bytes 983048 | tf_op jit(solution)/shard_map/ppermute | solution.py:475
  23.0 21.1 %collective-permute-start.4 = (f32[16,32,128]{2,1,0:T(8,128)S(1)}, f32[16,32,128]{2,1,0:T(8,128)S(1)}, u32[]{:S(2)}, u32[]{:S(2)}) collective-permute-start(f32[16,32,128]{2,1,0:T(8,128)S(1)} %get-tuple-element.39), channel_id=1, source_target_pairs={{0,4},{4,0},{8,12},{12,8},{16,20},{20,16},{24,28},{28,24},{1,5},{5... | collective-permute-start | bytes 786440 | tf_op jit(solution)/shard_map/ppermute | solution.py:484
  25.8 18.3 %collective-permute-start.5 = (f32[16,32,128]{2,1,0:T(8,128)S(1)}, f32[16,32,128]{2,1,0:T(8,128)S(1)}, u32[]{:S(2)}, u32[]{:S(2)}) collective-permute-start(f32[16,32,128]{2,1,0:T(8,128)S(1)} %get-tuple-element.40), channel_id=1, source_target_pairs={{4,8},{8,4},{12,16},{16,12},{20,24},{24,20},{5,9},{9,5},{13,17},{1... | collective-permute-start | bytes 786440 | tf_op jit(solution)/shard_map/ppermute | solution.py:483
  52.4 6.5 %collective-permute-start.6 = (f32[16,24,128]{2,1,0:T(8,128)S(1)}, f32[16,24,128]{2,1,0:T(8,128)S(1)}, u32[]{:S(2)}, u32[]{:S(2)}) collective-permute-start(f32[16,24,128]{2,1,0:T(8,128)S(1)} %get-tuple-element.42), channel_id=1, source_target_pairs={{0,1},{1,2},{2,3},{4,5},{5,6},{6,7},{8,9},{9,10},{10,11},{12,13},{... | collective-permute-start | bytes 589832 | tf_op jit(solution)/shard_map/ppermute | solution.py:470
  53.8 9.2 %collective-permute-start.7 = (f32[16,24,128]{2,1,0:T(8,128)S(1)}, f32[16,24,128]{2,1,0:T(8,128)S(1)}, u32[]{:S(2)}, u32[]{:S(2)}) collective-permute-start(f32[16,24,128]{2,1,0:T(8,128)S(1)} %get-tuple-element.43), channel_id=1, source_target_pairs={{1,0},{2,1},{3,2},{5,4},{6,5},{7,6},{9,8},{10,9},{11,10},{13,12},{... | collective-permute-start | bytes 589832 | tf_op jit(solution)/shard_map/ppermute | solution.py:475
  63.7 33.1 %collective-permute-start.8 = (f32[1056,128]{1,0:T(8,128)S(1)}, f32[1056,128]{1,0:T(8,128)S(1)}, u32[]{:S(2)}, u32[]{:S(2)}) collective-permute-start(f32[1056,128]{1,0:T(8,128)S(1)} %get-tuple-element.44), channel_id=1, source_target_pairs={{0,4},{4,0},{8,12},{12,8},{16,20},{20,16},{24,28},{28,24},{1,5},{5... | collective-permute-start | bytes 1622024 | tf_op jit(solution)/shard_map/ppermute | solution.py:484
  63.8 33.1 %collective-permute-start.9 = (f32[1056,128]{1,0:T(8,128)S(1)}, f32[1056,128]{1,0:T(8,128)S(1)}, u32[]{:S(2)}, u32[]{:S(2)}) collective-permute-start(f32[1056,128]{1,0:T(8,128)S(1)} %get-tuple-element.45), channel_id=1, source_target_pairs={{4,8},{8,4},{12,16},{16,12},{20,24},{24,20},{5,9},{9,5},{13,17},{1... | collective-permute-start | bytes 1622024 | tf_op jit(solution)/shard_map/ppermute | solution.py:483
  64.5 4.4 %collective-permute-start.10 = (f32[96,128]{1,0:T(8,128)S(1)}, f32[96,128]{1,0:T(8,128)S(1)}, u32[]{:S(2)}, u32[]{:S(2)}) collective-permute-start(f32[96,128]{1,0:T(8,128)S(1)} %get-tuple-element.47), channel_id=1, source_target_pairs={{0,1},{1,2},{2,3},{4,5},{5,6},{6,7},{8,9},{9,10},{10,11},{12,13},{... | collective-permute-start | bytes 147464 | tf_op jit(solution)/shard_map/ppermute | solution.py:470
  67.2 6.0 %collective-permute-start.11 = (f32[96,128]{1,0:T(8,128)S(1)}, f32[96,128]{1,0:T(8,128)S(1)}, u32[]{:S(2)}, u32[]{:S(2)}) collective-permute-start(f32[96,128]{1,0:T(8,128)S(1)} %get-tuple-element.48), channel_id=1, source_target_pairs={{1,0},{2,1},{3,2},{5,4},{6,5},{7,6},{9,8},{10,9},{11,10},{13,12},{... | collective-permute-start | bytes 147464 | tf_op jit(solution)/shard_map/ppermute | solution.py:475
  73.7 1.7 %collective-permute-start.12 = (f32[336,128]{1,0:T(8,128)S(1)}, f32[336,128]{1,0:T(8,128)S(1)}, u32[]{:S(2)}, u32[]{:S(2)}) collective-permute-start(f32[336,128]{1,0:T(8,128)S(1)} %get-tuple-element.49), channel_id=1, source_target_pairs={{0,4},{4,0},{8,12},{12,8},{16,20},{20,16},{24,28},{28,24},{1,5},{5... | collective-permute-start | bytes 516104 | tf_op jit(solution)/shard_map/ppermute | solution.py:484
  77.3 4.5 %collective-permute-start.14 = (f32[64,128]{1,0:T(8,128)S(1)}, f32[64,128]{1,0:T(8,128)S(1)}, u32[]{:S(2)}, u32[]{:S(2)}) collective-permute-start(f32[64,128]{1,0:T(8,128)S(1)} %get-tuple-element.52), channel_id=1, source_target_pairs={{0,1},{1,2},{2,3},{4,5},{5,6},{6,7},{8,9},{9,10},{10,11},{12,13},{... | collective-permute-start | bytes 98312 | tf_op jit(solution)/shard_map/ppermute | solution.py:470
  80.2 5.8 %collective-permute-start.15 = (f32[64,128]{1,0:T(8,128)S(1)}, f32[64,128]{1,0:T(8,128)S(1)}, u32[]{:S(2)}, u32[]{:S(2)}) collective-permute-start(f32[64,128]{1,0:T(8,128)S(1)} %get-tuple-element.53), channel_id=1, source_target_pairs={{1,0},{2,1},{3,2},{5,4},{6,5},{7,6},{9,8},{10,9},{11,10},{13,12},{... | collective-permute-start | bytes 98312 | tf_op jit(solution)/shard_map/ppermute | solution.py:475
  86.6 10.3 %collective-permute-start.16 = (f32[192,128]{1,0:T(8,128)S(1)}, f32[192,128]{1,0:T(8,128)S(1)}, u32[]{:S(2)}, u32[]{:S(2)}) collective-permute-start(f32[192,128]{1,0:T(8,128)S(1)} %get-tuple-element.54), channel_id=1, source_target_pairs={{0,4},{4,0},{8,12},{12,8},{16,20},{20,16},{24,28},{28,24},{1,5},{5... | collective-permute-start | bytes 294920 | tf_op jit(solution)/shard_map/ppermute | solution.py:484
  92.5 4.3 %collective-permute-start.17 = (f32[192,128]{1,0:T(8,128)S(1)}, f32[192,128]{1,0:T(8,128)S(1)}, u32[]{:S(2)}, u32[]{:S(2)}) collective-permute-start(f32[192,128]{1,0:T(8,128)S(1)} %get-tuple-element.55), channel_id=1, source_target_pairs={{4,8},{8,4},{12,16},{16,12},{20,24},{24,20},{5,9},{9,5},{13,17},{1... | collective-permute-start | bytes 294920 | tf_op jit(solution)/shard_map/ppermute | solution.py:483
  107.2 3.8 %collective-permute-start.20 = (f32[48,128]{1,0:T(8,128)S(1)}, f32[48,128]{1,0:T(8,128)S(1)}, u32[]{:S(2)}, u32[]{:S(2)}) collective-permute-start(f32[48,128]{1,0:T(8,128)S(1)} %get-tuple-element.62), channel_id=1, source_target_pairs={{0,3},{1,0},{2,1},{3,2},{4,7},{5,4},{6,5},{7,6},{8,11},{9,8},{10,9... | collective-permute-start | bytes 73736 | tf_op jit(solution)/shard_map/ppermute | solution.py:513
  108.1 5.9 %collective-permute-start.19 = (f32[48,128]{1,0:T(8,128)S(1)}, f32[48,128]{1,0:T(8,128)S(1)}, u32[]{:S(2)}, u32[]{:S(2)}) collective-permute-start(f32[48,128]{1,0:T(8,128)S(1)} %get-tuple-element.62), channel_id=1, source_target_pairs={{0,1},{1,2},{2,3},{3,0},{4,5},{5,6},{6,7},{7,4},{8,9},{9,10},{10,1... | collective-permute-start | bytes 73736 | tf_op jit(solution)/shard_map/ppermute | solution.py:513
  109.2 5.0 %collective-permute-start.18 = (f32[48,128]{1,0:T(8,128)S(1)}, f32[48,128]{1,0:T(8,128)S(1)}, u32[]{:S(2)}, u32[]{:S(2)}) collective-permute-start(f32[48,128]{1,0:T(8,128)S(1)} %get-tuple-element.62), channel_id=1, source_target_pairs={{0,2},{1,3},{2,0},{3,1},{4,6},{5,7},{6,4},{7,5},{8,10},{9,11},{10,... | collective-permute-start | bytes 73736 | tf_op jit(solution)/shard_map/ppermute | solution.py:513
  114.2 3.4 %collective-permute-start.21 = (f32[48,128]{1,0:T(8,128)S(1)}, f32[48,128]{1,0:T(8,128)S(1)}, u32[]{:S(2)}, u32[]{:S(2)}) collective-permute-start(f32[48,128]{1,0:T(8,128)S(1)} %add_add_fusion.1), channel_id=1, source_target_pairs={{0,4},{4,0},{8,12},{12,8},{16,20},{20,16},{24,28},{28,24},{1,5},{5... | collective-permute-start | bytes 73736 | tf_op jit(solution)/shard_map/ppermute | solution.py:513
  117.6 6.2 %collective-permute-start.24 = (f32[48,128]{1,0:T(8,128)S(1)}, f32[48,128]{1,0:T(8,128)S(1)}, u32[]{:S(2)}, u32[]{:S(2)}) collective-permute-start(f32[48,128]{1,0:T(8,128)S(1)} %add.29), channel_id=1, source_target_pairs={{0,24},{4,28},{8,0},{12,4},{16,8},{20,12},{24,16},{28,20},{1,25},{... | collective-permute-start | bytes 73736 | tf_op jit(solution)/shard_map/ppermute | solution.py:513
  122.1 4.7 %collective-permute-start.23 = (f32[48,128]{1,0:T(8,128)S(1)}, f32[48,128]{1,0:T(8,128)S(1)}, u32[]{:S(2)}, u32[]{:S(2)}) collective-permute-start(f32[48,128]{1,0:T(8,128)S(1)} %add.29), channel_id=1, source_target_pairs={{0,8},{4,12},{8,16},{12,20},{16,24},{20,28},{24,0},{28,4},{1,9},{5... | collective-permute-start | bytes 73736 | tf_op jit(solution)/shard_map/ppermute | solution.py:513
  122.1 4.7 %collective-permute-start.22 = (f32[48,128]{1,0:T(8,128)S(1)}, f32[48,128]{1,0:T(8,128)S(1)}, u32[]{:S(2)}, u32[]{:S(2)}) collective-permute-start(f32[48,128]{1,0:T(8,128)S(1)} %add.29), channel_id=1, source_target_pairs={{0,16},{4,20},{8,24},{12,28},{16,0},{20,4},{24,8},{28,12},{1,17},{... | collective-permute-start | bytes 73736 | tf_op jit(solution)/shard_map/ppermute | solution.py:513
  (5 other events, 137.0 us)

commit v6 on v5

--- a/solution.py
+++ b/solution.py
@@ -434,12 +434,13 @@
     by_pairs(cols, one)
 
 
-def image_kernel(flags, x_ref, p_ref, ylo, yhi, xa, xb, tx_ref, tp_ref, ax_ref, ap_ref, work):
+def image_kernel(flags, x_ref, p_ref, ylo, yhi, xa, xb, tx_ref, tp_ref, ax_ref, ap_ref, works):
     cols, nx, ny, _ = x_ref.shape
     even = flags[4]
     lanes = lane_index(ny)
 
-    def body(f, carry):
+    def one(f, u):
+        work = works.at[u]
         for ref, same, out, first, base, deep in (
             (x_ref, tx_ref, ax_ref, 0, 0, DEEP),
             (p_ref, tp_ref, ap_ref, DEEP, nx * DEEP, 1),
@@ -460,9 +461,8 @@
                 same[rows, :] = center
                 out[rows, :] = 6.0 * center - near
                 before, center = center, after
-        return carry
-
-    lax.fori_loop(0, cols, body, 0)
+
+    by_pairs(cols, one)
 
 
 def from_low(value, axis):
@@ -708,7 +708,7 @@
 
     flat_x, flat_p, image_x, image_p = call(
         image_kernel, [shape(nx * ny * cols, nz)] * 4,
-        [work((nx + 2, PAD + ny + 8, nz), F32)],
+        [work((2, nx + 2, PAD + ny + 8, nz), F32)],
         (flags, x, p, ylo, yhi, xlo, xhi), smem=1,
     )
     w, image_w = call(

time: 135 us -> 135 us (level)
  no operation moved by 1% of the time
where the time goes in v6:
time: 135 us; the launch traced here: 134 us
  starting transfers between devices  42.4 us (31%)
  Pallas kernels  36.6 us (27%)
  waiting for transfers between devices  34.4 us (25%)
  blocking collectives  17.6 us (13%)
  local copies, waits for them, and re-layouts  2.57 us (2%)
    pallas_call x10, Pallas kernels, call(): pl.pallas_call(kernel, out_shape=outs, in_specs=specs, out_specs=[VMEM] *...  28.9 us
    all_to_all x1, blocking collectives, step(): sums = lax.all_to_all(sums, ('gx', 'gy'), 0, 0)  17.6 us
    ppermute x4, waiting for transfers between devices, from_high(): return lax.ppermute(value, axis, [(i + 1, i) for i in range(count - 1)])  17.3 us
    ppermute x7, starting transfers between devices, sum_all(): parts.append(lax.ppermute(value, axis, pairs))  12.3 us
    ppermute x4, starting transfers between devices, from_low(): return lax.ppermute(value, axis, [(i, i + 1) for i in range(count - 1)])  11.5 us
    ppermute x5, starting transfers between devices, swap(): return (lax.ppermute(one, axis, pairs[0]), two)  10.1 us
    ppermute x4, waiting for transfers between devices, from_low(): return lax.ppermute(value, axis, [(i, i + 1) for i in range(count - 1)])  9.37 us
    pallas_call x1, Pallas kernels, step(): pl.pallas_call(functools.partial(finish_kernel, nx * ny * nz * devices),...  7.67 us
  transfers between devices with their start and end apart: 25, of which 14 were waited for; matrix products, arithmetic and copies ran while one was open for 0% of the time, Pallas kernels for 5%

profile of v6, /device:TPU:0, one launch (start us, length us, event | category | flops | bytes accessed | tf_op | source)
XLA Modules:
  0.0 134.4 jit_solution(2134784361830147312)
XLA Ops:
  5.3 4.5 %collective-permute-start = (f32[16,40,128]{2,1,0:T(8,128)S(1)}, f32[16,40,128]{2,1,0:T(8,128)S(1)}, u32[]{:S(2)}, u32[]{:S(2)}) collective-permute-start(f32[16,40,128]{2,1,0:T(8,128)S(1)} %get-tuple-element.33), channel_id=1, source_target_pairs={{0,1},{1,2},{2,3},{4,5},{5,6},{6,7},{8,9},{9,10},{10,11},{12,13},{... | collective-permute-start | bytes 983048 | tf_op jit(solution)/shard_map/ppermute | solution.py:470
  11.1 4.9 %collective-permute-done.ylo = f32[16,40,128]{2,1,0:T(8,128)S(1)} collective-permute-done((f32[16,40,128]{2,1,0:T(8,128)S(1)}, f32[16,40,128]{2,1,0:T(8,128)S(1)}, u32[]{:S(2)}, u32[]{:S(2)}) %collective-permute-start) | collective-permute-done | bytes 327712 | tf_op jit(solution)/shard_map/ppermute | solution.py:470
  16.1 4.7 %collective-permute-done.1.yhi = f32[16,40,128]{2,1,0:T(8,128)S(1)} collective-permute-done((f32[16,40,128]{2,1,0:T(8,128)S(1)}, f32[16,40,128]{2,1,0:T(8,128)S(1)}, u32[]{:S(2)}, u32[]{:S(2)}) %collective-permute-start.1) | collective-permute-done | bytes 327712 | tf_op jit(solution)/shard_map/ppermute | solution.py:475
  20.8 2.2 %shard_map.43 = (f32[32,8,128]{2,1,0:T(8,128)S(1)}, f32[16,32,128]{2,1,0:T(8,128)S(1)}, f32[16,32,128]{2,1,0:T(8,128)S(1)}) custom-call(s32[5]{0:T(128)S(1)} %convert_element_type.3.flags, f32[16,8,16,128]{3,2,1,0:T(8,128)S(1)} %copy-done, f32[16,40,128]{2,1,0:T(8,128)S(1)} %collective-permute-done.ylo, f32[16,40,128]{2,1,0:T(8,128)S(1)} %collective-permute-done.1.yhi, ...), custom_call_target="tpu_custom_call" | custom-call | tf_op jit(solution)/shard_map/pallas_call | solution.py:33
  23.0 2.8 %collective-permute-start.4 = (f32[16,32,128]{2,1,0:T(8,128)S(1)}, f32[16,32,128]{2,1,0:T(8,128)S(1)}, u32[]{:S(2)}, u32[]{:S(2)}) collective-permute-start(f32[16,32,128]{2,1,0:T(8,128)S(1)} %get-tuple-element.39), channel_id=1, source_target_pairs={{0,4},{4,0},{8,12},{12,8},{16,20},{20,16},{24,28},{28,24},{1,5},{5... | collective-permute-start | bytes 786440 | tf_op jit(solution)/shard_map/ppermute | solution.py:484
  26.5 17.6 %all_to_all.5.sums = f32[32,8,128]{2,1,0:T(8,128)S(1)} all-to-all(f32[32,8,128]{2,1,0:T(8,128)S(1)} %get-tuple-element.38), channel_id=1, replica_groups=mesh['gx'=8,'gy'=4] {'gx','gy'}, dimensions={0} | all-to-all | bytes 262144 | tf_op jit(solution)/shard_map/all_to_all | solution.py:669
  44.0 8.3 %shard_map.44 = (f32[16,12,24,128]{3,2,1,0:T(8,128)S(1)}, f32[16,8,16,128]{3,2,1,0:T(8,128)S(1)}, f32[8,4,8,128]{3,2,1,0:T(8,128)S(1)}, f32[96,128]{1,0:T(8,128)...) custom-call(s32[5]{0:T(128)S(1)} %convert_element_type.3.flags, ...), custom_call_target="tpu_custom_call" | custom-call | tf_op jit(solution)/shard_map/pallas_call | solution.py:33
  55.1 3.7 %collective-permute-done.6.ylo = f32[16,24,128]{2,1,0:T(8,128)S(1)} collective-permute-done((f32[16,24,128]{2,1,0:T(8,128)S(1)}, f32[16,24,128]{2,1,0:T(8,128)S(1)}, u32[]{:S(2)}, u32[]{:S(2)}) %collective-permute-start.6) | collective-permute-done | bytes 196640 | tf_op jit(solution)/shard_map/ppermute | solution.py:470
  58.9 4.1 %collective-permute-done.7.yhi = f32[16,24,128]{2,1,0:T(8,128)S(1)} collective-permute-done((f32[16,24,128]{2,1,0:T(8,128)S(1)}, f32[16,24,128]{2,1,0:T(8,128)S(1)}, u32[]{:S(2)}, u32[]{:S(2)}) %collective-permute-start.7) | collective-permute-done | bytes 196640 | tf_op jit(solution)/shard_map/ppermute | solution.py:475
  64.5 2.6 %collective-permute-start.10 = (f32[96,128]{1,0:T(8,128)S(1)}, f32[96,128]{1,0:T(8,128)S(1)}, u32[]{:S(2)}, u32[]{:S(2)}) collective-permute-start(f32[96,128]{1,0:T(8,128)S(1)} %get-tuple-element.47), channel_id=1, source_target_pairs={{0,1},{1,2},{2,3},{4,5},{5,6},{6,7},{8,9},{9,10},{10,11},{12,13},{... | collective-permute-start | bytes 147464 | tf_op jit(solution)/shard_map/ppermute | solution.py:470
  68.9 4.3 %collective-permute-done.11.yhi = f32[96,128]{1,0:T(8,128)S(1)} collective-permute-done((f32[96,128]{1,0:T(8,128)S(1)}, f32[96,128]{1,0:T(8,128)S(1)}, u32[]{:S(2)}, u32[]{:S(2)}) %collective-permute-start.11) | collective-permute-done | bytes 49184 | tf_op jit(solution)/shard_map/ppermute | solution.py:475
  75.5 1.8 %shard_map.47 = (f32[8,4,8,128]{3,2,1,0:T(8,128)S(1)}, f32[64,128]{1,0:T(8,128)S(1)}, f32[64,128]{1,0:T(8,128)S(1)}) custom-call(s32[5]{0:T(128)S(1)} %convert_element_type.3.flags, f32[8,4,8,128]{3,2,1,0:T(8,128)S(1)} %get-tuple-element.46.c_ref, f32[96,128]{1,0:T(8,128)S(1)} %collective-permute-done.10.ylo, f32[96,128]{1,0:T(8,128)S(1)} %collective-permute-done.11.yhi, ...), custom_call_target="tpu_custom_call" | custom-call | tf_op jit(solution)/shard_map/pallas_call | solution.py:33
  77.3 2.9 %collective-permute-start.14 = (f32[64,128]{1,0:T(8,128)S(1)}, f32[64,128]{1,0:T(8,128)S(1)}, u32[]{:S(2)}, u32[]{:S(2)}) collective-permute-start(f32[64,128]{1,0:T(8,128)S(1)} %get-tuple-element.52), channel_id=1, source_target_pairs={{0,1},{1,2},{2,3},{4,5},{5,6},{6,7},{8,9},{9,10},{10,11},{12,13},{... | collective-permute-start | bytes 98312 | tf_op jit(solution)/shard_map/ppermute | solution.py:470
  81.7 4.2 %collective-permute-done.15.yhi.cyhi = f32[64,128]{1,0:T(8,128)S(1)} collective-permute-done((f32[64,128]{1,0:T(8,128)S(1)}, f32[64,128]{1,0:T(8,128)S(1)}, u32[]{:S(2)}, u32[]{:S(2)}) %collective-permute-start.15) | collective-permute-done | bytes 32800 | tf_op jit(solution)/shard_map/ppermute | solution.py:475
  86.6 6.0 %collective-permute-start.16 = (f32[192,128]{1,0:T(8,128)S(1)}, f32[192,128]{1,0:T(8,128)S(1)}, u32[]{:S(2)}, u32[]{:S(2)}) collective-permute-start(f32[192,128]{1,0:T(8,128)S(1)} %get-tuple-element.54), channel_id=1, source_target_pairs={{0,4},{4,0},{8,12},{12,8},{16,20},{20,16},{24,28},{28,24},{1,5},{5... | collective-permute-start | bytes 294920 | tf_op jit(solution)/shard_map/ppermute | solution.py:484
  93.2 3.6 %shard_map.42 = (f32[2048,128]{1,0:T(8,128)S(1)}, f32[2048,128]{1,0:T(8,128)S(1)}, f32[2048,128]{1,0:T(8,128)S(1)}, f32[2048,128]{1,0:T(8,128)S(1)}) custom-call(s32[5]{0:T(128)S(1)} %convert_element_type.3.flags, f32[16,8,16,128]{3,2,1,0:T(8,128)S(1)} %copy-done.1, f32[16,8,16,128]{3,2,1,0:T(8,128)S(1)} %copy-done.3, ...), custom_call_target="tpu_custom_call" | custom-call | tf_op jit(solution)/shard_map/pallas_call | solution.py:33
  96.8 6.2 %shard_map.49 = (f32[2048,128]{1,0:T(8,128)S(1)}, f32[2048,128]{1,0:T(8,128)S(1)}) custom-call(s32[5]{0:T(128)S(1)} %convert_element_type.3.flags, f32[16,8,16,128]{3,2,1,0:T(8,128)S(1)} %get-tuple-element.41.corr_ref.e_ref, f32[16,24,128]{2,1,0:T(8,128)S(1)} %collective-permute-done.6.ylo, f32[16,24,128]{2,1,0:T(8,128)S(1)} %collective-permute-done.7.yhi, ...), custom_call_target="tpu_custom_call" | custom-call | tf_op jit(solution)/shard_map/pallas_call | solution.py:33
  103.0 4.1 %shard_map.50 = (f32[48,128]{1,0:T(8,128)S(1)}, bf16[8,96,2048]{2,1,0:T(8,128)(2,1)S(1)}) custom-call(f32[2048,128]{1,0:T(8,128)S(1)} %get-tuple-element.37.x_ref, f32[2048,128]{1,0:T(8,128)S(1)} %get-tuple-element.57.w_ref, f32[2048,128]{1,0:T(8,128)S(1)} %get-tuple-element.58.p_ref, f32[2048,128]{1,0:T(8,128)S(1)} %get-tuple-element.59.ax_ref, ...), custom_call_target="tpu_custom_call" | custom-call | tf_op jit(solution)/shard_map/pallas_call | solution.py:33
  111.0 3.0 %collective-permute-done.19 = f32[48,128]{1,0:T(8,128)S(1)} collective-permute-done((f32[48,128]{1,0:T(8,128)S(1)}, f32[48,128]{1,0:T(8,128)S(1)}, u32[]{:S(2)}, u32[]{:S(2)}) %collective-permute-start.19) | collective-permute-done | bytes 24608 | tf_op jit(solution)/shard_map/ppermute | solution.py:513
  114.1 2.6 %collective-permute-start.21 = (f32[48,128]{1,0:T(8,128)S(1)}, f32[48,128]{1,0:T(8,128)S(1)}, u32[]{:S(2)}, u32[]{:S(2)}) collective-permute-start(f32[48,128]{1,0:T(8,128)S(1)} %add_add_fusion.1), channel_id=1, source_target_pairs={{0,4},{4,0},{8,12},{12,8},{16,20},{20,16},{24,28},{28,24},{1,5},{5... | collective-permute-start | bytes 73736 | tf_op jit(solution)/shard_map/ppermute | solution.py:513
  117.6 4.5 %collective-permute-start.24 = (f32[48,128]{1,0:T(8,128)S(1)}, f32[48,128]{1,0:T(8,128)S(1)}, u32[]{:S(2)}, u32[]{:S(2)}) collective-permute-start(f32[48,128]{1,0:T(8,128)S(1)} %add.29), channel_id=1, source_target_pairs={{0,24},{4,28},{8,0},{12,4},{16,8},{20,12},{24,16},{28,20},{1,25},{... | collective-permute-start | bytes 73736 | tf_op jit(solution)/shard_map/ppermute | solution.py:513
  122.0 1.8 %collective-permute-start.22 = (f32[48,128]{1,0:T(8,128)S(1)}, f32[48,128]{1,0:T(8,128)S(1)}, u32[]{:S(2)}, u32[]{:S(2)}) collective-permute-start(f32[48,128]{1,0:T(8,128)S(1)} %add.29), channel_id=1, source_target_pairs={{0,16},{4,20},{8,24},{12,28},{16,0},{20,4},{24,8},{28,12},{1,17},{... | collective-permute-start | bytes 73736 | tf_op jit(solution)/shard_map/ppermute | solution.py:513
  123.8 3.0 %collective-permute-done.23 = f32[48,128]{1,0:T(8,128)S(1)} collective-permute-done((f32[48,128]{1,0:T(8,128)S(1)}, f32[48,128]{1,0:T(8,128)S(1)}, u32[]{:S(2)}, u32[]{:S(2)}) %collective-permute-start.23) | collective-permute-done | bytes 24608 | tf_op jit(solution)/shard_map/ppermute | solution.py:513
  126.8 7.7 %finish.1 = (f32[16,8,16,128]{3,2,1,0:T(8,128)}, f32[16,8,16,128]{3,2,1,0:T(8,128)}) custom-call(f32[48,128]{1,0:T(8,128)S(1)} %add_add_fusion.sums_ref, bf16[8,96,2048]{2,1,0:T(8,128)(2,1)S(1)} %get-tuple-element.63.s_ref), custom_call_target="tpu_custom_call" | custom-call | tf_op jit(solution)/shard_map/finish/pallas_call | solution.py:731
  (51 shorter events, 22.6 us)
Async XLA Ops:
  4.1 16.7 %collective-permute-start.2 = (f32[16,5,16,128]{3,2,1,0:T(8,128)S(1)}, f32[16,5,16,128]{3,2,1,0:T(8,128)S(1)}, u32[]{:S(2)}, u32[]{:S(2)}) collective-permute-start(f32[16,5,16,128]{3,2,1,0:T(8,128)S(1)} %get-tuple-element.35), channel_id=1, source_target_pairs={{0,4},{4,0},{8,12},{12,8},{16,20},{20,16},{24,28},{28,24},{1,5},{5... | collective-permute-start | bytes 1966088 | tf_op jit(solution)/shard_map/ppermute | solution.py:484
  4.6 16.1 %collective-permute-start.3 = (f32[16,5,16,128]{3,2,1,0:T(8,128)S(1)}, f32[16,5,16,128]{3,2,1,0:T(8,128)S(1)}, u32[]{:S(2)}, u32[]{:S(2)}) collective-permute-start(f32[16,5,16,128]{3,2,1,0:T(8,128)S(1)} %get-tuple-element.36), channel_id=1, source_target_pairs={{4,8},{8,4},{12,16},{16,12},{20,24},{24,20},{5,9},{9,5},{13,17},{1... | collective-permute-start | bytes 1966088 | tf_op jit(solution)/shard_map/ppermute | solution.py:483
  5.3 10.7 %collective-permute-start = (f32[16,40,128]{2,1,0:T(8,128)S(1)}, f32[16,40,128]{2,1,0:T(8,128)S(1)}, u32[]{:S(2)}, u32[]{:S(2)}) collective-permute-start(f32[16,40,128]{2,1,0:T(8,128)S(1)} %get-tuple-element.33), channel_id=1, source_target_pairs={{0,1},{1,2},{2,3},{4,5},{5,6},{6,7},{8,9},{9,10},{10,11},{12,13},{... | collective-permute-start | bytes 983048 | tf_op jit(solution)/shard_map/ppermute | solution.py:470
  9.8 10.9 %collective-permute-start.1 = (f32[16,40,128]{2,1,0:T(8,128)S(1)}, f32[16,40,128]{2,1,0:T(8,128)S(1)}, u32[]{:S(2)}, u32[]{:S(2)}) collective-permute-start(f32[16,40,128]{2,1,0:T(8,128)S(1)} %get-tuple-element.34), channel_id=1, source_target_pairs={{1,0},{2,1},{3,2},{5,4},{6,5},{7,6},{9,8},{10,9},{11,10},{13,12},{... | collective-permute-start | bytes 983048 | tf_op jit(solution)/shard_map/ppermute | solution.py:475
  23.0 21.1 %collective-permute-start.4 = (f32[16,32,128]{2,1,0:T(8,128)S(1)}, f32[16,32,128]{2,1,0:T(8,128)S(1)}, u32[]{:S(2)}, u32[]{:S(2)}) collective-permute-start(f32[16,32,128]{2,1,0:T(8,128)S(1)} %get-tuple-element.39), channel_id=1, source_target_pairs={{0,4},{4,0},{8,12},{12,8},{16,20},{20,16},{24,28},{28,24},{1,5},{5... | collective-permute-start | bytes 786440 | tf_op jit(solution)/shard_map/ppermute | solution.py:484
  25.8 18.3 %collective-permute-start.5 = (f32[16,32,128]{2,1,0:T(8,128)S(1)}, f32[16,32,128]{2,1,0:T(8,128)S(1)}, u32[]{:S(2)}, u32[]{:S(2)}) collective-permute-start(f32[16,32,128]{2,1,0:T(8,128)S(1)} %get-tuple-element.40), channel_id=1, source_target_pairs={{4,8},{8,4},{12,16},{16,12},{20,24},{24,20},{5,9},{9,5},{13,17},{1... | collective-permute-start | bytes 786440 | tf_op jit(solution)/shard_map/ppermute | solution.py:483
  52.4 6.5 %collective-permute-start.6 = (f32[16,24,128]{2,1,0:T(8,128)S(1)}, f32[16,24,128]{2,1,0:T(8,128)S(1)}, u32[]{:S(2)}, u32[]{:S(2)}) collective-permute-start(f32[16,24,128]{2,1,0:T(8,128)S(1)} %get-tuple-element.42), channel_id=1, source_target_pairs={{0,1},{1,2},{2,3},{4,5},{5,6},{6,7},{8,9},{9,10},{10,11},{12,13},{... | collective-permute-start | bytes 589832 | tf_op jit(solution)/shard_map/ppermute | solution.py:470
  53.8 9.2 %collective-permute-start.7 = (f32[16,24,128]{2,1,0:T(8,128)S(1)}, f32[16,24,128]{2,1,0:T(8,128)S(1)}, u32[]{:S(2)}, u32[]{:S(2)}) collective-permute-start(f32[16,24,128]{2,1,0:T(8,128)S(1)} %get-tuple-element.43), channel_id=1, source_target_pairs={{1,0},{2,1},{3,2},{5,4},{6,5},{7,6},{9,8},{10,9},{11,10},{13,12},{... | collective-permute-start | bytes 589832 | tf_op jit(solution)/shard_map/ppermute | solution.py:475
  63.7 33.1 %collective-permute-start.8 = (f32[1056,128]{1,0:T(8,128)S(1)}, f32[1056,128]{1,0:T(8,128)S(1)}, u32[]{:S(2)}, u32[]{:S(2)}) collective-permute-start(f32[1056,128]{1,0:T(8,128)S(1)} %get-tuple-element.44), channel_id=1, source_target_pairs={{0,4},{4,0},{8,12},{12,8},{16,20},{20,16},{24,28},{28,24},{1,5},{5... | collective-permute-start | bytes 1622024 | tf_op jit(solution)/shard_map/ppermute | solution.py:484
  63.8 33.0 %collective-permute-start.9 = (f32[1056,128]{1,0:T(8,128)S(1)}, f32[1056,128]{1,0:T(8,128)S(1)}, u32[]{:S(2)}, u32[]{:S(2)}) collective-permute-start(f32[1056,128]{1,0:T(8,128)S(1)} %get-tuple-element.45), channel_id=1, source_target_pairs={{4,8},{8,4},{12,16},{16,12},{20,24},{24,20},{5,9},{9,5},{13,17},{1... | collective-permute-start | bytes 1622024 | tf_op jit(solution)/shard_map/ppermute | solution.py:483
  64.5 4.4 %collective-permute-start.10 = (f32[96,128]{1,0:T(8,128)S(1)}, f32[96,128]{1,0:T(8,128)S(1)}, u32[]{:S(2)}, u32[]{:S(2)}) collective-permute-start(f32[96,128]{1,0:T(8,128)S(1)} %get-tuple-element.47), channel_id=1, source_target_pairs={{0,1},{1,2},{2,3},{4,5},{5,6},{6,7},{8,9},{9,10},{10,11},{12,13},{... | collective-permute-start | bytes 147464 | tf_op jit(solution)/shard_map/ppermute | solution.py:470
  67.2 6.0 %collective-permute-start.11 = (f32[96,128]{1,0:T(8,128)S(1)}, f32[96,128]{1,0:T(8,128)S(1)}, u32[]{:S(2)}, u32[]{:S(2)}) collective-permute-start(f32[96,128]{1,0:T(8,128)S(1)} %get-tuple-element.48), channel_id=1, source_target_pairs={{1,0},{2,1},{3,2},{5,4},{6,5},{7,6},{9,8},{10,9},{11,10},{13,12},{... | collective-permute-start | bytes 147464 | tf_op jit(solution)/shard_map/ppermute | solution.py:475
  73.7 1.7 %collective-permute-start.12 = (f32[336,128]{1,0:T(8,128)S(1)}, f32[336,128]{1,0:T(8,128)S(1)}, u32[]{:S(2)}, u32[]{:S(2)}) collective-permute-start(f32[336,128]{1,0:T(8,128)S(1)} %get-tuple-element.49), channel_id=1, source_target_pairs={{0,4},{4,0},{8,12},{12,8},{16,20},{20,16},{24,28},{28,24},{1,5},{5... | collective-permute-start | bytes 516104 | tf_op jit(solution)/shard_map/ppermute | solution.py:484
  77.3 4.5 %collective-permute-start.14 = (f32[64,128]{1,0:T(8,128)S(1)}, f32[64,128]{1,0:T(8,128)S(1)}, u32[]{:S(2)}, u32[]{:S(2)}) collective-permute-start(f32[64,128]{1,0:T(8,128)S(1)} %get-tuple-element.52), channel_id=1, source_target_pairs={{0,1},{1,2},{2,3},{4,5},{5,6},{6,7},{8,9},{9,10},{10,11},{12,13},{... | collective-permute-start | bytes 98312 | tf_op jit(solution)/shard_map/ppermute | solution.py:470
  80.2 5.8 %collective-permute-start.15 = (f32[64,128]{1,0:T(8,128)S(1)}, f32[64,128]{1,0:T(8,128)S(1)}, u32[]{:S(2)}, u32[]{:S(2)}) collective-permute-start(f32[64,128]{1,0:T(8,128)S(1)} %get-tuple-element.53), channel_id=1, source_target_pairs={{1,0},{2,1},{3,2},{5,4},{6,5},{7,6},{9,8},{10,9},{11,10},{13,12},{... | collective-permute-start | bytes 98312 | tf_op jit(solution)/shard_map/ppermute | solution.py:475
  86.6 10.2 %collective-permute-start.16 = (f32[192,128]{1,0:T(8,128)S(1)}, f32[192,128]{1,0:T(8,128)S(1)}, u32[]{:S(2)}, u32[]{:S(2)}) collective-permute-start(f32[192,128]{1,0:T(8,128)S(1)} %get-tuple-element.54), channel_id=1, source_target_pairs={{0,4},{4,0},{8,12},{12,8},{16,20},{20,16},{24,28},{28,24},{1,5},{5... | collective-permute-start | bytes 294920 | tf_op jit(solution)/shard_map/ppermute | solution.py:484
  92.5 4.3 %collective-permute-start.17 = (f32[192,128]{1,0:T(8,128)S(1)}, f32[192,128]{1,0:T(8,128)S(1)}, u32[]{:S(2)}, u32[]{:S(2)}) collective-permute-start(f32[192,128]{1,0:T(8,128)S(1)} %get-tuple-element.55), channel_id=1, source_target_pairs={{4,8},{8,4},{12,16},{16,12},{20,24},{24,20},{5,9},{9,5},{13,17},{1... | collective-permute-start | bytes 294920 | tf_op jit(solution)/shard_map/ppermute | solution.py:483
  107.1 3.8 %collective-permute-start.20 = (f32[48,128]{1,0:T(8,128)S(1)}, f32[48,128]{1,0:T(8,128)S(1)}, u32[]{:S(2)}, u32[]{:S(2)}) collective-permute-start(f32[48,128]{1,0:T(8,128)S(1)} %get-tuple-element.62), channel_id=1, source_target_pairs={{0,3},{1,0},{2,1},{3,2},{4,7},{5,4},{6,5},{7,6},{8,11},{9,8},{10,9... | collective-permute-start | bytes 73736 | tf_op jit(solution)/shard_map/ppermute | solution.py:513
  108.0 5.9 %collective-permute-start.19 = (f32[48,128]{1,0:T(8,128)S(1)}, f32[48,128]{1,0:T(8,128)S(1)}, u32[]{:S(2)}, u32[]{:S(2)}) collective-permute-start(f32[48,128]{1,0:T(8,128)S(1)} %get-tuple-element.62), channel_id=1, source_target_pairs={{0,1},{1,2},{2,3},{3,0},{4,5},{5,6},{6,7},{7,4},{8,9},{9,10},{10,1... | collective-permute-start | bytes 73736 | tf_op jit(solution)/shard_map/ppermute | solution.py:513
  109.2 5.0 %collective-permute-start.18 = (f32[48,128]{1,0:T(8,128)S(1)}, f32[48,128]{1,0:T(8,128)S(1)}, u32[]{:S(2)}, u32[]{:S(2)}) collective-permute-start(f32[48,128]{1,0:T(8,128)S(1)} %get-tuple-element.62), channel_id=1, source_target_pairs={{0,2},{1,3},{2,0},{3,1},{4,6},{5,7},{6,4},{7,5},{8,10},{9,11},{10,... | collective-permute-start | bytes 73736 | tf_op jit(solution)/shard_map/ppermute | solution.py:513
  114.1 3.4 %collective-permute-start.21 = (f32[48,128]{1,0:T(8,128)S(1)}, f32[48,128]{1,0:T(8,128)S(1)}, u32[]{:S(2)}, u32[]{:S(2)}) collective-permute-start(f32[48,128]{1,0:T(8,128)S(1)} %add_add_fusion.1), channel_id=1, source_target_pairs={{0,4},{4,0},{8,12},{12,8},{16,20},{20,16},{24,28},{28,24},{1,5},{5... | collective-permute-start | bytes 73736 | tf_op jit(solution)/shard_map/ppermute | solution.py:513
  117.6 6.2 %collective-permute-start.24 = (f32[48,128]{1,0:T(8,128)S(1)}, f32[48,128]{1,0:T(8,128)S(1)}, u32[]{:S(2)}, u32[]{:S(2)}) collective-permute-start(f32[48,128]{1,0:T(8,128)S(1)} %add.29), channel_id=1, source_target_pairs={{0,24},{4,28},{8,0},{12,4},{16,8},{20,12},{24,16},{28,20},{1,25},{... | collective-permute-start | bytes 73736 | tf_op jit(solution)/shard_map/ppermute | solution.py:513
  122.0 4.7 %collective-permute-start.23 = (f32[48,128]{1,0:T(8,128)S(1)}, f32[48,128]{1,0:T(8,128)S(1)}, u32[]{:S(2)}, u32[]{:S(2)}) collective-permute-start(f32[48,128]{1,0:T(8,128)S(1)} %add.29), channel_id=1, source_target_pairs={{0,8},{4,12},{8,16},{12,20},{16,24},{20,28},{24,0},{28,4},{1,9},{5... | collective-permute-start | bytes 73736 | tf_op jit(solution)/shard_map/ppermute | solution.py:513
  122.0 4.7 %collective-permute-start.22 = (f32[48,128]{1,0:T(8,128)S(1)}, f32[48,128]{1,0:T(8,128)S(1)}, u32[]{:S(2)}, u32[]{:S(2)}) collective-permute-start(f32[48,128]{1,0:T(8,128)S(1)} %add.29), channel_id=1, source_target_pairs={{0,16},{4,20},{8,24},{12,28},{16,0},{20,4},{24,8},{28,12},{1,17},{... | collective-permute-start | bytes 73736 | tf_op jit(solution)/shard_map/ppermute | solution.py:513
  (5 other events, 137.0 us)
